TPU v7x, 32 devices: a whole 2x2x4 slice. The times are simulated.
32 devices in a mesh: row: 4 (over x, core), col: 8 (over z, y).
Axes of the slice: x: 2, y: 2, z: 4, core: 2. Of those that a mesh axis runs over, the one named last changes fastest.
Arguments:
- hidden_in: bfloat16 [4, 8, 512, 896], P('row', 'col'), may hold values from -6 to 6
- targets: bfloat16 [4, 8, 512, 896], P('row', 'col'), may hold values from -6 to 6
- first_params: float32 [4, 896, 896], P('row', 'col'), may hold values from -0.1875 to 0.1875
- first_moment: float32 [4, 896, 896], P('row', 'col'), may hold values from -0.06 to 0.06
- second_params: float32 [8, 896, 896], P('col', 'row'), may hold values from -0.1875 to 0.1875
- second_moment: float32 [8, 896, 896], P('col', 'row'), may hold values from -0.06 to 0.06
Outputs:
- first_params_new: float32 [4, 896, 896], P('row', 'col')
- first_moment_new: float32 [4, 896, 896], P('row', 'col')
- second_params_new: float32 [8, 896, 896], P('col', 'row')
- second_moment_new: float32 [8, 896, 896], P('col', 'row')
All inputs are finite; a program needn't handle non-finite values.
Results may differ from a plain program's by a relative error of at most 0.022.
Values may be sent and summed in bfloat16 or wider, within the bound.
No kernel may reach another device: no remote copies, remote signals or barrier semaphores. Data moves between devices by JAX's collectives and lax.ppermute only.
A program may use at most 64 MiB of HBM per device.

v0:
```python
import jax
import jax.numpy as jnp
from jax import lax
from jax.sharding import PartitionSpec as P

outer_momentum = 0.9
outer_rate = 0.7


def passed_along(x, axis, by):
    length = lax.axis_size(axis)
    return lax.ppermute(x, axis, [(i, (i + by) % length) for i in range(length)])


def gelu_tanh(value):
    return jax.nn.gelu(value, approximate=True)


def nesterov(params, moment, grad):
    moment_new = outer_momentum * moment + grad
    return (params - outer_rate * (grad + outer_momentum * moment_new), moment_new)


def per_device(hidden_in, targets, first_params, first_moment, second_params, second_moment):
    inputs = hidden_in[0, 0]
    wanted = targets[0, 0]
    tokens = inputs.shape[0]
    offset = lax.axis_size("col") // 4
    pre = jnp.dot(
        inputs,
        lax.all_gather(first_params[0].astype(jnp.bfloat16), "col", axis=0, tiled=True),
        preferred_element_type=jnp.float32,
    )
    second_full = lax.all_gather(second_params[0].astype(jnp.bfloat16), "row", axis=0, tiled=True)
    active, slope = jax.vjp(gelu_tanh, pre)
    active_b = active.astype(jnp.bfloat16)
    output = jnp.dot(active_b, second_full, preferred_element_type=jnp.float32)
    error = ((output - wanted.astype(jnp.float32)) / tokens).astype(jnp.bfloat16)
    back = lax.dot_general(
        error, second_full, (((1,), (1,)), ((), ())), preferred_element_type=jnp.float32
    )
    grad_pre = slope(back)[0].astype(jnp.bfloat16)
    picked = active_b
    second_grad = lax.psum_scatter(
        lax.dot_general(
            picked, error, (((0,), (0,)), ((), ())), preferred_element_type=jnp.float32
        ).astype(jnp.bfloat16),
        "row",
        scatter_dimension=0,
        tiled=True,
    ).astype(jnp.float32) / lax.axis_size("row")
    picked = inputs
    first_grad = lax.psum_scatter(
        lax.dot_general(
            picked, grad_pre, (((0,), (0,)), ((), ())), preferred_element_type=jnp.float32
        ).astype(jnp.bfloat16),
        "col",
        scatter_dimension=0,
        tiled=True,
    ).astype(jnp.float32) / lax.axis_size("col")
    first_params_new, first_moment_new = nesterov(first_params, first_moment, first_grad[None])
    second_upd, second_mom = nesterov(second_params, second_moment, second_grad[None])
    stacked = jnp.stack([second_upd, second_mom])
    moved = passed_along(stacked.astype(jnp.bfloat16), "col", offset).astype(stacked.dtype)
    return (first_params_new, first_moment_new, moved[0], moved[1])


def solution(mesh):
    return jax.shard_map(
        per_device,
        mesh=mesh,
        in_specs=(
            P("row", "col", None, None),
            P("row", "col", None, None),
            P("row", "col", None),
            P("row", "col", None),
            P("col", "row", None),
            P("col", "row", None),
        ),
        out_specs=(
            P("row", "col", None),
            P("row", "col", None),
            P("col", "row", None),
            P("col", "row", None),
        ),
        check_vma=False,
    )
```

profile of v0, /device:TPU:0, one launch (start us, length us, event | category | flops | bytes accessed | tf_op | source)
XLA Modules:
  0.0 197.8 jit_solution(2901205608396926962)
XLA Ops:
  7.2 0.0 copy-start
  7.2 0.0 all-gather.5.cloned.1.call-start
  7.2 1.8 convert_element_type.54
  9.0 0.0 all-gather.5.cloned.1.call-update
  9.0 0.0 all-gather.7.cloned.1.call-start
  9.1 1.9 convert_element_type.57
  11.0 0.0 all-gather.7.cloned.1.call-update
  11.0 0.0 copy-start.5
  11.0 0.0 reduce-scatter.5.cloned.1.call-start
  11.1 47.0 %all-gather.5.cloned.1.call-done = bf16[1,896,896]{2,1,0:T(8,128)(2,1)} async-done(((bf16[1,112,896]{2,1,0:T(8,128)(2,1)}), bf16[1,896,896]{2,1,0:T(8,128)(2,1)}) %all-gather.5.cloned.1.call-update) | async-done | bytes 1605648 | tf_op jit(solution)/shard_map/all_gather | solution.py:31
  58.0 0.0 copy-done
  58.0 3.9 %fusion.13 = f32[512,896]{1,0:T(8,128)} fusion(bf16[1,896,896]{2,1,0:T(8,128)(2,1)} %all-gather.5.cloned.1.call-done, bf16[1,1,512,896]{3,2,1,0:T(8,128)(2,1)S(1)} %copy-done), kind=kOutput, calls=%fused_computation.19 | convolution fusion | flops 822083584 | bytes 4358144 | tf_op jit(solution)/shard_map/dot_general | solution.py:29
  61.9 16.5 %all-gather.7.cloned.1.call-done = bf16[1,896,896]{2,1,0:T(8,128)(2,1)} async-done(((bf16[1,224,896]{2,1,0:T(8,128)(2,1)}), bf16[1,896,896]{2,1,0:T(8,128)(2,1)}) %all-gather.7.cloned.1.call-update) | async-done | bytes 1605648 | tf_op jit(solution)/shard_map/all_gather | solution.py:34
  78.4 0.0 copy-done.5
  78.4 0.0 copy-start.6
  78.4 3.4 %fusion.8 = bf16[512,896]{1,0:T(8,128)(2,1)S(1)} fusion(bf16[1,896,896]{2,1,0:T(8,128)(2,1)} %all-gather.7.cloned.1.call-done, bf16[1,1,512,896]{3,2,1,0:T(8,128)(2,1)S(1)} %copy-done.5, f32[512,896]{1,0:T(8,128)} %fusion.13), kind=kOutput, calls=%fused_computation.11 | convolution fusion | flops 828047360 | bytes 5275648 | tf_op jit(solution)/shard_map/dot_general | solution.py:37
  81.8 0.0 copy-start.7
  81.8 1.0 copy-done.7
  82.8 0.0 copy-done.6
  82.8 2.4 %convolution_convert_fusion = bf16[896,896]{1,0:T(8,128)(2,1)} fusion(bf16[512,896]{1,0:T(8,128)(2,1)S(1)} %fusion.8, f32[512,896]{1,0:T(8,128)S(1)} %copy-done.6), kind=kOutput, calls=%fused_computation.13 | convolution fusion | flops 827015168 | bytes 4358144 | tf_op jit(solution)/shard_map/dot_general | solution.py:45
  85.2 0.0 reduce-scatter.5.cloned.1.call-update
  85.2 0.0 reduce-scatter.7.cloned.1.call-start
  85.2 4.9 %fusion.17 = bf16[896,896]{0,1:T(8,128)(2,1)S(1)} fusion(f32[512,896]{1,0:T(8,128)} %fusion.13, bf16[512,896]{1,0:T(8,128)(2,1)} %copy-done.7, bf16[1,896,896]{2,1,0:T(8,128)(2,1)} %all-gather.7.cloned.1.call-done, bf16[1,1,512,896]{3,2,1,0:T(8,128)(2,1)S(1)} %copy-done), kind=kOutput, calls=%fused_computation.21 | convolution fusion | flops 1654145024 | bytes 6881280 | tf_op jit(solution)/shard_map/dot_general | solution.py:54
  90.1 0.0 copy-start.1
  90.1 2.3 %copy.18 = bf16[896,896]{1,0:T(8,128)(2,1)} copy(bf16[896,896]{0,1:T(8,128)(2,1)S(1)} %fusion.17) | data formatting | bytes 3211264
  92.5 0.0 copy-start.3
  92.5 0.0 reduce-scatter.7.cloned.1.call-update
  92.5 0.0 copy-start.2
  92.5 21.0 %reduce-scatter.5.cloned.1.call-done = bf16[224,896]{1,0:T(8,128)(2,1)} async-done(((bf16[896,896]{1,0:T(8,128)(2,1)}), bf16[224,896]{1,0:T(8,128)(2,1)}) %reduce-scatter.5.cloned.1.call-update) | async-done | bytes 401424 | tf_op jit(solution)/shard_map/reduce_scatter | solution.py:44
  113.5 0.0 copy-done.1
  113.5 0.0 copy-done.3
  113.5 1.2 fusion.37
  114.8 0.0 copy-start.4
  114.8 1.0 pad_maximum_fusion
  115.8 1.5 collective-permute-start
  117.3 0.0 copy-done.2
  117.3 0.2 copy.15
  117.5 0.0 copy-done.4
  117.5 0.2 copy.14
  117.7 67.9 %reduce-scatter.7.cloned.1.call-done = bf16[112,896]{1,0:T(8,128)(2,1)} async-done(((bf16[896,896]{1,0:T(8,128)(2,1)}), bf16[112,896]{1,0:T(8,128)(2,1)}) %reduce-scatter.7.cloned.1.call-update) | async-done | bytes 200720
  185.6 1.1 copy.19
  186.7 0.1 bitcast_add_fusion.3
  186.9 0.9 copy.16
  187.8 0.9 copy.17
  188.7 0.0 collective-permute-done
  188.7 1.2 convert_element_type.68
  190.0 1.3 slice_bitcast_fusion
Async XLA Ops:
  7.2 50.9 %copy-start = (bf16[1,1,512,896]{3,2,1,0:T(8,128)(2,1)S(1)}, bf16[1,1,512,896]{3,2,1,0:T(8,128)(2,1)}, u32[]{:S(2)}) copy-start(bf16[1,1,512,896]{3,2,1,0:T(8,128)(2,1)} %param.6) | copy-start | bytes 2752516
  7.2 50.9 %all-gather.5.cloned.1.call-start = ((), (), s32[]{:S(2)}) async-start(), calls=%async_computation.3 | async-start | bytes 1806336 | tf_op jit(solution)/shard_map/all_gather | solution.py:31
  9.0 69.4 %all-gather.7.cloned.1.call-start = ((), (), s32[]{:S(2)}) async-start(), calls=%async_computation.4 | async-start | bytes 2007040 | tf_op jit(solution)/shard_map/all_gather | solution.py:34
  11.0 67.4 %copy-start.5 = (bf16[1,1,512,896]{3,2,1,0:T(8,128)(2,1)S(1)}, bf16[1,1,512,896]{3,2,1,0:T(8,128)(2,1)}, u32[]{:S(2)}) copy-start(bf16[1,1,512,896]{3,2,1,0:T(8,128)(2,1)} %param.7) | copy-start | bytes 2752516
  11.0 102.5 %reduce-scatter.5.cloned.1.call-start = ((), (), s32[]{:S(2)}) async-start(), calls=%async_computation.2 | async-start | bytes 2007040 | tf_op jit(solution)/shard_map/reduce_scatter | solution.py:44
  78.4 4.4 %copy-start.6 = (f32[512,896]{1,0:T(8,128)S(1)}, f32[512,896]{1,0:T(8,128)}, u32[]{:S(2)}) copy-start(f32[512,896]{1,0:T(8,128)} %fusion.13) | copy-start | bytes 5505028
  81.8 1.0 copy-start.7
  85.2 100.4 %reduce-scatter.7.cloned.1.call-start = ((), (), s32[]{:S(2)}) async-start(), calls=%async_computation.5 | async-start | bytes 1806336
  90.1 23.4 %copy-start.1 = (f32[1,224,896]{2,1,0:T(8,128)S(1)}, f32[1,224,896]{2,1,0:T(8,128)}, u32[]{:S(2)}) copy-start(f32[1,224,896]{2,1,0:T(8,128)} %param.10) | copy-start | bytes 2408452
  92.5 21.1 %copy-start.3 = (f32[1,224,896]{2,1,0:T(8,128)S(1)}, f32[1,224,896]{2,1,0:T(8,128)}, u32[]{:S(2)}) copy-start(f32[1,224,896]{2,1,0:T(8,128)} %param.11) | copy-start | bytes 2408452
  92.5 24.8 %copy-start.2 = (f32[1,112,896]{2,1,0:T(8,128)S(1)}, f32[1,112,896]{2,1,0:T(8,128)}, u32[]{:S(2)}) copy-start(f32[1,112,896]{2,1,0:T(8,128)} %param.8) | copy-start | bytes 1204228
  114.8 2.7 %copy-start.4 = (f32[1,112,896]{2,1,0:T(8,128)S(1)}, f32[1,112,896]{2,1,0:T(8,128)}, u32[]{:S(2)}) copy-start(f32[1,112,896]{2,1,0:T(8,128)} %param.9) | copy-start | bytes 1204228
  115.8 73.0 %collective-permute-start = (bf16[2,1,224,896]{3,2,1,0:T(8,128)(2,1)}, bf16[2,1,224,896]{3,2,1,0:T(8,128)(2,1)}, u32[]{:S(2)}, u32[]{:S(2)}) collective-permute-start(bf16[2,1,224,896]{3,2,1,0:T(8,128)(2,1)} %pad_maximum_fusion), channel_id=1, source_target_pairs={{0,2},{1,3},{2,4},{3,5},{4,6},{5,7},{6,0},{7,1},{8,10},{9,11},{10,... | collective-permute-start | bytes 2408456 | tf_op jit(solution)/shard_map/ppermute | solution.py:12
Sparse Core Ops, SparseCore 0:
  10.7 47.2 all-gather.4
  60.2 18.1 all-gather.6
  85.3 28.1 reduce-scatter.4
  116.9 68.7 reduce-scatter.6
where the time goes:
time: 198 us
  waiting for transfers between devices  152 us (77%)
  matrix products  14.6 us (7%)
  between operations  13.9 us (7%)
  local copies, waits for them, and re-layouts  7.96 us (4%)
  other arithmetic  7.29 us (4%)
    unnamed x5, waiting for transfers between devices  68 us
    all_gather x1, waiting for transfers between devices, per_device(): lax.all_gather(first_params[0].astype(jnp.bfloat16), 'col', axis=0, tiled...  47 us
    reduce_scatter x1, waiting for transfers between devices, per_device(): lax.psum_scatter(lax.dot_general(picked, error, (((0,), (0,)), ((), ())),...  21 us
    all_gather x1, waiting for transfers between devices, per_device(): lax.all_gather(second_params[0].astype(jnp.bfloat16), 'row', axis=0, tile...  16.5 us
    unnamed x22, local copies, waits for them, and re-layouts  6.71 us
    dot_general x1, matrix products, per_device(): lax.dot_general(picked, grad_pre, (((0,), (0,)), ((), ())), preferred_ele...  4.88 us
  transfers between devices with their start and end apart: 5, of which 4 were waited for; matrix products, arithmetic and copies ran while one was open for 9% of the time, Pallas kernels for 0%

commit v1 on v0

v1 whole, which is shorter than its diff:
```python
import jax
import jax.numpy as jnp
from jax import lax
from jax.sharding import PartitionSpec as P

outer_momentum = 0.9
outer_rate = 0.7


def passed_along(x, axis, by):
    length = lax.axis_size(axis)
    return lax.ppermute(x, axis, [(i, (i + by) % length) for i in range(length)])


def gelu_tanh(value):
    return jax.nn.gelu(value, approximate=True)


def nesterov(params, moment, grad):
    moment_new = outer_momentum * moment + grad
    return (params - outer_rate * (grad + outer_momentum * moment_new), moment_new)


def snake(length):
    return list(range(0, length, 2)) + list(range(length - 1, 0, -2))


def place_of(member, length):
    return jnp.where(member % 2 == 0, member // 2, length - 1 - member // 2)


def member_at(place, length):
    place = lax.rem(place + 2 * length, length)
    return jnp.where(place < length // 2, 2 * place, 2 * (length - 1 - place) + 1)


def ring_pairs(length):
    order = snake(length)
    up = [(order[i], order[(i + 1) % length]) for i in range(length)]
    return up, [(b, a) for a, b in up]


def ring_gather(shard, axis):
    length = lax.axis_size(axis)
    rows = shard.shape[0]
    half = rows // 2
    up, down = ring_pairs(length)
    place = place_of(lax.axis_index(axis), length)
    full = jnp.zeros((rows * length,) + shard.shape[1:], shard.dtype)

    def put(full, block, back, offset=0):
        return lax.dynamic_update_slice(
            full, block, (member_at(place + back, length) * rows + offset, 0)
        )

    full = put(full, shard, 0)
    forward = backward = shard
    for step in range(1, length // 2 + 1):
        if step == length // 2:
            forward, backward = forward[:half], backward[half:]
        forward = lax.ppermute(forward, axis, up)
        backward = lax.ppermute(backward, axis, down)
        full = put(full, forward, -step)
        full = put(full, backward, step, half if step == length // 2 else 0)
    return full


def ring_scatter(parts, axis):
    length = lax.axis_size(axis)
    up, down = ring_pairs(length)
    term = parts(length // 2)
    half = term.shape[0] // 2
    forward = lax.ppermute(term[:half].astype(jnp.bfloat16), axis, up)
    backward = lax.ppermute(term[half:].astype(jnp.bfloat16), axis, down)
    for left in range(length // 2 - 1, 0, -1):
        ahead, behind = parts(left), parts(-left)
        if left == length // 2 - 1:
            zero = jnp.zeros_like(forward)
            forward = jnp.concatenate([forward, zero])
            backward = jnp.concatenate([zero, backward])
        forward = (ahead + forward.astype(jnp.float32)).astype(jnp.bfloat16)
        backward = (behind + backward.astype(jnp.float32)).astype(jnp.bfloat16)
        forward = lax.ppermute(forward, axis, up)
        backward = lax.ppermute(backward, axis, down)
    return parts(0) + forward.astype(jnp.float32) + backward.astype(jnp.float32)


def doubling_gather(shard, axis):
    length = lax.axis_size(axis)
    me = lax.axis_index(axis)
    rows = shard.shape[0]
    held = shard[None]
    members = [me]
    bit = length // 2
    while bit >= 1:
        other = lax.ppermute(held, axis, [(i, i ^ bit) for i in range(length)])
        held = jnp.concatenate([held, other])
        members = members + [m ^ bit for m in members]
        bit //= 2
    full = jnp.zeros((rows * length,) + shard.shape[1:], shard.dtype)
    for k, member in enumerate(members):
        full = lax.dynamic_update_slice(full, held[k], (member * rows, 0))
    return full


def halving_scatter(terms, axis):
    length = lax.axis_size(axis)
    me = lax.axis_index(axis)
    rows = terms.shape[0] // length
    held = terms.reshape((length, rows) + terms.shape[1:])
    bit = 1
    while bit < length:
        mine = (me // bit) % 2
        pairs = held.reshape((held.shape[0] // 2, 2) + held.shape[1:])
        away = lax.dynamic_index_in_dim(pairs, 1 - mine, 1, keepdims=False)
        kept = lax.dynamic_index_in_dim(pairs, mine, 1, keepdims=False)
        came = lax.ppermute(away.astype(jnp.bfloat16), axis, [(i, i ^ bit) for i in range(length)])
        held = kept.astype(jnp.float32) + came.astype(jnp.float32)
        bit *= 2
    return held[0]


def per_device(hidden_in, targets, first_params, first_moment, second_params, second_moment):
    inputs = hidden_in[0, 0]
    wanted = targets[0, 0]
    tokens = inputs.shape[0]
    columns = lax.axis_size("col")
    offset = columns // 4
    first_full = ring_gather(first_params[0].astype(jnp.bfloat16), "col")
    second_full = doubling_gather(second_params[0].astype(jnp.bfloat16), "row")
    pre = jnp.dot(inputs, first_full, preferred_element_type=jnp.float32)
    active, slope = jax.vjp(gelu_tanh, pre)
    active_b = active.astype(jnp.bfloat16)
    output = jnp.dot(active_b, second_full, preferred_element_type=jnp.float32)
    error = ((output - wanted.astype(jnp.float32)) / tokens).astype(jnp.bfloat16)
    path_second = lax.dot_general(
        active_b, error, (((0,), (0,)), ((), ())), preferred_element_type=jnp.float32
    ).astype(jnp.bfloat16)
    second_grad = halving_scatter(path_second, "row") / lax.axis_size("row")
    back = lax.dot_general(
        error, second_full, (((1,), (1,)), ((), ())), preferred_element_type=jnp.float32
    )
    grad_pre = slope(back)[0].astype(jnp.bfloat16)
    path_first = lax.dot_general(
        inputs, grad_pre, (((0,), (0,)), ((), ())), preferred_element_type=jnp.float32
    ).astype(jnp.bfloat16)
    rows = first_params.shape[1]
    place = place_of(lax.axis_index("col"), columns)

    def part(away):
        block = lax.dynamic_slice_in_dim(path_first, member_at(place + away, columns) * rows, rows, 0)
        return block.astype(jnp.float32)

    first_grad = ring_scatter(part, "col") / columns
    first_params_new, first_moment_new = nesterov(first_params, first_moment, first_grad[None])
    second_upd, second_mom = nesterov(second_params, second_moment, second_grad[None])
    stacked = jnp.stack([second_upd, second_mom])
    moved = passed_along(stacked.astype(jnp.bfloat16), "col", offset).astype(stacked.dtype)
    return (first_params_new, first_moment_new, moved[0], moved[1])


def solution(mesh):
    return jax.shard_map(
        per_device,
        mesh=mesh,
        in_specs=(
            P("row", "col", None, None),
            P("row", "col", None, None),
            P("row", "col", None),
            P("row", "col", None),
            P("col", "row", None),
            P("col", "row", None),
        ),
        out_specs=(
            P("row", "col", None),
            P("row", "col", None),
            P("col", "row", None),
            P("col", "row", None),
        ),
        check_vma=False,
    )
```

time: 198 us -> 106 us (0.54)
  waiting for transfers between devices: 152 us -> 46.2 us
  starting transfers between devices: 1.66 us -> 22.2 us
  between operations: 13.9 us -> 0.96 us
  other arithmetic: 7.29 us -> 12.4 us
  local copies, waits for them, and re-layouts: 7.96 us -> 12 us
  matrix products: 14.6 us -> 11.6 us
    unnamed x5 -> x0, waiting for transfers between devices: 68 us -> none
    all_gather x2 -> x0, waiting for transfers between devices: 63.4 us -> none  [the longest x1 47 us: per_device(): lax.all_gather(first_params[0].astype(jnp.bfloat16), 'col', axis=0, tiled...]
    ppermute x0 -> x20, waiting for transfers between devices: none -> 46.2 us  [the longest x3 23.2 us: ring_scatter(): backward = lax.ppermute(backward, axis, down)]
    reduce_scatter x1 -> x0, waiting for transfers between devices: 21 us -> none  [per_device(): lax.psum_scatter(lax.dot_general(picked, error, (((0,), (0,)), ((), ())),...]
    ppermute x0 -> x20, starting transfers between devices: none -> 20.6 us  [the longest x4 8.44 us: ring_gather(): forward = lax.ppermute(forward, axis, up)]
    dynamic_update_slice x0 -> x11, local copies, waits for them, and re-layouts: none -> 3.6 us  [the longest x8 2.47 us: put(): lax.dynamic_update_slice(full, block, (member_at(place + back, length) *...]
    unnamed x22 -> x26, local copies, waits for them, and re-layouts: 6.71 us -> 4.4 us
    sub x0 -> x1, other arithmetic: none -> 1.98 us  [nesterov(): params - outer_rate * (grad + outer_momentum * moment_new)]
  transfers between devices with their start and end apart: 5 -> 21, of which waited for: 4 -> 12; matrix products, arithmetic and copies ran while one was open for 9% -> 20% of each run, Pallas kernels for 0% -> 0%
where the time goes in v1:
time: 106 us; the launch traced here: 105 us
  waiting for transfers between devices  46.2 us (44%)
  starting transfers between devices  22.2 us (21%)
  other arithmetic  12.4 us (12%)
  local copies, waits for them, and re-layouts  12 us (11%)
  matrix products  11.6 us (11%)
    ppermute x3, waiting for transfers between devices, ring_scatter(): backward = lax.ppermute(backward, axis, down)  23.2 us
    ppermute x4, waiting for transfers between devices, ring_gather(): forward = lax.ppermute(forward, axis, up)  9.01 us
    ppermute x4, starting transfers between devices, ring_gather(): forward = lax.ppermute(forward, axis, up)  8.44 us
    dot_general x1, matrix products, per_device(): lax.dot_general(inputs, grad_pre, (((0,), (0,)), ((), ())), preferred_ele...  5.2 us
    ppermute x3, starting transfers between devices, ring_scatter(): forward = lax.ppermute(forward, axis, up)  4.78 us
    ppermute x1, waiting for transfers between devices, ring_scatter(): backward = lax.ppermute(term[half:].astype(jnp.bfloat16), axis, down)  4.51 us
    unnamed x26, local copies, waits for them, and re-layouts  4.4 us
    ppermute x3, waiting for transfers between devices, ring_scatter(): forward = lax.ppermute(forward, axis, up)  3.19 us
  transfers between devices with their start and end apart: 21, of which 12 were waited for; matrix products, arithmetic and copies ran while one was open for 20% of the time, Pallas kernels for 0%

profile of v1, /device:TPU:0, one launch (start us, length us, event | category | flops | bytes accessed | tf_op | source)
XLA Modules:
  0.0 105.4 jit_solution(4154713717634066171)
XLA Ops:
  0.6 0.0 copy-start
  0.6 0.0 copy-start.3
  0.7 0.1 broadcast.45.clone
  0.8 0.9 copy-done.3
  1.7 0.7 constant_dynamic-update-slice_fusion.8
  2.4 1.2 %copy-done.7 = bf16[896,896]{1,0:T(8,128)(2,1)} copy-done((bf16[896,896]{1,0:T(8,128)(2,1)}, bf16[896,896]{1,0:T(8,128)(2,1)S(1)}, u32[]{:S(2)}) %copy-start.7) | copy-done | bytes 1605656
  3.6 3.1 %collective-permute-start = (bf16[112,896]{1,0:T(8,128)(2,1)}, bf16[112,896]{1,0:T(8,128)(2,1)}, u32[]{:S(2)}, u32[]{:S(2)}) collective-permute-start(bf16[112,896]{1,0:T(8,128)(2,1)} %get-tuple-element.9), channel_id=1, source_target_pairs={{0,2},{2,4},{4,6},{6,7},{7,5},{5,3},{3,1},{1,0},{8,10},{10,12},{12... | collective-permute-start | bytes 602120 | tf_op jit(solution)/shard_map/ppermute | solution.py:61
  6.7 0.1 broadcast.45.clone.1
  6.8 0.8 bitcast_dynamic-update-slice_fusion.1
  7.6 1.9 %collective-permute-start.8 = (bf16[1,224,896]{2,1,0:T(8,128)(2,1)}, bf16[1,224,896]{2,1,0:T(8,128)(2,1)}, u32[]{:S(2)}, u32[]{:S(2)}) collective-permute-start(bf16[1,224,896]{2,1,0:T(8,128)(2,1)} %get-tuple-element.7), channel_id=1, source_target_pairs={{0,16},{8,24},{16,0},{24,8},{1,17},{9,25},{17,1},{25,9},{2,18},{10... | collective-permute-start | bytes 1204232 | tf_op jit(solution)/shard_map/ppermute | solution.py:96
  9.6 2.3 %collective-permute-done = bf16[112,896]{1,0:T(8,128)(2,1)} collective-permute-done((bf16[112,896]{1,0:T(8,128)(2,1)}, bf16[112,896]{1,0:T(8,128)(2,1)}, u32[]{:S(2)}, u32[]{:S(2)}) %collective-permute-start) | collective-permute-done | bytes 200736 | tf_op jit(solution)/shard_map/ppermute | solution.py:61
  11.9 1.8 %collective-permute-start.2 = (bf16[112,896]{1,0:T(8,128)(2,1)}, bf16[112,896]{1,0:T(8,128)(2,1)S(1)}, u32[]{:S(2)}, u32[]{:S(2)}) collective-permute-start(bf16[112,896]{1,0:T(8,128)(2,1)} %collective-permute-done), channel_id=1, source_target_pairs={{0,2},{2,4},{4,6},{6,7},{7,5},{5,3},{3,1},{1,0},{8,10},{10,12},{12... | collective-permute-start | bytes 602120 | tf_op jit(solution)/shard_map/ppermute | solution.py:61
  13.7 0.2 collective-permute-start.3
  14.0 1.6 %constant_dynamic-update-slice_fusion.7 = bf16[896,896]{1,0:T(8,128)(2,1)} fusion(bf16[896,896]{1,0:T(8,128)(2,1)} %copy-done.7, bf16[112,896]{1,0:T(8,128)(2,1)} %collective-permute-done, s32[]{:T(128)S(6)} %select_n.136), kind=kLoop, calls=%fused_computation.69 | loop fusion | bytes 401412 | tf_op jit(solution)/shard_map/dynamic_update_slice | solution.py:52
  15.6 0.7 constant_dynamic-update-slice_fusion.6
  16.3 2.4 %collective-permute-done.8 = bf16[1,224,896]{2,1,0:T(8,128)(2,1)} collective-permute-done((bf16[1,224,896]{2,1,0:T(8,128)(2,1)}, bf16[1,224,896]{2,1,0:T(8,128)(2,1)}, u32[]{:S(2)}, u32[]{:S(2)}) %collective-permute-start.8) | collective-permute-done | bytes 401440 | tf_op jit(solution)/shard_map/ppermute | solution.py:96
  18.7 1.2 %pad_maximum_fusion = bf16[2,224,896]{2,1,0:T(8,128)(2,1)S(1)} fusion(bf16[1,224,896]{2,1,0:T(8,128)(2,1)} %collective-permute-done.8, bf16[1,224,896]{2,1,0:T(8,128)(2,1)} %get-tuple-element.7), kind=kLoop, calls=%fused_computation.25 | loop fusion | flops 401408 | bytes 1605632 | tf_op jit(solution)/shard_map/concatenate | solution.py:97
  19.9 0.1 collective-permute-start.9
  20.0 1.8 %collective-permute-start.4 = (bf16[112,896]{1,0:T(8,128)(2,1)S(1)}, bf16[112,896]{1,0:T(8,128)(2,1)S(1)}, u32[]{:S(2)}, u32[]{:S(2)}) collective-permute-start(bf16[112,896]{1,0:T(8,128)(2,1)S(1)} %collective-permute-done.2), channel_id=1, source_target_pairs={{0,2},{2,4},{4,6},{6,7},{7,5},{5,3},{3,1},{1,0},{8,10},{10,12},{12... | collective-permute-start | bytes 602120 | tf_op jit(solution)/shard_map/ppermute | solution.py:61
  21.8 0.3 collective-permute-start.5
  22.1 1.0 bitcast_dynamic-update-slice_fusion
  23.2 4.2 %collective-permute-done.4 = bf16[112,896]{1,0:T(8,128)(2,1)S(1)} collective-permute-done((bf16[112,896]{1,0:T(8,128)(2,1)S(1)}, bf16[112,896]{1,0:T(8,128)(2,1)S(1)}, u32[]{:S(2)}, u32[]{:S(2)}) %collective-permute-start.4) | collective-permute-done | bytes 200736 | tf_op jit(solution)/shard_map/ppermute | solution.py:61
  27.4 1.8 %collective-permute-start.6 = (bf16[56,896]{1,0:T(8,128)(2,1)S(1)}, bf16[56,896]{1,0:T(8,128)(2,1)S(1)}, u32[]{:S(2)}, u32[]{:S(2)}) collective-permute-start(bf16[56,896]{1,0:T(8,128)(2,1)S(1)} %slice.34), channel_id=1, source_target_pairs={{0,2},{2,4},{4,6},{6,7},{7,5},{5,3},{3,1},{1,0},{8,10},{10,12},{12... | collective-permute-start | bytes 301064 | tf_op jit(solution)/shard_map/ppermute | solution.py:61
  29.2 0.3 collective-permute-start.7
  29.6 2.5 %collective-permute-done.6 = bf16[56,896]{1,0:T(8,128)(2,1)S(1)} collective-permute-done((bf16[56,896]{1,0:T(8,128)(2,1)S(1)}, bf16[56,896]{1,0:T(8,128)(2,1)S(1)}, u32[]{:S(2)}, u32[]{:S(2)}) %collective-permute-start.6) | collective-permute-done | bytes 100384 | tf_op jit(solution)/shard_map/ppermute | solution.py:61
  32.1 1.8 %collective-permute-done.7 = bf16[56,896]{1,0:T(8,128)(2,1)S(1)} collective-permute-done((bf16[56,896]{1,0:T(8,128)(2,1)S(1)}, bf16[56,896]{1,0:T(8,128)(2,1)S(1)}, u32[]{:S(2)}, u32[]{:S(2)}) %collective-permute-start.7) | collective-permute-done | bytes 100384 | tf_op jit(solution)/shard_map/ppermute | solution.py:62
  33.9 1.2 %fusion.13 = f32[896,512]{1,0:T(8,128)S(1)} fusion(bf16[896,896]{1,0:T(8,128)(2,1)S(1)} %constant_dynamic-update-slice_fusion, bf16[1,1,512,896]{3,2,1,0:T(8,128)(2,1)S(1)} %copy-done), kind=kOutput, calls=%fused_computation.21 | convolution fusion | flops 822083584 | bytes 4358144 | tf_op jit(solution)/shard_map/dot_general | solution.py:131
  35.1 0.0 copy-start.11
  35.3 1.1 %copy-done.12 = f32[896,512]{1,0:T(8,128)} copy-done((f32[896,512]{1,0:T(8,128)}, f32[896,512]{1,0:T(8,128)S(1)}, u32[]{:S(2)}) %copy-start.12) | copy-done | bytes 1835032
  36.4 1.1 %copy-done.6 = bf16[896,896]{1,0:T(8,128)(2,1)} copy-done((bf16[896,896]{1,0:T(8,128)(2,1)}, bf16[896,896]{1,0:T(8,128)(2,1)S(1)}, u32[]{:S(2)}) %copy-start.6) | copy-done | bytes 1605656
  37.5 2.3 %fusion.8 = bf16[512,896]{1,0:T(8,128)(2,1)} fusion(bf16[896,896]{1,0:T(8,128)(2,1)S(1)} %fusion.18, bf16[1,1,512,896]{3,2,1,0:T(8,128)(2,1)S(1)} %copy-done.11, f32[896,512]{1,0:T(8,128)S(1)} %fusion.13), kind=kOutput, calls=%fused_computation.11 | convolution fusion | flops 828047360 | bytes 5275648 | tf_op jit(solution)/shard_map/dot_general | solution.py:134
  39.8 5.2 %convolution_convert_fusion.1 = bf16[896,896]{0,1:T(8,128)(2,1)S(1)} fusion(bf16[1,1,512,896]{3,2,1,0:T(8,128)(2,1)S(1)} %copy-done, f32[896,512]{1,0:T(8,128)} %copy-done.12, bf16[512,896]{1,0:T(8,128)(2,1)} %fusion.8, bf16[896,896]{1,0:T(8,128)(2,1)} %copy-done.6), kind=kOutput, calls=%fused_computation.18 | convolution fusion | flops 1654145024 | bytes 6881280 | tf_op jit(solution)/shard_map/dot_general | solution.py:144
  45.0 0.7 fusion.39
  45.8 1.6 %collective-permute-start.10 = (bf16[56,896]{1,0:T(8,128)(2,1)S(1)}, bf16[56,896]{1,0:T(8,128)(2,1)S(1)}, u32[]{:S(2)}, u32[]{:S(2)}) collective-permute-start(bf16[56,896]{1,0:T(8,128)(2,1)S(1)} %get-tuple-element.16), channel_id=1, source_target_pairs={{0,2},{2,4},{4,6},{6,7},{7,5},{5,3},{3,1},{1,0},{8,10},{10,12},{12... | collective-permute-start | bytes 301064 | tf_op jit(solution)/shard_map/ppermute | solution.py:73
  47.4 3.0 %convolution_convert_fusion = bf16[896,896]{1,0:T(8,128)(2,1)S(1)} fusion(bf16[512,896]{1,0:T(8,128)(2,1)} %fusion.8, f32[896,512]{1,0:T(8,128)} %copy-done.12), kind=kOutput, calls=%fused_computation.17 | convolution fusion | flops 827015168 | bytes 4358144 | tf_op jit(solution)/shard_map/dot_general | solution.py:136
  50.3 0.1 collective-permute-done.10
  50.5 1.6 %collective-permute-start.11 = (bf16[112,896]{1,0:T(8,128)(2,1)S(1)}, bf16[112,896]{1,0:T(8,128)(2,1)S(1)}, u32[]{:S(2)}, u32[]{:S(2)}) collective-permute-start(bf16[112,896]{1,0:T(8,128)(2,1)S(1)} %fusion.25), channel_id=1, source_target_pairs={{0,2},{2,4},{4,6},{6,7},{7,5},{5,3},{3,1},{1,0},{8,10},{10,12},{12... | collective-permute-start | bytes 602120 | tf_op jit(solution)/shard_map/ppermute | solution.py:83
  52.1 0.9 dynamic-slice_bitcast_fusion
  53.0 3.2 %collective-permute-done.11 = bf16[112,896]{1,0:T(8,128)(2,1)S(1)} collective-permute-done((bf16[112,896]{1,0:T(8,128)(2,1)S(1)}, bf16[112,896]{1,0:T(8,128)(2,1)S(1)}, u32[]{:S(2)}, u32[]{:S(2)}) %collective-permute-start.11) | collective-permute-done | bytes 200736 | tf_op jit(solution)/shard_map/ppermute | solution.py:83
  56.2 0.7 fusion.26
  57.0 1.6 %collective-permute-start.12 = (bf16[112,896]{1,0:T(8,128)(2,1)}, bf16[112,896]{1,0:T(8,128)(2,1)S(1)}, u32[]{:S(2)}, u32[]{:S(2)}) collective-permute-start(bf16[112,896]{1,0:T(8,128)(2,1)} %fusion.26), channel_id=1, source_target_pairs={{0,2},{2,4},{4,6},{6,7},{7,5},{5,3},{3,1},{1,0},{8,10},{10,12},{12... | collective-permute-start | bytes 602120 | tf_op jit(solution)/shard_map/ppermute | solution.py:83
  58.5 0.4 collective-permute-start.14
  59.0 4.5 %collective-permute-done.14 = bf16[56,896]{1,0:T(8,128)(2,1)} collective-permute-done((bf16[56,896]{1,0:T(8,128)(2,1)}, bf16[56,896]{1,0:T(8,128)(2,1)}, u32[]{:S(2)}, u32[]{:S(2)}) %collective-permute-start.14) | collective-permute-done | bytes 100384 | tf_op jit(solution)/shard_map/ppermute | solution.py:74
  63.5 1.7 %fusion.27 = (bf16[112,896]{1,0:T(8,128)(2,1)}, bf16[112,896]{1,0:T(8,128)(2,1)}) fusion(bf16[112,896]{1,0:T(8,128)(2,1)S(1)} %collective-permute-done.12, bf16[896,896]{0,1:T(8,128)(2,1)S(1)} %convolution_convert_fusion.1, s32[]{:T(128)S(6)} %select_n.138, bf16[56,896]{1,0:T(8,128)(2,1)} %collective-permute-done.14, s32[]{:T(128)S(6)} %select_n.144), kind=kLoop, calls=%fused_computation.53 | loop fusion | flops 802816 | bytes 1103880 | tf_op jit(solution)/shard_map/convert_element_type | solution.py:81
  65.2 0.4 collective-permute-start.15
  65.7 1.5 %convert_add_fusion = f32[2,224,896]{2,1,0:T(8,128)S(1)} fusion(bf16[2,224,896]{2,1,0:T(8,128)(2,1)} %collective-permute-done.18, bf16[2,2,224,896]{3,2,1,0:T(8,128)(2,1)} %bitcast.110, s32[]{:T(128)S(6)} %select_n.157), kind=kLoop, calls=%fused_computation.19 | loop fusion | flops 1204224 | bytes 3211268 | tf_op jit(solution)/shard_map/add | solution.py:118
  67.2 0.8 dynamic-slice_convert_fusion
  68.0 1.5 %collective-permute-start.19 = (bf16[1,224,896]{2,1,0:T(8,128)(2,1)}, bf16[1,224,896]{2,1,0:T(8,128)(2,1)}, u32[]{:S(2)}, u32[]{:S(2)}) collective-permute-start(bf16[1,224,896]{2,1,0:T(8,128)(2,1)} %dynamic-slice_convert_fusion), channel_id=1, source_target_pairs={{0,16},{8,24},{16,0},{24,8},{1,17},{9,25},{17,1},{25,9},{2,18},{10... | collective-permute-start | bytes 1204232 | tf_op jit(solution)/shard_map/ppermute | solution.py:117
  69.5 3.3 %collective-permute-done.15 = bf16[112,896]{1,0:T(8,128)(2,1)S(1)} collective-permute-done((bf16[112,896]{1,0:T(8,128)(2,1)}, bf16[112,896]{1,0:T(8,128)(2,1)S(1)}, u32[]{:S(2)}, u32[]{:S(2)}) %collective-permute-start.15) | collective-permute-done | bytes 200736 | tf_op jit(solution)/shard_map/ppermute | solution.py:84
  72.8 1.0 fusion.23
  73.7 0.5 collective-permute-start.16
  74.2 2.0 %collective-permute-done.19 = bf16[1,224,896]{2,1,0:T(8,128)(2,1)} collective-permute-done((bf16[1,224,896]{2,1,0:T(8,128)(2,1)}, bf16[1,224,896]{2,1,0:T(8,128)(2,1)}, u32[]{:S(2)}, u32[]{:S(2)}) %collective-permute-start.19) | collective-permute-done | bytes 401440 | tf_op jit(solution)/shard_map/ppermute | solution.py:117
  76.2 1.5 %fusion.30 = (bf16[1,1,224,896]{3,2,1,0:T(8,128)(2,1)S(1)}, bf16[1,1,224,896]{3,2,1,0:T(8,128)(2,1)S(1)}) fusion(f32[1,224,896]{2,1,0:T(8,128)S(1)} %copy-done.1, f32[1,224,896]{2,1,0:T(8,128)} %param.11, bf16[1,224,896]{2,1,0:T(8,128)(2,1)} %collective-permute-done.19, f32[2,224,896]{2,1,0:T(8,128)S(1)} %convert_add_fusion, s32[]{:T(128)S(6)} %select_n.161), kind=kLoop, calls=%fused_computation.59 | loop fusion | flops 2207744 | bytes 3612676 | tf_op jit(solution)/shard_map/stack | solution.py:157
  77.7 0.0 copy-start.9
  77.7 0.1 pad_maximum_fusion.1
  77.8 1.6 %collective-permute-start.20 = (bf16[2,1,224,896]{3,2,1,0:T(8,128)(2,1)S(1)}, bf16[2,1,224,896]{3,2,1,0:T(8,128)(2,1)S(1)}, u32[]{:S(2)}, u32[]{:S(2)}) collective-permute-start(bf16[2,1,224,896]{3,2,1,0:T(8,128)(2,1)S(1)} %pad_maximum_fusion.1), channel_id=1, source_target_pairs={{0,2},{1,3},{2,4},{3,5},{4,6},{5,7},{6,0},{7,1},{8,10},{9,11},{10,... | collective-permute-start | bytes 2408456 | tf_op jit(solution)/shard_map/ppermute | solution.py:12
  79.5 1.6 %collective-permute-start.13 = (bf16[112,896]{1,0:T(8,128)(2,1)S(1)}, bf16[112,896]{1,0:T(8,128)(2,1)S(1)}, u32[]{:S(2)}, u32[]{:S(2)}) collective-permute-start(bf16[112,896]{1,0:T(8,128)(2,1)S(1)} %copy-done.10), channel_id=1, source_target_pairs={{0,2},{2,4},{4,6},{6,7},{7,5},{5,3},{3,1},{1,0},{8,10},{10,12},{12... | collective-permute-start | bytes 602120 | tf_op jit(solution)/shard_map/ppermute | solution.py:83
  81.0 14.3 %collective-permute-done.16 = bf16[112,896]{1,0:T(8,128)(2,1)S(1)} collective-permute-done((bf16[112,896]{1,0:T(8,128)(2,1)S(1)}, bf16[112,896]{1,0:T(8,128)(2,1)S(1)}, u32[]{:S(2)}, u32[]{:S(2)}) %collective-permute-start.16) | collective-permute-done | bytes 200736 | tf_op jit(solution)/shard_map/ppermute | solution.py:84
  95.3 1.0 fusion.24
  96.3 0.1 collective-permute-start.17
  96.3 5.7 %collective-permute-done.17 = bf16[112,896]{1,0:T(8,128)(2,1)S(1)} collective-permute-done((bf16[112,896]{1,0:T(8,128)(2,1)S(1)}, bf16[112,896]{1,0:T(8,128)(2,1)S(1)}, u32[]{:S(2)}, u32[]{:S(2)}) %collective-permute-start.17) | collective-permute-done | bytes 200736 | tf_op jit(solution)/shard_map/ppermute | solution.py:84
  102.0 2.0 %fusion.21 = (f32[1,112,896]{2,1,0:T(8,128)}, f32[1,112,896]{2,1,0:T(8,128)}) fusion(f32[1,112,896]{2,1,0:T(8,128)S(1)} %copy-done.4, bf16[112,896]{1,0:T(8,128)(2,1)S(1)} %collective-permute-done.17, bf16[112,896]{1,0:T(8,128)(2,1)S(1)} %collective-permute-done.13, bf16[896,896]{0,1:T(8,128)(2,1)} %copy-done.2, s32[]{:T(128)S(6)} %select_n.134, ...), kind=kLoop, calls=%fused_computation.41 | loop fusion | flops 1204224 | bytes 2207748 | tf_op jit(solution)/shard_map/sub | solution.py:21
  104.0 0.1 convert_element_type.199
  104.1 1.3 %slice_bitcast_fusion = (f32[1,224,896]{2,1,0:T(8,128)}, f32[1,224,896]{2,1,0:T(8,128)}) fusion(f32[2,1,224,896]{3,2,1,0:T(8,128)S(1)} %convert_element_type.199), kind=kLoop, calls=%fused_computation.23 | loop fusion | bytes 3211264 | tf_op jit(solution)/shard_map/squeeze | solution.py:159
  (41 shorter events, 0.4 us)
Async XLA Ops:
  0.6 33.3 %copy-start = (bf16[1,1,512,896]{3,2,1,0:T(8,128)(2,1)S(1)}, bf16[1,1,512,896]{3,2,1,0:T(8,128)(2,1)}, u32[]{:S(2)}) copy-start(bf16[1,1,512,896]{3,2,1,0:T(8,128)(2,1)} %param.6) | copy-start | bytes 2752516
  0.6 1.1 %copy-start.3 = (f32[1,112,896]{2,1,0:T(8,128)S(1)}, f32[1,112,896]{2,1,0:T(8,128)}, u32[]{:S(2)}) copy-start(f32[1,112,896]{2,1,0:T(8,128)} %param.8) | copy-start | bytes 1204228
  1.7 5.1 %copy-start.1 = (f32[1,224,896]{2,1,0:T(8,128)S(1)}, f32[1,224,896]{2,1,0:T(8,128)}, u32[]{:S(2)}) copy-start(f32[1,224,896]{2,1,0:T(8,128)} %param.10) | copy-start | bytes 2408452
  2.4 1.2 %copy-start.7 = (bf16[896,896]{1,0:T(8,128)(2,1)}, bf16[896,896]{1,0:T(8,128)(2,1)S(1)}, u32[]{:S(2)}) copy-start(bf16[896,896]{1,0:T(8,128)(2,1)S(1)} %get-tuple-element.8) | copy-start | bytes 4816900
  3.6 8.3 %collective-permute-start = (bf16[112,896]{1,0:T(8,128)(2,1)}, bf16[112,896]{1,0:T(8,128)(2,1)}, u32[]{:S(2)}, u32[]{:S(2)}) collective-permute-start(bf16[112,896]{1,0:T(8,128)(2,1)} %get-tuple-element.9), channel_id=1, source_target_pairs={{0,2},{2,4},{4,6},{6,7},{7,5},{5,3},{3,1},{1,0},{8,10},{10,12},{12... | collective-permute-start | bytes 602120 | tf_op jit(solution)/shard_map/ppermute | solution.py:61
  6.7 7.0 %collective-permute-start.1 = (bf16[112,896]{1,0:T(8,128)(2,1)}, bf16[112,896]{1,0:T(8,128)(2,1)S(1)}, u32[]{:S(2)}, u32[]{:S(2)}) collective-permute-start(bf16[112,896]{1,0:T(8,128)(2,1)} %get-tuple-element.9), channel_id=1, source_target_pairs={{2,0},{4,2},{6,4},{7,6},{5,7},{3,5},{1,3},{0,1},{10,8},{12,10},{14... | collective-permute-start | bytes 602120 | tf_op jit(solution)/shard_map/ppermute | solution.py:62
  7.6 11.1 %collective-permute-start.8 = (bf16[1,224,896]{2,1,0:T(8,128)(2,1)}, bf16[1,224,896]{2,1,0:T(8,128)(2,1)}, u32[]{:S(2)}, u32[]{:S(2)}) collective-permute-start(bf16[1,224,896]{2,1,0:T(8,128)(2,1)} %get-tuple-element.7), channel_id=1, source_target_pairs={{0,16},{8,24},{16,0},{24,8},{1,17},{9,25},{17,1},{25,9},{2,18},{10... | collective-permute-start | bytes 1204232 | tf_op jit(solution)/shard_map/ppermute | solution.py:96
  11.9 8.1 %collective-permute-start.2 = (bf16[112,896]{1,0:T(8,128)(2,1)}, bf16[112,896]{1,0:T(8,128)(2,1)S(1)}, u32[]{:S(2)}, u32[]{:S(2)}) collective-permute-start(bf16[112,896]{1,0:T(8,128)(2,1)} %collective-permute-done), channel_id=1, source_target_pairs={{0,2},{2,4},{4,6},{6,7},{7,5},{5,3},{3,1},{1,0},{8,10},{10,12},{12... | collective-permute-start | bytes 602120 | tf_op jit(solution)/shard_map/ppermute | solution.py:61
  13.7 8.1 %collective-permute-start.3 = (bf16[112,896]{1,0:T(8,128)(2,1)S(1)}, bf16[112,896]{1,0:T(8,128)(2,1)S(1)}, u32[]{:S(2)}, u32[]{:S(2)}) collective-permute-start(bf16[112,896]{1,0:T(8,128)(2,1)S(1)} %collective-permute-done.1), channel_id=1, source_target_pairs={{2,0},{4,2},{6,4},{7,6},{5,7},{3,5},{1,3},{0,1},{10,8},{12,10},{14... | collective-permute-start | bytes 602120 | tf_op jit(solution)/shard_map/ppermute | solution.py:62
  16.3 6.9 %copy-start.8 = (bf16[896,896]{1,0:T(8,128)(2,1)S(1)}, bf16[896,896]{1,0:T(8,128)(2,1)}, u32[]{:S(2)}) copy-start(bf16[896,896]{1,0:T(8,128)(2,1)} %constant_dynamic-update-slice_fusion.6) | copy-start | bytes 4816900
  19.9 15.2 %collective-permute-start.9 = (bf16[2,224,896]{2,1,0:T(8,128)(2,1)S(1)}, bf16[2,224,896]{2,1,0:T(8,128)(2,1)S(1)}, u32[]{:S(2)}, u32[]{:S(2)}) collective-permute-start(bf16[2,224,896]{2,1,0:T(8,128)(2,1)S(1)} %pad_maximum_fusion), channel_id=1, source_target_pairs={{0,8},{8,0},{16,24},{24,16},{1,9},{9,1},{17,25},{25,17},{2,10},{10... | collective-permute-start | bytes 2408456 | tf_op jit(solution)/shard_map/ppermute | solution.py:96
  20.0 7.4 %collective-permute-start.4 = (bf16[112,896]{1,0:T(8,128)(2,1)S(1)}, bf16[112,896]{1,0:T(8,128)(2,1)S(1)}, u32[]{:S(2)}, u32[]{:S(2)}) collective-permute-start(bf16[112,896]{1,0:T(8,128)(2,1)S(1)} %collective-permute-done.2), channel_id=1, source_target_pairs={{0,2},{2,4},{4,6},{6,7},{7,5},{5,3},{3,1},{1,0},{8,10},{10,12},{12... | collective-permute-start | bytes 602120 | tf_op jit(solution)/shard_map/ppermute | solution.py:61
  21.8 7.4 %collective-permute-start.5 = (bf16[112,896]{1,0:T(8,128)(2,1)S(1)}, bf16[112,896]{1,0:T(8,128)(2,1)S(1)}, u32[]{:S(2)}, u32[]{:S(2)}) collective-permute-start(bf16[112,896]{1,0:T(8,128)(2,1)S(1)} %collective-permute-done.3), channel_id=1, source_target_pairs={{2,0},{4,2},{6,4},{7,6},{5,7},{3,5},{1,3},{0,1},{10,8},{12,10},{14... | collective-permute-start | bytes 602120 | tf_op jit(solution)/shard_map/ppermute | solution.py:62
  27.4 4.7 %collective-permute-start.6 = (bf16[56,896]{1,0:T(8,128)(2,1)S(1)}, bf16[56,896]{1,0:T(8,128)(2,1)S(1)}, u32[]{:S(2)}, u32[]{:S(2)}) collective-permute-start(bf16[56,896]{1,0:T(8,128)(2,1)S(1)} %slice.34), channel_id=1, source_target_pairs={{0,2},{2,4},{4,6},{6,7},{7,5},{5,3},{3,1},{1,0},{8,10},{10,12},{12... | collective-permute-start | bytes 301064 | tf_op jit(solution)/shard_map/ppermute | solution.py:61
  29.2 4.7 %collective-permute-start.7 = (bf16[56,896]{1,0:T(8,128)(2,1)S(1)}, bf16[56,896]{1,0:T(8,128)(2,1)S(1)}, u32[]{:S(2)}, u32[]{:S(2)}) collective-permute-start(bf16[56,896]{1,0:T(8,128)(2,1)S(1)} %slice.35), channel_id=1, source_target_pairs={{2,0},{4,2},{6,4},{7,6},{5,7},{3,5},{1,3},{0,1},{10,8},{12,10},{14... | collective-permute-start | bytes 301064 | tf_op jit(solution)/shard_map/ppermute | solution.py:62
  35.1 1.3 %copy-start.12 = (f32[896,512]{1,0:T(8,128)}, f32[896,512]{1,0:T(8,128)S(1)}, u32[]{:S(2)}) copy-start(f32[896,512]{1,0:T(8,128)S(1)} %fusion.13) | copy-start | bytes 5505028
  35.1 2.4 %copy-start.11 = (bf16[1,1,512,896]{3,2,1,0:T(8,128)(2,1)S(1)}, bf16[1,1,512,896]{3,2,1,0:T(8,128)(2,1)}, u32[]{:S(2)}) copy-start(bf16[1,1,512,896]{3,2,1,0:T(8,128)(2,1)} %param.7) | copy-start | bytes 2752516
  36.4 1.1 %copy-start.6 = (bf16[896,896]{1,0:T(8,128)(2,1)}, bf16[896,896]{1,0:T(8,128)(2,1)S(1)}, u32[]{:S(2)}) copy-start(bf16[896,896]{1,0:T(8,128)(2,1)S(1)} %fusion.18) | copy-start | bytes 4816900
  45.0 18.5 %copy-start.2 = (bf16[896,896]{0,1:T(8,128)(2,1)}, bf16[896,896]{0,1:T(8,128)(2,1)S(1)}, u32[]{:S(2)}) copy-start(bf16[896,896]{0,1:T(8,128)(2,1)S(1)} %convolution_convert_fusion.1) | copy-start | bytes 4816900
  45.8 4.6 %collective-permute-start.10 = (bf16[56,896]{1,0:T(8,128)(2,1)S(1)}, bf16[56,896]{1,0:T(8,128)(2,1)S(1)}, u32[]{:S(2)}, u32[]{:S(2)}) collective-permute-start(bf16[56,896]{1,0:T(8,128)(2,1)S(1)} %get-tuple-element.16), channel_id=1, source_target_pairs={{0,2},{2,4},{4,6},{6,7},{7,5},{5,3},{3,1},{1,0},{8,10},{10,12},{12... | collective-permute-start | bytes 301064 | tf_op jit(solution)/shard_map/ppermute | solution.py:73
  50.3 1.8 %copy-start.5 = (bf16[896,896]{1,0:T(8,128)(2,1)}, bf16[896,896]{1,0:T(8,128)(2,1)S(1)}, u32[]{:S(2)}) copy-start(bf16[896,896]{1,0:T(8,128)(2,1)S(1)} %convolution_convert_fusion) | copy-start | bytes 4816900
  50.5 5.8 %collective-permute-start.11 = (bf16[112,896]{1,0:T(8,128)(2,1)S(1)}, bf16[112,896]{1,0:T(8,128)(2,1)S(1)}, u32[]{:S(2)}, u32[]{:S(2)}) collective-permute-start(bf16[112,896]{1,0:T(8,128)(2,1)S(1)} %fusion.25), channel_id=1, source_target_pairs={{0,2},{2,4},{4,6},{6,7},{7,5},{5,3},{3,1},{1,0},{8,10},{10,12},{12... | collective-permute-start | bytes 602120 | tf_op jit(solution)/shard_map/ppermute | solution.py:83
  53.0 12.6 %collective-permute-start.18 = (bf16[2,224,896]{2,1,0:T(8,128)(2,1)}, bf16[2,224,896]{2,1,0:T(8,128)(2,1)}, u32[]{:S(2)}, u32[]{:S(2)}) collective-permute-start(bf16[2,224,896]{2,1,0:T(8,128)(2,1)} %dynamic-slice_bitcast_fusion), channel_id=1, source_target_pairs={{0,8},{8,0},{16,24},{24,16},{1,9},{9,1},{17,25},{25,17},{2,10},{10... | collective-permute-start | bytes 2408456 | tf_op jit(solution)/shard_map/ppermute | solution.py:117
  57.0 6.5 %collective-permute-start.12 = (bf16[112,896]{1,0:T(8,128)(2,1)}, bf16[112,896]{1,0:T(8,128)(2,1)S(1)}, u32[]{:S(2)}, u32[]{:S(2)}) collective-permute-start(bf16[112,896]{1,0:T(8,128)(2,1)} %fusion.26), channel_id=1, source_target_pairs={{0,2},{2,4},{4,6},{6,7},{7,5},{5,3},{3,1},{1,0},{8,10},{10,12},{12... | collective-permute-start | bytes 602120 | tf_op jit(solution)/shard_map/ppermute | solution.py:83
  58.5 5.0 %collective-permute-start.14 = (bf16[56,896]{1,0:T(8,128)(2,1)}, bf16[56,896]{1,0:T(8,128)(2,1)}, u32[]{:S(2)}, u32[]{:S(2)}) collective-permute-start(bf16[56,896]{1,0:T(8,128)(2,1)} %get-tuple-element.17), channel_id=1, source_target_pairs={{2,0},{4,2},{6,4},{7,6},{5,7},{3,5},{1,3},{0,1},{10,8},{12,10},{14... | collective-permute-start | bytes 301064 | tf_op jit(solution)/shard_map/ppermute | solution.py:74
  65.2 7.5 %collective-permute-start.15 = (bf16[112,896]{1,0:T(8,128)(2,1)}, bf16[112,896]{1,0:T(8,128)(2,1)S(1)}, u32[]{:S(2)}, u32[]{:S(2)}) collective-permute-start(bf16[112,896]{1,0:T(8,128)(2,1)} %get-tuple-element.15), channel_id=1, source_target_pairs={{2,0},{4,2},{6,4},{7,6},{5,7},{3,5},{1,3},{0,1},{10,8},{12,10},{14... | collective-permute-start | bytes 602120 | tf_op jit(solution)/shard_map/ppermute | solution.py:84
  68.0 8.2 %collective-permute-start.19 = (bf16[1,224,896]{2,1,0:T(8,128)(2,1)}, bf16[1,224,896]{2,1,0:T(8,128)(2,1)}, u32[]{:S(2)}, u32[]{:S(2)}) collective-permute-start(bf16[1,224,896]{2,1,0:T(8,128)(2,1)} %dynamic-slice_convert_fusion), channel_id=1, source_target_pairs={{0,16},{8,24},{16,0},{24,8},{1,17},{9,25},{17,1},{25,9},{2,18},{10... | collective-permute-start | bytes 1204232 | tf_op jit(solution)/shard_map/ppermute | solution.py:117
  73.7 21.6 %collective-permute-start.16 = (bf16[112,896]{1,0:T(8,128)(2,1)S(1)}, bf16[112,896]{1,0:T(8,128)(2,1)S(1)}, u32[]{:S(2)}, u32[]{:S(2)}) collective-permute-start(bf16[112,896]{1,0:T(8,128)(2,1)S(1)} %fusion.23), channel_id=1, source_target_pairs={{2,0},{4,2},{6,4},{7,6},{5,7},{3,5},{1,3},{0,1},{10,8},{12,10},{14... | collective-permute-start | bytes 602120 | tf_op jit(solution)/shard_map/ppermute | solution.py:84
  77.7 1.8 %copy-start.10 = (bf16[112,896]{1,0:T(8,128)(2,1)S(1)}, bf16[112,896]{1,0:T(8,128)(2,1)}, u32[]{:S(2)}) copy-start(bf16[112,896]{1,0:T(8,128)(2,1)} %get-tuple-element.14) | copy-start | bytes 602116
  77.7 24.3 %copy-start.4 = (f32[1,112,896]{2,1,0:T(8,128)S(1)}, f32[1,112,896]{2,1,0:T(8,128)}, u32[]{:S(2)}) copy-start(f32[1,112,896]{2,1,0:T(8,128)} %param.8) | copy-start | bytes 1204228
  77.7 24.3 %copy-start.9 = (f32[1,112,896]{2,1,0:T(8,128)S(1)}, f32[1,112,896]{2,1,0:T(8,128)}, u32[]{:S(2)}) copy-start(f32[1,112,896]{2,1,0:T(8,128)} %param.9) | copy-start | bytes 1204228
  77.8 26.2 %collective-permute-start.20 = (bf16[2,1,224,896]{3,2,1,0:T(8,128)(2,1)S(1)}, bf16[2,1,224,896]{3,2,1,0:T(8,128)(2,1)S(1)}, u32[]{:S(2)}, u32[]{:S(2)}) collective-permute-start(bf16[2,1,224,896]{3,2,1,0:T(8,128)(2,1)S(1)} %pad_maximum_fusion.1), channel_id=1, source_target_pairs={{0,2},{1,3},{2,4},{3,5},{4,6},{5,7},{6,0},{7,1},{8,10},{9,11},{10,... | collective-permute-start | bytes 2408456 | tf_op jit(solution)/shard_map/ppermute | solution.py:12
  79.5 16.9 %collective-permute-start.13 = (bf16[112,896]{1,0:T(8,128)(2,1)S(1)}, bf16[112,896]{1,0:T(8,128)(2,1)S(1)}, u32[]{:S(2)}, u32[]{:S(2)}) collective-permute-start(bf16[112,896]{1,0:T(8,128)(2,1)S(1)} %copy-done.10), channel_id=1, source_target_pairs={{0,2},{2,4},{4,6},{6,7},{7,5},{5,3},{3,1},{1,0},{8,10},{10,12},{12... | collective-permute-start | bytes 602120 | tf_op jit(solution)/shard_map/ppermute | solution.py:83
  96.3 5.8 %collective-permute-start.17 = (bf16[112,896]{1,0:T(8,128)(2,1)S(1)}, bf16[112,896]{1,0:T(8,128)(2,1)S(1)}, u32[]{:S(2)}, u32[]{:S(2)}) collective-permute-start(bf16[112,896]{1,0:T(8,128)(2,1)S(1)} %fusion.24), channel_id=1, source_target_pairs={{2,0},{4,2},{6,4},{7,6},{5,7},{3,5},{1,3},{0,1},{10,8},{12,10},{14... | collective-permute-start | bytes 602120 | tf_op jit(solution)/shard_map/ppermute | solution.py:84

commit v2 on v0

v2 whole, which is shorter than its diff:
```python
import math

import jax
import jax.numpy as jnp
from jax import lax
from jax.experimental import pallas as pl
from jax.experimental.pallas import tpu as pltpu
from jax.sharding import PartitionSpec as P

outer_momentum = 0.9
outer_rate = 0.7
BF16 = jnp.bfloat16
F32 = jnp.float32
WHOLE = pl.BlockSpec(memory_space=pltpu.VMEM)


def shape_of(shape, kind=BF16):
    return jax.ShapeDtypeStruct(shape, kind)


def call(kernel, outs, scratch, *operands, flops=0):
    moved = sum(o.size * o.dtype.itemsize for o in operands)
    return pl.pallas_call(
        kernel,
        out_shape=tuple(outs),
        in_specs=[WHOLE] * len(operands),
        out_specs=(WHOLE,) * len(outs),
        scratch_shapes=scratch,
        compiler_params=pltpu.CompilerParams(vmem_limit_bytes=32 * 2**20),
        cost_estimate=pl.CostEstimate(flops=flops, bytes_accessed=moved, transcendentals=0),
    )(*operands)


def tiled(rows):
    return rows % 16 == 0


def together(*values):
    return lax.optimization_barrier(values)


def place_of(member, length):
    return jnp.where(member % 2 == 0, member // 2, length - 1 - member // 2)


def member_at(place, length):
    place = lax.rem(place + 2 * length, length)
    return jnp.where(place < length // 2, 2 * place, 2 * (length - 1 - place) + 1)


def ring_pairs(length):
    order = list(range(0, length, 2)) + list(range(length - 1, 0, -2))
    up = [(order[i], order[(i + 1) % length]) for i in range(length)]
    return up, [(b, a) for a, b in up]


def swap_pairs(length, bit):
    return [(i, i ^ bit) for i in range(length)]


def gelu_and_slope(value):
    scale = math.sqrt(2 / math.pi)
    square = value * value
    bent = jnp.tanh(scale * (value + 0.044715 * value * square))
    half = 0.5 * (1 + bent)
    slope = half + (0.5 * scale) * value * (1 - bent * bent) * (1 + 3 * 0.044715 * square)
    return value * half, slope


def rows_from(pieces, rows, length):
    full = jnp.zeros((rows * length,) + pieces[0][0].shape[1:], pieces[0][0].dtype)
    for block, member, first in pieces:
        full = lax.dynamic_update_slice(full, block, (member * rows + first, 0))
    return full


def forward_kernel(first_plan, second_plan, columns, n_row, *refs):
    n1, n2 = len(first_plan), len(second_plan)
    first_refs, second_refs = refs[:n1], refs[n1 : n1 + n2]
    inputs, wanted = refs[n1 + n2 : n1 + n2 + 2]
    away, kept, error_ref, slope_ref, second_ref = refs[n1 + n2 + 2 : n1 + n2 + 7]
    first_full, active, grad = refs[n1 + n2 + 7 :]
    tokens, width = inputs.shape
    col, row = lax.axis_index("col"), lax.axis_index("row")
    place = place_of(col, columns)
    for ref, back in zip(first_refs, first_plan):
        if back is None:
            first_full[...] = ref[...]
        else:
            rows = ref.shape[0]
            first_full[pl.ds(pl.multiple_of(member_at(place + back, columns) * rows, rows), rows), :] = ref[...]
    for ref, flips in zip(second_refs, second_plan):
        if flips is None:
            second_ref[...] = ref[...]
        else:
            rows = ref.shape[1]
            for k, flip in enumerate(flips):
                second_ref[pl.ds(pl.multiple_of((row ^ flip) * rows, rows), rows), :] = ref[k]
    pre = jnp.dot(inputs[...], first_full[...], preferred_element_type=F32)
    value, slope = gelu_and_slope(pre)
    active[...] = value.astype(BF16)
    slope_ref[...] = slope
    output = jnp.dot(active[...], second_ref[...], preferred_element_type=F32)
    error = ((output - wanted[...].astype(F32)) / tokens).astype(BF16)
    error_ref[...] = error
    grad[...] = lax.dot_general(
        active[...], error, (((0,), (0,)), ((), ())), preferred_element_type=F32
    ).astype(BF16)
    rows = width // n_row
    if tiled(rows):
        mine = row % 2
        for k in range(n_row // 2):
            for ref, side in ((away, 1 - mine), (kept, mine)):
                ref[k] = grad[pl.ds(pl.multiple_of((2 * k + side) * rows, rows), rows), :]
    else:
        away[...] = grad[: width // 2].reshape(away.shape)
        kept[...] = grad[width // 2 :].reshape(kept.shape)


def backward_kernel(columns, inputs, second_full, error, slope, *refs):
    outs, grad = refs[:-1], refs[-1]
    back = lax.dot_general(
        error[...], second_full[...], (((1,), (1,)), ((), ())), preferred_element_type=F32
    )
    grad_pre = (back * slope[...]).astype(BF16)
    value = lax.dot_general(
        inputs[...], grad_pre, (((0,), (0,)), ((), ())), preferred_element_type=F32
    )
    if len(outs) == 1:
        outs[0][...] = value.astype(BF16)
        return
    grad[...] = value
    place = place_of(lax.axis_index("col"), columns)
    rows = grad.shape[0] // columns
    half = rows // 2

    def block(away, first, count):
        start = member_at(place + away, columns) * rows + first
        return grad[pl.ds(pl.multiple_of(start, 8), count), :].astype(BF16)

    outs[0][...] = block(columns // 2, 0, half)
    outs[1][...] = block(columns // 2, half, half)
    outs[2][...] = block(0, 0, rows)
    for k in range(1, columns // 2):
        outs[2 * k + 1][...] = block(k, 0, rows)
        outs[2 * k + 2][...] = block(-k, 0, rows)


def add_kernel(ahead, forward, behind, backward, ahead_out, behind_out):
    rows, got = ahead.shape[0], forward.shape[0]
    if rows == got:
        ahead_out[...] = (ahead[...].astype(F32) + forward[...].astype(F32)).astype(BF16)
        behind_out[...] = (behind[...].astype(F32) + backward[...].astype(F32)).astype(BF16)
        return
    term = ahead[...].astype(F32)
    top = term[:got] + forward[...].astype(F32)
    ahead_out[...] = jnp.concatenate([top, term[got:]]).astype(BF16)
    term = behind[...].astype(F32)
    low = term[rows - got :] + backward[...].astype(F32)
    behind_out[...] = jnp.concatenate([term[: rows - got], low]).astype(BF16)


def add_both(ahead, forward, behind, backward):
    rows, got = ahead.shape[0], forward.shape[0]
    if tiled(rows):
        outs = [shape_of(ahead.shape)] * 2
        return call(add_kernel, outs, [], ahead, forward, behind, backward)
    zero = jnp.zeros((rows - got,) + forward.shape[1:], BF16)
    forward, backward = jnp.concatenate([forward, zero]), jnp.concatenate([zero, backward])
    return (
        (ahead.astype(F32) + forward.astype(F32)).astype(BF16),
        (behind.astype(F32) + backward.astype(F32)).astype(BF16),
    )


def first_kernel(columns, own, forward, backward, params, moment, params_out, moment_out):
    total = own[...].astype(F32) + forward[...].astype(F32) + backward[...].astype(F32)
    grad = total / columns
    moment_new = outer_momentum * moment[...] + grad
    moment_out[...] = moment_new
    params_out[...] = params[...] - outer_rate * (grad + outer_momentum * moment_new)


def halve_kernel(bit, kept, came, away_out, kept_out):
    mine = (lax.axis_index("row") // bit) % 2
    for k in range(kept_out.shape[0]):
        total = kept[2 * k + mine].astype(F32) + came[2 * k + mine].astype(F32)
        kept_out[k] = total
        other = kept[2 * k + 1 - mine].astype(F32) + came[2 * k + 1 - mine].astype(F32)
        away_out[k] = other.astype(BF16)


def per_device(hidden_in, targets, first_params, first_moment, second_params, second_moment):
    inputs, wanted = hidden_in[0, 0], targets[0, 0]
    tokens, width = inputs.shape
    columns, n_row = lax.axis_size("col"), lax.axis_size("row")
    offset = columns // 4
    rows1, rows2 = first_params.shape[1], second_params.shape[1]
    up, down = ring_pairs(columns)
    ahead_by = [(i, (i + offset) % columns) for i in range(columns)]
    last = columns // 2
    half = rows1 // 2
    place = place_of(lax.axis_index("col"), columns)
    row = lax.axis_index("row")

    own1 = first_params[0].astype(BF16)
    held = second_params[0].astype(BF16)[None]
    early_params = (second_params[0] - outer_rate * outer_momentum**2 * second_moment[0]).astype(BF16)
    early_moment = second_moment[0].astype(BF16)

    first_pieces = [(own1, 0, 0)]
    second_pieces, flips = [(held, [0])], [0]
    bit = n_row // 2
    forward = backward = own1
    for step in range(1, last + 1):
        if step == last:
            forward, backward = forward[:half], backward[half:]
        if step == EARLY_PARAMS:
            early_params, forward, backward = together(early_params, forward, backward)
        if step == EARLY_MOMENT:
            early_moment, forward, backward = together(early_moment, forward, backward)
        forward = lax.ppermute(forward, "col", up)
        backward = lax.ppermute(backward, "col", down)
        if step == EARLY_PARAMS:
            early_params = lax.ppermute(early_params, "col", ahead_by)
        if step == EARLY_MOMENT:
            early_moment = lax.ppermute(early_moment, "col", ahead_by)
        if step == last:
            break
        first_pieces += [(forward, -step, 0), (backward, step, 0)]
        while bit >= 1 and (step < last - 1 or True):
            other = lax.ppermute(held, "row", swap_pairs(n_row, bit))
            others = [f ^ bit for f in flips]
            second_pieces.append((other, others))
            flips = flips + others
            bit //= 2
            if bit >= 1:
                held = jnp.concatenate([held, other])
            break
    while bit >= 1:
        other = lax.ppermute(held, "row", swap_pairs(n_row, bit))
        others = [f ^ bit for f in flips]
        second_pieces.append((other, others))
        flips = flips + others
        bit //= 2
        if bit >= 1:
            held = jnp.concatenate([held, other])
    if tiled(rows1):
        antipode = jnp.concatenate([forward, backward])
        first_pieces.append((antipode, last, 0))
        first_plan = [p[1] for p in first_pieces]
        first_blocks = [p[0] for p in first_pieces]
    else:
        first_pieces += [(forward, last, 0), (backward, last, half)]
        placed = [(b, member_at(place + back, columns), at) for b, back, at in first_pieces]
        first_blocks, first_plan = [rows_from(placed, rows1, columns)], [None]
    if tiled(rows2):
        second_plan = [p[1] for p in second_pieces]
        second_blocks = [p[0] for p in second_pieces]
    else:
        placed = [(b[k], row ^ f, 0) for b, fs in second_pieces for k, f in enumerate(fs)]
        second_blocks, second_plan = [rows_from(placed, rows2, n_row)], [None]

    def fwd(*refs):
        forward_kernel(first_plan, second_plan, columns, n_row, *refs)

    part = shape_of((n_row // 2, rows2, width))
    away, kept, error, slope, second_full = call(
        fwd,
        [part, part, shape_of((tokens, width)), shape_of((tokens, width), F32), shape_of((width, width))],
        [pltpu.VMEM((width, width), BF16), pltpu.VMEM((tokens, width), BF16), pltpu.VMEM((width, width), BF16)],
        *first_blocks,
        *second_blocks,
        inputs,
        wanted,
        flops=6 * tokens * width * width,
    )
    if not tiled(rows2):
        pairs = jnp.concatenate([away, kept]).reshape(n_row // 2, 2, rows2, width)
        away = lax.dynamic_index_in_dim(pairs, 1 - row % 2, 1, keepdims=False)
        kept = lax.dynamic_index_in_dim(pairs, row % 2, 1, keepdims=False)
    came = lax.ppermute(away, "row", swap_pairs(n_row, 1))

    def bwd(*refs):
        backward_kernel(columns, *refs)

    block, piece = shape_of((rows1, width)), shape_of((half, width))
    outs = [piece, piece] + [block] * (columns - 1) if tiled(rows1) else [shape_of((width, width))]
    blocks = call(
        bwd,
        outs,
        [pltpu.VMEM((width, width), F32)],
        inputs,
        second_full,
        error,
        slope,
        flops=4 * tokens * width * width,
    )
    if not tiled(rows1):
        def cut(away, first=0, count=rows1):
            start = member_at(place + away, columns) * rows1 + first
            return lax.dynamic_slice_in_dim(blocks_full, start, count, 0)

        blocks_full = blocks[0]
        blocks = [cut(last, 0, half), cut(last, half, half), cut(0)]
        for k in range(1, last):
            blocks += [cut(k), cut(-k)]

    forward = lax.ppermute(blocks[0], "col", up)
    backward = lax.ppermute(blocks[1], "col", down)
    bit = 2
    grad2 = None
    for left in range(last - 1, 0, -1):
        if bit < n_row:
            if tiled(rows2):
                n = kept.shape[0] // 2
                away, kept = call(
                    lambda *refs, bit=bit: halve_kernel(bit, *refs),
                    [shape_of((n, rows2, width)), shape_of((n, rows2, width), F32)],
                    [],
                    kept,
                    came,
                )
            else:
                total = (kept.astype(F32) + came.astype(F32)).reshape(-1, 2, rows2, width)
                mine = (row // bit) % 2
                away = lax.dynamic_index_in_dim(total, 1 - mine, 1, keepdims=False).astype(BF16)
                kept = lax.dynamic_index_in_dim(total, mine, 1, keepdims=False)
            forward, backward, away = together(forward, backward, away)
            came = lax.ppermute(away, "row", swap_pairs(n_row, bit))
            bit *= 2
        elif grad2 is None:
            grad2 = ((kept[0].astype(F32) + came[0].astype(F32)) / n_row).astype(BF16)
            forward, backward, grad2 = together(forward, backward, grad2)
            grad2 = lax.ppermute(grad2, "col", ahead_by)
        forward, backward = add_both(blocks[2 * left + 1], forward, blocks[2 * left + 2], backward)
        forward = lax.ppermute(forward, "col", up)
        backward = lax.ppermute(backward, "col", down)
    if grad2 is None:
        grad2 = ((kept[0].astype(F32) + came[0].astype(F32)) / n_row).astype(BF16)
        grad2 = lax.ppermute(grad2, "col", ahead_by)

    if tiled(rows1):
        out = shape_of((rows1, width), F32)
        first_new = call(
            lambda *refs: first_kernel(columns, *refs),
            [out, out],
            [],
            blocks[2],
            forward,
            backward,
            first_params[0],
            first_moment[0],
        )
    else:
        total = blocks[2].astype(F32) + forward.astype(F32) + backward.astype(F32)
        grad = total / columns
        moment_new = outer_momentum * first_moment[0] + grad
        first_new = (first_params[0] - outer_rate * (grad + outer_momentum * moment_new), moment_new)
    grad2 = grad2.astype(F32)
    second_moment_new = outer_momentum * early_moment.astype(F32) + grad2
    second_params_new = early_params.astype(F32) - outer_rate * (1 + outer_momentum) * grad2
    return (first_new[0][None], first_new[1][None], second_params_new[None], second_moment_new[None])


EARLY_PARAMS = 4
EARLY_MOMENT = 3


def solution(mesh):
    return jax.shard_map(
        per_device,
        mesh=mesh,
        in_specs=(
            P("row", "col", None, None),
            P("row", "col", None, None),
            P("row", "col", None),
            P("row", "col", None),
            P("col", "row", None),
            P("col", "row", None),
        ),
        out_specs=(
            P("row", "col", None),
            P("row", "col", None),
            P("col", "row", None),
            P("col", "row", None),
        ),
        check_vma=False,
    )
```

time: 198 us -> 103 us (0.52)
  waiting for transfers between devices: 152 us -> 65.1 us
  starting transfers between devices: 1.66 us -> 24.8 us
  matrix products: 14.6 us -> 0 us
  between operations: 13.9 us -> 0.79 us
  Pallas kernels: 0 us -> 8.31 us
  local copies, waits for them, and re-layouts: 7.96 us -> 0.04 us
  other arithmetic: 7.29 us -> 3.85 us
    unnamed x5 -> x0, waiting for transfers between devices: 68 us -> none
    ppermute x1 -> x23, waiting for transfers between devices: 0.01 us -> 65.1 us  [the longest x7 35 us: per_device(): forward = lax.ppermute(forward, 'col', up)]
    all_gather x2 -> x0, waiting for transfers between devices: 63.4 us -> none  [the longest x1 47 us: per_device(): lax.all_gather(first_params[0].astype(jnp.bfloat16), 'col', axis=0, tiled...]
    ppermute x1 -> x23, starting transfers between devices: 1.49 us -> 24.8 us  [the longest x7 8.63 us: per_device(): backward = lax.ppermute(backward, 'col', down)]
    reduce_scatter x1 -> x0, waiting for transfers between devices: 21 us -> none  [per_device(): lax.psum_scatter(lax.dot_general(picked, error, (((0,), (0,)), ((), ())),...]
    dot_general x4 -> x0, matrix products: 14.6 us -> none  [the longest x1 4.88 us: per_device(): lax.dot_general(picked, grad_pre, (((0,), (0,)), ((), ())), preferred_ele...]
    pallas_call x0 -> x7, Pallas kernels: none -> 8.31 us  [call(): pl.pallas_call(kernel, out_shape=tuple(outs), in_specs=[WHOLE] * len(oper...]
    unnamed x22 -> x8, local copies, waits for them, and re-layouts: 6.71 us -> 0.02 us
  transfers between devices with their start and end apart: 5 -> 23, of which waited for: 4 -> 16; matrix products, arithmetic and copies ran while one was open for 9% -> 2% of each run, Pallas kernels for 0% -> 3%
where the time goes in v2:
time: 103 us
  waiting for transfers between devices  65.1 us (63%)
  starting transfers between devices  24.8 us (24%)
  Pallas kernels  8.31 us (8%)
  other arithmetic  3.85 us (4%)
    ppermute x7, waiting for transfers between devices, per_device(): forward = lax.ppermute(forward, 'col', up)  35 us
    ppermute x7, waiting for transfers between devices, per_device(): backward = lax.ppermute(backward, 'col', down)  14.7 us
    ppermute x7, starting transfers between devices, per_device(): backward = lax.ppermute(backward, 'col', down)  8.63 us
    pallas_call x7, Pallas kernels, call(): pl.pallas_call(kernel, out_shape=tuple(outs), in_specs=[WHOLE] * len(oper...  8.31 us
    ppermute x2, waiting for transfers between devices, per_device(): other = lax.ppermute(held, 'row', swap_pairs(n_row, bit))  7.18 us
    ppermute x7, starting transfers between devices, per_device(): forward = lax.ppermute(forward, 'col', up)  5.86 us
    ppermute x1, waiting for transfers between devices, per_device(): came = lax.ppermute(away, 'row', swap_pairs(n_row, bit))  3.93 us
    ppermute x2, starting transfers between devices, per_device(): other = lax.ppermute(held, 'row', swap_pairs(n_row, bit))  3.1 us
  transfers between devices with their start and end apart: 23, of which 16 were waited for; matrix products, arithmetic and copies ran while one was open for 2% of the time, Pallas kernels for 3%

profile of v2, /device:TPU:0, one launch (start us, length us, event | category | flops | bytes accessed | tf_op | source)
XLA Modules:
  0.0 102.8 jit_solution(16320390914089168108)
XLA Ops:
  0.6 0.0 copy-start
  0.6 2.3 %fusion.5 = (bf16[1,224,896]{2,1,0:T(8,128)(2,1)S(1)}, bf16[224,896]{1,0:T(8,128)(2,1)S(1)}, bf16[224,896]{1,0:T(8,128)(2,1)S(1)}) fusion(f32[1,224,896]{2,1,0:T(8,128)} %param.10, f32[1,224,896]{2,1,0:T(8,128)} %param.11), kind=kLoop, calls=%fused_computation.13 | loop fusion | flops 1003520 | bytes 2809856 | tf_op jit(solution)/shard_map/convert_element_type | solution.py:207
  2.9 0.0 copy-start.2
  2.9 0.0 copy-start.3
  2.9 3.0 %collective-permute-start.8 = (bf16[1,224,896]{2,1,0:T(8,128)(2,1)S(1)}, bf16[1,224,896]{2,1,0:T(8,128)(2,1)S(1)}, u32[]{:S(2)}, u32[]{:S(2)}) collective-permute-start(bf16[1,224,896]{2,1,0:T(8,128)(2,1)S(1)} %get-tuple-element.76.refs_8_), channel_id=1, source_target_pairs={{0,16},{8,24},{16,0},{24,8},{1,17},{9,25},{17,1},{25,9},{2,18},{10... | collective-permute-start | bytes 1204232 | tf_op jit(solution)/shard_map/ppermute | solution.py:232
  6.0 0.0 copy-done
  6.0 1.6 %collective-permute-start.1 = (bf16[112,896]{1,0:T(8,128)(2,1)S(1)}, bf16[112,896]{1,0:T(8,128)(2,1)S(1)}, u32[]{:S(2)}, u32[]{:S(2)}) collective-permute-start(bf16[112,896]{1,0:T(8,128)(2,1)S(1)} %bitcast_convert_fusion.refs_0_), channel_id=1, source_target_pairs={{2,0},{4,2},{6,4},{7,6},{5,7},{3,5},{1,3},{0,1},{10,8},{12,10},{14... | collective-permute-start | bytes 602120 | tf_op jit(solution)/shard_map/ppermute | solution.py:223
  7.6 0.5 collective-permute-start
  8.1 7.2 %collective-permute-done.8.refs_9_ = bf16[1,224,896]{2,1,0:T(8,128)(2,1)S(1)} collective-permute-done((bf16[1,224,896]{2,1,0:T(8,128)(2,1)S(1)}, bf16[1,224,896]{2,1,0:T(8,128)(2,1)S(1)}, u32[]{:S(2)}, u32[]{:S(2)}) %collective-permute-start.8) | collective-permute-done | bytes 401440 | tf_op jit(solution)/shard_map/ppermute | solution.py:232
  15.3 0.1 pad_maximum_fusion
  15.3 0.1 collective-permute-start.9
  15.4 0.0 collective-permute-done.1.refs_2_
  15.4 1.8 %collective-permute-start.3 = (bf16[112,896]{1,0:T(8,128)(2,1)S(1)}, bf16[112,896]{1,0:T(8,128)(2,1)S(1)}, u32[]{:S(2)}, u32[]{:S(2)}) collective-permute-start(bf16[112,896]{1,0:T(8,128)(2,1)S(1)} %collective-permute-done.1.refs_2_), channel_id=1, source_target_pairs={{2,0},{4,2},{6,4},{7,6},{5,7},{3,5},{1,3},{0,1},{10,8},{12,10},{14... | collective-permute-start | bytes 602120 | tf_op jit(solution)/shard_map/ppermute | solution.py:223
  17.3 0.0 collective-permute-done.refs_1_
  17.3 0.3 collective-permute-start.2
  17.5 5.4 %collective-permute-done.3.refs_4_ = bf16[112,896]{1,0:T(8,128)(2,1)S(1)} collective-permute-done((bf16[112,896]{1,0:T(8,128)(2,1)S(1)}, bf16[112,896]{1,0:T(8,128)(2,1)S(1)}, u32[]{:S(2)}, u32[]{:S(2)}) %collective-permute-start.3) | collective-permute-done | bytes 200736 | tf_op jit(solution)/shard_map/ppermute | solution.py:223
  22.9 1.4 %collective-permute-done.2.refs_3_ = bf16[112,896]{1,0:T(8,128)(2,1)S(1)} collective-permute-done((bf16[112,896]{1,0:T(8,128)(2,1)S(1)}, bf16[112,896]{1,0:T(8,128)(2,1)S(1)}, u32[]{:S(2)}, u32[]{:S(2)}) %collective-permute-start.2) | collective-permute-done | bytes 200736 | tf_op jit(solution)/shard_map/ppermute | solution.py:222
  24.3 0.4 collective-permute-start.4
  24.7 1.6 %collective-permute-start.5 = (bf16[112,896]{1,0:T(8,128)(2,1)S(1)}, bf16[112,896]{1,0:T(8,128)(2,1)S(1)}, u32[]{:S(2)}, u32[]{:S(2)}) collective-permute-start(bf16[112,896]{1,0:T(8,128)(2,1)S(1)} %collective-permute-done.3.refs_4_), channel_id=1, source_target_pairs={{2,0},{4,2},{6,4},{7,6},{5,7},{3,5},{1,3},{0,1},{10,8},{12,10},{14... | collective-permute-start | bytes 602120 | tf_op jit(solution)/shard_map/ppermute | solution.py:223
  26.3 4.2 %collective-permute-done.4.refs_5_ = bf16[112,896]{1,0:T(8,128)(2,1)S(1)} collective-permute-done((bf16[112,896]{1,0:T(8,128)(2,1)S(1)}, bf16[112,896]{1,0:T(8,128)(2,1)S(1)}, u32[]{:S(2)}, u32[]{:S(2)}) %collective-permute-start.4) | collective-permute-done | bytes 200736 | tf_op jit(solution)/shard_map/ppermute | solution.py:222
  30.5 0.3 collective-permute-done.5.refs_6_
  30.9 1.6 %collective-permute-start.6 = (bf16[56,896]{1,0:T(8,128)(2,1)S(1)}, bf16[56,896]{1,0:T(8,128)(2,1)S(1)}, u32[]{:S(2)}, u32[]{:S(2)}) collective-permute-start(bf16[56,896]{1,0:T(8,128)(2,1)S(1)} %slice.8), channel_id=1, source_target_pairs={{0,2},{2,4},{4,6},{6,7},{7,5},{5,3},{3,1},{1,0},{8,10},{10,12},{12... | collective-permute-start | bytes 301064 | tf_op jit(solution)/shard_map/ppermute | solution.py:222
  32.5 0.5 collective-permute-start.7
  32.9 2.6 %collective-permute-done.6 = bf16[56,896]{1,0:T(8,128)(2,1)S(1)} collective-permute-done((bf16[56,896]{1,0:T(8,128)(2,1)S(1)}, bf16[56,896]{1,0:T(8,128)(2,1)S(1)}, u32[]{:S(2)}, u32[]{:S(2)}) %collective-permute-start.6) | collective-permute-done | bytes 100384 | tf_op jit(solution)/shard_map/ppermute | solution.py:222
  35.6 1.6 %collective-permute-done.7 = bf16[56,896]{1,0:T(8,128)(2,1)S(1)} collective-permute-done((bf16[56,896]{1,0:T(8,128)(2,1)S(1)}, bf16[56,896]{1,0:T(8,128)(2,1)S(1)}, u32[]{:S(2)}, u32[]{:S(2)}) %collective-permute-start.7) | collective-permute-done | bytes 100384 | tf_op jit(solution)/shard_map/ppermute | solution.py:223
  37.1 0.0 collective-permute-done.9.refs_10_
  37.2 0.0 copy-done.2
  37.2 0.0 copy-done.3
  37.2 4.4 %shard_map.93 = (bf16[2,224,896]{2,1,0:T(8,128)(2,1)S(1)}, bf16[2,224,896]{2,1,0:T(8,128)(2,1)S(1)}, bf16[512,896]{1,0:T(8,128)(2,1)S(1)}, f32[512,896]{1,0:T(8,128)S(1)}, bf16[896,896]{1,0:T(8,128)(2,1)S(1)}) custom-call(bf16[112,896]{1,0:T(8,128)(2,1)S(1)} %bitcast_convert_fusion.refs_0_, bf16[112,896]{1,0:T(8,128)(2,1)S(1)} %collective-permute-done.refs_1_, ...), custom_call_target="tpu_custom_call" | custom-call | flops 2466250752 | bytes 5046272 | tf_op jit(solution)/shard_map/pallas_call | solution.py:23
  41.6 0.1 collective-permute-start.12
  41.7 2.4 %shard_map.94 = (bf16[56,896]{1,0:T(8,128)(2,1)S(1)}, bf16[56,896]{1,0:T(8,128)(2,1)S(1)}, bf16[112,896]{1,0:T(8,128)(2,1)S(1)}, bf16[112,896]{1,0:T(8,128)(2,1)...) custom-call(bf16[512,896]{1,0:T(8,128)(2,1)S(1)} %bitcast.21, ...), custom_call_target="tpu_custom_call" | custom-call | flops 1644167168 | bytes 5275648 | tf_op jit(solution)/shard_map/pallas_call | solution.py:23
  44.1 1.6 %collective-permute-start.10 = (bf16[56,896]{1,0:T(8,128)(2,1)S(1)}, bf16[56,896]{1,0:T(8,128)(2,1)S(1)}, u32[]{:S(2)}, u32[]{:S(2)}) collective-permute-start(bf16[56,896]{1,0:T(8,128)(2,1)S(1)} %get-tuple-element.51), channel_id=1, source_target_pairs={{0,2},{2,4},{4,6},{6,7},{7,5},{5,3},{3,1},{1,0},{8,10},{10,12},{12... | collective-permute-start | bytes 301064 | tf_op jit(solution)/shard_map/ppermute | solution.py:309
  45.7 0.4 collective-permute-start.11
  46.2 0.0 collective-permute-done.12.refs_1_
  46.2 0.2 shard_map.95
  46.4 3.0 %collective-permute-done.10.forward = bf16[56,896]{1,0:T(8,128)(2,1)S(1)} collective-permute-done((bf16[56,896]{1,0:T(8,128)(2,1)S(1)}, bf16[56,896]{1,0:T(8,128)(2,1)S(1)}, u32[]{:S(2)}, u32[]{:S(2)}) %collective-permute-start.10) | collective-permute-done | bytes 100384 | tf_op jit(solution)/shard_map/ppermute | solution.py:309
  49.4 1.3 %collective-permute-done.11.backward = bf16[56,896]{1,0:T(8,128)(2,1)S(1)} collective-permute-done((bf16[56,896]{1,0:T(8,128)(2,1)S(1)}, bf16[56,896]{1,0:T(8,128)(2,1)S(1)}, u32[]{:S(2)}, u32[]{:S(2)}) %collective-permute-start.11) | collective-permute-done | bytes 100384 | tf_op jit(solution)/shard_map/ppermute | solution.py:310
  50.7 1.5 %collective-permute-start.15 = (bf16[1,224,896]{2,1,0:T(8,128)(2,1)S(1)}, bf16[1,224,896]{2,1,0:T(8,128)(2,1)S(1)}, u32[]{:S(2)}, u32[]{:S(2)}) collective-permute-start(bf16[1,224,896]{2,1,0:T(8,128)(2,1)S(1)} %get-tuple-element.62), channel_id=1, source_target_pairs={{0,16},{8,24},{16,0},{24,8},{1,17},{9,25},{17,1},{25,9},{2,18},{10... | collective-permute-start | bytes 1204232 | tf_op jit(solution)/shard_map/ppermute | solution.py:330
  52.2 1.5 %collective-permute-start.22 = (bf16[224,896]{1,0:T(8,128)(2,1)S(1)}, bf16[224,896]{1,0:T(8,128)(2,1)S(1)}, u32[]{:S(2)}, u32[]{:S(2)}) collective-permute-start(bf16[224,896]{1,0:T(8,128)(2,1)S(1)} %get-tuple-element.75), channel_id=1, source_target_pairs={{0,2},{1,3},{2,4},{3,5},{4,6},{5,7},{6,0},{7,1},{8,10},{9,11},{10,... | collective-permute-start | bytes 1204232 | tf_op jit(solution)/shard_map/ppermute | solution.py:227
  53.7 1.5 %collective-permute-start.20 = (bf16[224,896]{1,0:T(8,128)(2,1)S(1)}, bf16[224,896]{1,0:T(8,128)(2,1)S(1)}, u32[]{:S(2)}, u32[]{:S(2)}) collective-permute-start(bf16[224,896]{1,0:T(8,128)(2,1)S(1)} %get-tuple-element.73), channel_id=1, source_target_pairs={{0,2},{1,3},{2,4},{3,5},{4,6},{5,7},{6,0},{7,1},{8,10},{9,11},{10,... | collective-permute-start | bytes 1204232 | tf_op jit(solution)/shard_map/ppermute | solution.py:225
  55.2 0.1 shard_map.96
  55.2 0.5 collective-permute-start.13
  55.7 1.6 %collective-permute-start.14 = (bf16[112,896]{1,0:T(8,128)(2,1)S(1)}, bf16[112,896]{1,0:T(8,128)(2,1)S(1)}, u32[]{:S(2)}, u32[]{:S(2)}) collective-permute-start(bf16[112,896]{1,0:T(8,128)(2,1)S(1)} %get-tuple-element.60), channel_id=1, source_target_pairs={{2,0},{4,2},{6,4},{7,6},{5,7},{3,5},{1,3},{0,1},{10,8},{12,10},{14... | collective-permute-start | bytes 602120 | tf_op jit(solution)/shard_map/ppermute | solution.py:338
  57.3 3.9 %collective-permute-done.15 = bf16[1,224,896]{2,1,0:T(8,128)(2,1)S(1)} collective-permute-done((bf16[1,224,896]{2,1,0:T(8,128)(2,1)S(1)}, bf16[1,224,896]{2,1,0:T(8,128)(2,1)S(1)}, u32[]{:S(2)}, u32[]{:S(2)}) %collective-permute-start.15) | collective-permute-done | bytes 401440 | tf_op jit(solution)/shard_map/ppermute | solution.py:330
  61.2 0.1 fusion.4
  61.4 13.0 %collective-permute-done.13.forward = bf16[112,896]{1,0:T(8,128)(2,1)S(1)} collective-permute-done((bf16[112,896]{1,0:T(8,128)(2,1)S(1)}, bf16[112,896]{1,0:T(8,128)(2,1)S(1)}, u32[]{:S(2)}, u32[]{:S(2)}) %collective-permute-start.13) | collective-permute-done | bytes 200736 | tf_op jit(solution)/shard_map/ppermute | solution.py:337
  74.4 2.8 %collective-permute-done.14.backward = bf16[112,896]{1,0:T(8,128)(2,1)S(1)} collective-permute-done((bf16[112,896]{1,0:T(8,128)(2,1)S(1)}, bf16[112,896]{1,0:T(8,128)(2,1)S(1)}, u32[]{:S(2)}, u32[]{:S(2)}) %collective-permute-start.14) | collective-permute-done | bytes 200736 | tf_op jit(solution)/shard_map/ppermute | solution.py:338
  77.2 0.6 collective-permute-start.21
  77.7 0.1 shard_map.97
  77.8 0.0 copy-start.1
  77.8 0.7 collective-permute-start.16
  78.5 1.4 %collective-permute-start.17 = (bf16[112,896]{1,0:T(8,128)(2,1)S(1)}, bf16[112,896]{1,0:T(8,128)(2,1)S(1)}, u32[]{:S(2)}, u32[]{:S(2)}) collective-permute-start(bf16[112,896]{1,0:T(8,128)(2,1)S(1)} %get-tuple-element.68), channel_id=1, source_target_pairs={{2,0},{4,2},{6,4},{7,6},{5,7},{3,5},{1,3},{0,1},{10,8},{12,10},{14... | collective-permute-start | bytes 602120 | tf_op jit(solution)/shard_map/ppermute | solution.py:338
  79.9 10.8 %collective-permute-done.16.forward = bf16[112,896]{1,0:T(8,128)(2,1)S(1)} collective-permute-done((bf16[112,896]{1,0:T(8,128)(2,1)S(1)}, bf16[112,896]{1,0:T(8,128)(2,1)S(1)}, u32[]{:S(2)}, u32[]{:S(2)}) %collective-permute-start.16) | collective-permute-done | bytes 200736 | tf_op jit(solution)/shard_map/ppermute | solution.py:337
  90.7 2.4 %collective-permute-done.17.backward = bf16[112,896]{1,0:T(8,128)(2,1)S(1)} collective-permute-done((bf16[112,896]{1,0:T(8,128)(2,1)S(1)}, bf16[112,896]{1,0:T(8,128)(2,1)S(1)}, u32[]{:S(2)}, u32[]{:S(2)}) %collective-permute-start.17) | collective-permute-done | bytes 200736 | tf_op jit(solution)/shard_map/ppermute | solution.py:338
  93.2 0.1 shard_map.98
  93.3 1.9 %collective-permute-start.18 = (bf16[112,896]{1,0:T(8,128)(2,1)S(1)}, bf16[112,896]{1,0:T(8,128)(2,1)S(1)}, u32[]{:S(2)}, u32[]{:S(2)}) collective-permute-start(bf16[112,896]{1,0:T(8,128)(2,1)S(1)} %get-tuple-element.69), channel_id=1, source_target_pairs={{0,2},{2,4},{4,6},{6,7},{7,5},{5,3},{3,1},{1,0},{8,10},{10,12},{12... | collective-permute-start | bytes 602120 | tf_op jit(solution)/shard_map/ppermute | solution.py:337
  95.2 0.2 collective-permute-start.19
  95.4 0.0 collective-permute-done.22
  95.4 0.0 collective-permute-done.20
  95.4 0.0 collective-permute-done.21
  95.4 1.3 %fusion.2 = (f32[1,224,896]{2,1,0:T(8,128)}, f32[1,224,896]{2,1,0:T(8,128)}) fusion(bf16[224,896]{1,0:T(8,128)(2,1)S(1)} %collective-permute-done.21, bf16[224,896]{1,0:T(8,128)(2,1)S(1)} %collective-permute-done.22, bf16[224,896]{1,0:T(8,128)(2,1)S(1)} %collective-permute-done.20), kind=kLoop, calls=%fused_computation.4 | loop fusion | flops 1404928 | bytes 2809856 | tf_op jit(solution)/shard_map/broadcast_in_dim | solution.py:363
  96.7 2.9 %collective-permute-done.18.refs_1_ = bf16[112,896]{1,0:T(8,128)(2,1)S(1)} collective-permute-done((bf16[112,896]{1,0:T(8,128)(2,1)S(1)}, bf16[112,896]{1,0:T(8,128)(2,1)S(1)}, u32[]{:S(2)}, u32[]{:S(2)}) %collective-permute-start.18) | collective-permute-done | bytes 200736 | tf_op jit(solution)/shard_map/ppermute | solution.py:337
  99.6 2.2 %collective-permute-done.19.refs_2_ = bf16[112,896]{1,0:T(8,128)(2,1)S(1)} collective-permute-done((bf16[112,896]{1,0:T(8,128)(2,1)S(1)}, bf16[112,896]{1,0:T(8,128)(2,1)S(1)}, u32[]{:S(2)}, u32[]{:S(2)}) %collective-permute-start.19) | collective-permute-done | bytes 200736 | tf_op jit(solution)/shard_map/ppermute | solution.py:338
  101.8 1.0 shard_map.99
  (5 shorter events, 0.1 us)
Async XLA Ops:
  0.6 5.3 %copy-start = (f32[1,112,896]{2,1,0:T(8,128)S(1)}, f32[1,112,896]{2,1,0:T(8,128)}, u32[]{:S(2)}) copy-start(f32[1,112,896]{2,1,0:T(8,128)} %param.8) | copy-start | bytes 1204228
  2.9 34.2 %copy-start.2 = (bf16[1,1,512,896]{3,2,1,0:T(8,128)(2,1)S(1)}, bf16[1,1,512,896]{3,2,1,0:T(8,128)(2,1)}, u32[]{:S(2)}) copy-start(bf16[1,1,512,896]{3,2,1,0:T(8,128)(2,1)} %param.7) | copy-start | bytes 2752516
  2.9 34.2 %copy-start.3 = (bf16[1,1,512,896]{3,2,1,0:T(8,128)(2,1)S(1)}, bf16[1,1,512,896]{3,2,1,0:T(8,128)(2,1)}, u32[]{:S(2)}) copy-start(bf16[1,1,512,896]{3,2,1,0:T(8,128)(2,1)} %param.6) | copy-start | bytes 2752516
  2.9 12.3 %collective-permute-start.8 = (bf16[1,224,896]{2,1,0:T(8,128)(2,1)S(1)}, bf16[1,224,896]{2,1,0:T(8,128)(2,1)S(1)}, u32[]{:S(2)}, u32[]{:S(2)}) collective-permute-start(bf16[1,224,896]{2,1,0:T(8,128)(2,1)S(1)} %get-tuple-element.76.refs_8_), channel_id=1, source_target_pairs={{0,16},{8,24},{16,0},{24,8},{1,17},{9,25},{17,1},{25,9},{2,18},{10... | collective-permute-start | bytes 1204232 | tf_op jit(solution)/shard_map/ppermute | solution.py:232
  6.0 9.4 %collective-permute-start.1 = (bf16[112,896]{1,0:T(8,128)(2,1)S(1)}, bf16[112,896]{1,0:T(8,128)(2,1)S(1)}, u32[]{:S(2)}, u32[]{:S(2)}) collective-permute-start(bf16[112,896]{1,0:T(8,128)(2,1)S(1)} %bitcast_convert_fusion.refs_0_), channel_id=1, source_target_pairs={{2,0},{4,2},{6,4},{7,6},{5,7},{3,5},{1,3},{0,1},{10,8},{12,10},{14... | collective-permute-start | bytes 602120 | tf_op jit(solution)/shard_map/ppermute | solution.py:223
  7.6 9.7 %collective-permute-start = (bf16[112,896]{1,0:T(8,128)(2,1)S(1)}, bf16[112,896]{1,0:T(8,128)(2,1)S(1)}, u32[]{:S(2)}, u32[]{:S(2)}) collective-permute-start(bf16[112,896]{1,0:T(8,128)(2,1)S(1)} %bitcast_convert_fusion.refs_0_), channel_id=1, source_target_pairs={{0,2},{2,4},{4,6},{6,7},{7,5},{5,3},{3,1},{1,0},{8,10},{10,12},{12... | collective-permute-start | bytes 602120 | tf_op jit(solution)/shard_map/ppermute | solution.py:222
  15.3 21.8 %collective-permute-start.9 = (bf16[2,224,896]{2,1,0:T(8,128)(2,1)S(1)}, bf16[2,224,896]{2,1,0:T(8,128)(2,1)S(1)}, u32[]{:S(2)}, u32[]{:S(2)}) collective-permute-start(bf16[2,224,896]{2,1,0:T(8,128)(2,1)S(1)} %pad_maximum_fusion), channel_id=1, source_target_pairs={{0,8},{8,0},{16,24},{24,16},{1,9},{9,1},{17,25},{25,17},{2,10},{10... | collective-permute-start | bytes 2408456 | tf_op jit(solution)/shard_map/ppermute | solution.py:232
  15.4 7.5 %collective-permute-start.3 = (bf16[112,896]{1,0:T(8,128)(2,1)S(1)}, bf16[112,896]{1,0:T(8,128)(2,1)S(1)}, u32[]{:S(2)}, u32[]{:S(2)}) collective-permute-start(bf16[112,896]{1,0:T(8,128)(2,1)S(1)} %collective-permute-done.1.refs_2_), channel_id=1, source_target_pairs={{2,0},{4,2},{6,4},{7,6},{5,7},{3,5},{1,3},{0,1},{10,8},{12,10},{14... | collective-permute-start | bytes 602120 | tf_op jit(solution)/shard_map/ppermute | solution.py:223
  17.3 7.1 %collective-permute-start.2 = (bf16[112,896]{1,0:T(8,128)(2,1)S(1)}, bf16[112,896]{1,0:T(8,128)(2,1)S(1)}, u32[]{:S(2)}, u32[]{:S(2)}) collective-permute-start(bf16[112,896]{1,0:T(8,128)(2,1)S(1)} %collective-permute-done.refs_1_), channel_id=1, source_target_pairs={{0,2},{2,4},{4,6},{6,7},{7,5},{5,3},{3,1},{1,0},{8,10},{10,12},{12... | collective-permute-start | bytes 602120 | tf_op jit(solution)/shard_map/ppermute | solution.py:222
  24.3 6.2 %collective-permute-start.4 = (bf16[112,896]{1,0:T(8,128)(2,1)S(1)}, bf16[112,896]{1,0:T(8,128)(2,1)S(1)}, u32[]{:S(2)}, u32[]{:S(2)}) collective-permute-start(bf16[112,896]{1,0:T(8,128)(2,1)S(1)} %collective-permute-done.2.refs_3_), channel_id=1, source_target_pairs={{0,2},{2,4},{4,6},{6,7},{7,5},{5,3},{3,1},{1,0},{8,10},{10,12},{12... | collective-permute-start | bytes 602120 | tf_op jit(solution)/shard_map/ppermute | solution.py:222
  24.7 6.1 %collective-permute-start.5 = (bf16[112,896]{1,0:T(8,128)(2,1)S(1)}, bf16[112,896]{1,0:T(8,128)(2,1)S(1)}, u32[]{:S(2)}, u32[]{:S(2)}) collective-permute-start(bf16[112,896]{1,0:T(8,128)(2,1)S(1)} %collective-permute-done.3.refs_4_), channel_id=1, source_target_pairs={{2,0},{4,2},{6,4},{7,6},{5,7},{3,5},{1,3},{0,1},{10,8},{12,10},{14... | collective-permute-start | bytes 602120 | tf_op jit(solution)/shard_map/ppermute | solution.py:223
  30.9 4.7 %collective-permute-start.6 = (bf16[56,896]{1,0:T(8,128)(2,1)S(1)}, bf16[56,896]{1,0:T(8,128)(2,1)S(1)}, u32[]{:S(2)}, u32[]{:S(2)}) collective-permute-start(bf16[56,896]{1,0:T(8,128)(2,1)S(1)} %slice.8), channel_id=1, source_target_pairs={{0,2},{2,4},{4,6},{6,7},{7,5},{5,3},{3,1},{1,0},{8,10},{10,12},{12... | collective-permute-start | bytes 301064 | tf_op jit(solution)/shard_map/ppermute | solution.py:222
  32.5 4.6 %collective-permute-start.7 = (bf16[56,896]{1,0:T(8,128)(2,1)S(1)}, bf16[56,896]{1,0:T(8,128)(2,1)S(1)}, u32[]{:S(2)}, u32[]{:S(2)}) collective-permute-start(bf16[56,896]{1,0:T(8,128)(2,1)S(1)} %slice.9), channel_id=1, source_target_pairs={{2,0},{4,2},{6,4},{7,6},{5,7},{3,5},{1,3},{0,1},{10,8},{12,10},{14... | collective-permute-start | bytes 301064 | tf_op jit(solution)/shard_map/ppermute | solution.py:223
  41.6 4.6 %collective-permute-start.12 = (bf16[2,224,896]{2,1,0:T(8,128)(2,1)S(1)}, bf16[2,224,896]{2,1,0:T(8,128)(2,1)S(1)}, u32[]{:S(2)}, u32[]{:S(2)}) collective-permute-start(bf16[2,224,896]{2,1,0:T(8,128)(2,1)S(1)} %get-tuple-element.54), channel_id=1, source_target_pairs={{0,8},{8,0},{16,24},{24,16},{1,9},{9,1},{17,25},{25,17},{2,10},{10... | collective-permute-start | bytes 2408456 | tf_op jit(solution)/shard_map/ppermute | solution.py:282
  44.1 5.3 %collective-permute-start.10 = (bf16[56,896]{1,0:T(8,128)(2,1)S(1)}, bf16[56,896]{1,0:T(8,128)(2,1)S(1)}, u32[]{:S(2)}, u32[]{:S(2)}) collective-permute-start(bf16[56,896]{1,0:T(8,128)(2,1)S(1)} %get-tuple-element.51), channel_id=1, source_target_pairs={{0,2},{2,4},{4,6},{6,7},{7,5},{5,3},{3,1},{1,0},{8,10},{10,12},{12... | collective-permute-start | bytes 301064 | tf_op jit(solution)/shard_map/ppermute | solution.py:309
  45.7 5.0 %collective-permute-start.11 = (bf16[56,896]{1,0:T(8,128)(2,1)S(1)}, bf16[56,896]{1,0:T(8,128)(2,1)S(1)}, u32[]{:S(2)}, u32[]{:S(2)}) collective-permute-start(bf16[56,896]{1,0:T(8,128)(2,1)S(1)} %get-tuple-element.52), channel_id=1, source_target_pairs={{2,0},{4,2},{6,4},{7,6},{5,7},{3,5},{1,3},{0,1},{10,8},{12,10},{14... | collective-permute-start | bytes 301064 | tf_op jit(solution)/shard_map/ppermute | solution.py:310
  50.7 10.6 %collective-permute-start.15 = (bf16[1,224,896]{2,1,0:T(8,128)(2,1)S(1)}, bf16[1,224,896]{2,1,0:T(8,128)(2,1)S(1)}, u32[]{:S(2)}, u32[]{:S(2)}) collective-permute-start(bf16[1,224,896]{2,1,0:T(8,128)(2,1)S(1)} %get-tuple-element.62), channel_id=1, source_target_pairs={{0,16},{8,24},{16,0},{24,8},{1,17},{9,25},{17,1},{25,9},{2,18},{10... | collective-permute-start | bytes 1204232 | tf_op jit(solution)/shard_map/ppermute | solution.py:330
  52.2 43.2 %collective-permute-start.22 = (bf16[224,896]{1,0:T(8,128)(2,1)S(1)}, bf16[224,896]{1,0:T(8,128)(2,1)S(1)}, u32[]{:S(2)}, u32[]{:S(2)}) collective-permute-start(bf16[224,896]{1,0:T(8,128)(2,1)S(1)} %get-tuple-element.75), channel_id=1, source_target_pairs={{0,2},{1,3},{2,4},{3,5},{4,6},{5,7},{6,0},{7,1},{8,10},{9,11},{10,... | collective-permute-start | bytes 1204232 | tf_op jit(solution)/shard_map/ppermute | solution.py:227
  53.7 41.7 %collective-permute-start.20 = (bf16[224,896]{1,0:T(8,128)(2,1)S(1)}, bf16[224,896]{1,0:T(8,128)(2,1)S(1)}, u32[]{:S(2)}, u32[]{:S(2)}) collective-permute-start(bf16[224,896]{1,0:T(8,128)(2,1)S(1)} %get-tuple-element.73), channel_id=1, source_target_pairs={{0,2},{1,3},{2,4},{3,5},{4,6},{5,7},{6,0},{7,1},{8,10},{9,11},{10,... | collective-permute-start | bytes 1204232 | tf_op jit(solution)/shard_map/ppermute | solution.py:225
  55.2 19.2 %collective-permute-start.13 = (bf16[112,896]{1,0:T(8,128)(2,1)S(1)}, bf16[112,896]{1,0:T(8,128)(2,1)S(1)}, u32[]{:S(2)}, u32[]{:S(2)}) collective-permute-start(bf16[112,896]{1,0:T(8,128)(2,1)S(1)} %get-tuple-element.59), channel_id=1, source_target_pairs={{0,2},{2,4},{4,6},{6,7},{7,5},{5,3},{3,1},{1,0},{8,10},{10,12},{12... | collective-permute-start | bytes 602120 | tf_op jit(solution)/shard_map/ppermute | solution.py:337
  55.7 21.4 %collective-permute-start.14 = (bf16[112,896]{1,0:T(8,128)(2,1)S(1)}, bf16[112,896]{1,0:T(8,128)(2,1)S(1)}, u32[]{:S(2)}, u32[]{:S(2)}) collective-permute-start(bf16[112,896]{1,0:T(8,128)(2,1)S(1)} %get-tuple-element.60), channel_id=1, source_target_pairs={{2,0},{4,2},{6,4},{7,6},{5,7},{3,5},{1,3},{0,1},{10,8},{12,10},{14... | collective-permute-start | bytes 602120 | tf_op jit(solution)/shard_map/ppermute | solution.py:338
  77.2 18.2 %collective-permute-start.21 = (bf16[224,896]{1,0:T(8,128)(2,1)S(1)}, bf16[224,896]{1,0:T(8,128)(2,1)S(1)}, u32[]{:S(2)}, u32[]{:S(2)}) collective-permute-start(bf16[224,896]{1,0:T(8,128)(2,1)S(1)} %fusion.4), channel_id=1, source_target_pairs={{0,2},{1,3},{2,4},{3,5},{4,6},{5,7},{6,0},{7,1},{8,10},{9,11},{10,... | collective-permute-start | bytes 1204232 | tf_op jit(solution)/shard_map/ppermute | solution.py:335
  77.8 24.0 %copy-start.1 = (f32[1,112,896]{2,1,0:T(8,128)S(1)}, f32[1,112,896]{2,1,0:T(8,128)}, u32[]{:S(2)}) copy-start(f32[1,112,896]{2,1,0:T(8,128)} %param.9) | copy-start | bytes 1204228
  77.8 12.9 %collective-permute-start.16 = (bf16[112,896]{1,0:T(8,128)(2,1)S(1)}, bf16[112,896]{1,0:T(8,128)(2,1)S(1)}, u32[]{:S(2)}, u32[]{:S(2)}) collective-permute-start(bf16[112,896]{1,0:T(8,128)(2,1)S(1)} %get-tuple-element.66), channel_id=1, source_target_pairs={{0,2},{2,4},{4,6},{6,7},{7,5},{5,3},{3,1},{1,0},{8,10},{10,12},{12... | collective-permute-start | bytes 602120 | tf_op jit(solution)/shard_map/ppermute | solution.py:337
  78.5 14.7 %collective-permute-start.17 = (bf16[112,896]{1,0:T(8,128)(2,1)S(1)}, bf16[112,896]{1,0:T(8,128)(2,1)S(1)}, u32[]{:S(2)}, u32[]{:S(2)}) collective-permute-start(bf16[112,896]{1,0:T(8,128)(2,1)S(1)} %get-tuple-element.68), channel_id=1, source_target_pairs={{2,0},{4,2},{6,4},{7,6},{5,7},{3,5},{1,3},{0,1},{10,8},{12,10},{14... | collective-permute-start | bytes 602120 | tf_op jit(solution)/shard_map/ppermute | solution.py:338
  93.3 6.3 %collective-permute-start.18 = (bf16[112,896]{1,0:T(8,128)(2,1)S(1)}, bf16[112,896]{1,0:T(8,128)(2,1)S(1)}, u32[]{:S(2)}, u32[]{:S(2)}) collective-permute-start(bf16[112,896]{1,0:T(8,128)(2,1)S(1)} %get-tuple-element.69), channel_id=1, source_target_pairs={{0,2},{2,4},{4,6},{6,7},{7,5},{5,3},{3,1},{1,0},{8,10},{10,12},{12... | collective-permute-start | bytes 602120 | tf_op jit(solution)/shard_map/ppermute | solution.py:337
  95.2 6.6 %collective-permute-start.19 = (bf16[112,896]{1,0:T(8,128)(2,1)S(1)}, bf16[112,896]{1,0:T(8,128)(2,1)S(1)}, u32[]{:S(2)}, u32[]{:S(2)}) collective-permute-start(bf16[112,896]{1,0:T(8,128)(2,1)S(1)} %get-tuple-element.70), channel_id=1, source_target_pairs={{2,0},{4,2},{6,4},{7,6},{5,7},{3,5},{1,3},{0,1},{10,8},{12,10},{14... | collective-permute-start | bytes 602120 | tf_op jit(solution)/shard_map/ppermute | solution.py:338

commit v3 on v2

--- a/solution.py
+++ b/solution.py
@@ -6,6 +6,7 @@
 from jax.experimental import pallas as pl
 from jax.experimental.pallas import tpu as pltpu
 from jax.sharding import PartitionSpec as P
+
 
 outer_momentum = 0.9
 outer_rate = 0.7
@@ -35,10 +36,6 @@
     return rows % 16 == 0
 
 
-def together(*values):
-    return lax.optimization_barrier(values)
-
-
 def place_of(member, length):
     return jnp.where(member % 2 == 0, member // 2, length - 1 - member // 2)
 
@@ -72,6 +69,12 @@
     for block, member, first in pieces:
         full = lax.dynamic_update_slice(full, block, (member * rows + first, 0))
     return full
+
+
+def prepare_kernel(params, moment, params_out, early_params, early_moment):
+    params_out[...] = params[...].astype(BF16)
+    early_params[...] = (params[...] - outer_rate * outer_momentum**2 * moment[...]).astype(BF16)
+    early_moment[...] = moment[...].astype(BF16)
 
 
 def forward_kernel(first_plan, second_plan, columns, n_row, *refs):
@@ -204,47 +207,33 @@
     row = lax.axis_index("row")
 
     own1 = first_params[0].astype(BF16)
-    held = second_params[0].astype(BF16)[None]
-    early_params = (second_params[0] - outer_rate * outer_momentum**2 * second_moment[0]).astype(BF16)
-    early_moment = second_moment[0].astype(BF16)
-
+    shard = shape_of((rows2, width))
+    held, early_params, early_moment = call(
+        prepare_kernel, [shard] * 3, [], second_params[0], second_moment[0]
+    )
+    held = held[None]
     first_pieces = [(own1, 0, 0)]
-    second_pieces, flips = [(held, [0])], [0]
-    bit = n_row // 2
     forward = backward = own1
     for step in range(1, last + 1):
         if step == last:
             forward, backward = forward[:half], backward[half:]
-        if step == EARLY_PARAMS:
-            early_params, forward, backward = together(early_params, forward, backward)
-        if step == EARLY_MOMENT:
-            early_moment, forward, backward = together(early_moment, forward, backward)
         forward = lax.ppermute(forward, "col", up)
         backward = lax.ppermute(backward, "col", down)
-        if step == EARLY_PARAMS:
-            early_params = lax.ppermute(early_params, "col", ahead_by)
-        if step == EARLY_MOMENT:
-            early_moment = lax.ppermute(early_moment, "col", ahead_by)
-        if step == last:
-            break
-        first_pieces += [(forward, -step, 0), (backward, step, 0)]
-        while bit >= 1 and (step < last - 1 or True):
-            other = lax.ppermute(held, "row", swap_pairs(n_row, bit))
-            others = [f ^ bit for f in flips]
-            second_pieces.append((other, others))
-            flips = flips + others
-            bit //= 2
-            if bit >= 1:
-                held = jnp.concatenate([held, other])
-            break
+        forward, backward = lax.optimization_barrier((forward, backward))
+        if step < last:
+            first_pieces += [(forward, -step, 0), (backward, step, 0)]
+    second_pieces, flips = [(held, [0])], [0]
+    bit = n_row // 2
     while bit >= 1:
         other = lax.ppermute(held, "row", swap_pairs(n_row, bit))
         others = [f ^ bit for f in flips]
         second_pieces.append((other, others))
         flips = flips + others
-        bit //= 2
+        bit = bit // 2
         if bit >= 1:
             held = jnp.concatenate([held, other])
+    early_params = lax.ppermute(early_params, "col", ahead_by)
+    early_moment = lax.ppermute(early_moment, "col", ahead_by)
     if tiled(rows1):
         antipode = jnp.concatenate([forward, backward])
         first_pieces.append((antipode, last, 0))
@@ -306,39 +295,32 @@
         for k in range(1, last):
             blocks += [cut(k), cut(-k)]
 
+    bit = 2
+    while bit < n_row:
+        if tiled(rows2):
+            n = kept.shape[0] // 2
+            away, kept = call(
+                lambda *refs, bit=bit: halve_kernel(bit, *refs),
+                [shape_of((n, rows2, width)), shape_of((n, rows2, width), F32)],
+                [],
+                kept,
+                came,
+            )
+        else:
+            total = (kept.astype(F32) + came.astype(F32)).reshape(-1, 2, rows2, width)
+            mine = (row // bit) % 2
+            away = lax.dynamic_index_in_dim(total, 1 - mine, 1, keepdims=False).astype(BF16)
+            kept = lax.dynamic_index_in_dim(total, mine, 1, keepdims=False)
+        came = lax.ppermute(away, "row", swap_pairs(n_row, bit))
+        bit = bit * 2
+    grad2 = ((kept[0].astype(F32) + came[0].astype(F32)) / n_row).astype(BF16)
+    grad2 = lax.ppermute(grad2, "col", ahead_by)
     forward = lax.ppermute(blocks[0], "col", up)
     backward = lax.ppermute(blocks[1], "col", down)
-    bit = 2
-    grad2 = None
     for left in range(last - 1, 0, -1):
-        if bit < n_row:
-            if tiled(rows2):
-                n = kept.shape[0] // 2
-                away, kept = call(
-                    lambda *refs, bit=bit: halve_kernel(bit, *refs),
-                    [shape_of((n, rows2, width)), shape_of((n, rows2, width), F32)],
-                    [],
-                    kept,
-                    came,
-                )
-            else:
-                total = (kept.astype(F32) + came.astype(F32)).reshape(-1, 2, rows2, width)
-                mine = (row // bit) % 2
-                away = lax.dynamic_index_in_dim(total, 1 - mine, 1, keepdims=False).astype(BF16)
-                kept = lax.dynamic_index_in_dim(total, mine, 1, keepdims=False)
-            forward, backward, away = together(forward, backward, away)
-            came = lax.ppermute(away, "row", swap_pairs(n_row, bit))
-            bit *= 2
-        elif grad2 is None:
-            grad2 = ((kept[0].astype(F32) + came[0].astype(F32)) / n_row).astype(BF16)
-            forward, backward, grad2 = together(forward, backward, grad2)
-            grad2 = lax.ppermute(grad2, "col", ahead_by)
         forward, backward = add_both(blocks[2 * left + 1], forward, blocks[2 * left + 2], backward)
         forward = lax.ppermute(forward, "col", up)
         backward = lax.ppermute(backward, "col", down)
-    if grad2 is None:
-        grad2 = ((kept[0].astype(F32) + came[0].astype(F32)) / n_row).astype(BF16)
-        grad2 = lax.ppermute(grad2, "col", ahead_by)
 
     if tiled(rows1):
         out = shape_of((rows1, width), F32)
@@ -363,14 +345,9 @@
     return (first_new[0][None], first_new[1][None], second_params_new[None], second_moment_new[None])
 
 
-EARLY_PARAMS = 4
-EARLY_MOMENT = 3
-
-
 def solution(mesh):
     return jax.shard_map(
-        per_device,
-        mesh=mesh,
+        per_device,        mesh=mesh,
         in_specs=(
             P("row", "col", None, None),
             P("row", "col", None, None),

time: 103 us -> 102 us (level)
  waiting for transfers between devices: 65.1 us -> 49.4 us
  starting transfers between devices: 24.8 us -> 39.4 us
  local copies, waits for them, and re-layouts: 0.04 us -> 2.36 us
  other arithmetic: 3.85 us -> 1.58 us
    ppermute x7, starting transfers between devices: 5.86 us -> 22.3 us  [per_device(): forward = lax.ppermute(forward, 'col', up)]
    ppermute x7, waiting for transfers between devices: 35 us -> 18.6 us  [per_device(): forward = lax.ppermute(forward, 'col', up)]
    ppermute x1, waiting for transfers between devices: 3.93 us -> 0.01 us  [per_device(): came = lax.ppermute(away, 'row', swap_pairs(n_row, bit))]
    ppermute x7, starting transfers between devices: 8.63 us -> 5.19 us  [per_device(): backward = lax.ppermute(backward, 'col', down)]
    ppermute x7, waiting for transfers between devices: 14.7 us -> 17.1 us  [per_device(): backward = lax.ppermute(backward, 'col', down)]
    unnamed x8 -> x12, local copies, waits for them, and re-layouts: 0.02 us -> 2.34 us
    ppermute x1, waiting for transfers between devices: 0.01 us -> 2.3 us  [per_device(): came = lax.ppermute(away, 'row', swap_pairs(n_row, 1))]
    convert_element_type x1 -> x0, other arithmetic: 2.27 us -> none  [per_device(): held = second_params[0].astype(BF16)[None]]
  transfers between devices with their start and end apart: 23 -> 23, of which waited for: 16 -> 16; matrix products, arithmetic and copies ran while one was open for 2% -> 0% of each run, Pallas kernels for 3% -> 4%
where the time goes in v3:
time: 102 us
  waiting for transfers between devices  49.4 us (48%)
  starting transfers between devices  39.4 us (39%)
  Pallas kernels  8.43 us (8%)
  local copies, waits for them, and re-layouts  2.36 us (2%)
  other arithmetic  1.58 us (2%)
    ppermute x7, starting transfers between devices, per_device(): forward = lax.ppermute(forward, 'col', up)  22.3 us
    ppermute x7, waiting for transfers between devices, per_device(): forward = lax.ppermute(forward, 'col', up)  18.6 us
    ppermute x7, waiting for transfers between devices, per_device(): backward = lax.ppermute(backward, 'col', down)  17.1 us
    pallas_call x8, Pallas kernels, call(): pl.pallas_call(kernel, out_shape=tuple(outs), in_specs=[WHOLE] * len(oper...  8.43 us
    ppermute x2, waiting for transfers between devices, per_device(): other = lax.ppermute(held, 'row', swap_pairs(n_row, bit))  7.18 us
    ppermute x7, starting transfers between devices, per_device(): backward = lax.ppermute(backward, 'col', down)  5.19 us
    ppermute x2, starting transfers between devices, per_device(): other = lax.ppermute(held, 'row', swap_pairs(n_row, bit))  3.1 us
    ppermute x1, waiting for transfers between devices, per_device(): forward = lax.ppermute(blocks[0], 'col', up)  2.61 us
  transfers between devices with their start and end apart: 23, of which 16 were waited for; matrix products, arithmetic and copies ran while one was open for 0% of the time, Pallas kernels for 4%

profile of v3, /device:TPU:0, one launch (start us, length us, event | category | flops | bytes accessed | tf_op | source)
XLA Modules:
  0.0 102.0 jit_solution(8554262072507812435)
XLA Ops:
  0.6 0.0 copy-start
  0.6 0.0 copy-start.1
  0.7 1.2 %copy-done.1 = f32[1,224,896]{2,1,0:T(8,128)S(1)} copy-done((f32[1,224,896]{2,1,0:T(8,128)S(1)}, f32[1,224,896]{2,1,0:T(8,128)}, u32[]{:S(2)}) %copy-start.1) | copy-done | bytes 802840
  1.8 1.1 %copy-done.2 = f32[1,224,896]{2,1,0:T(8,128)S(1)} copy-done((f32[1,224,896]{2,1,0:T(8,128)S(1)}, f32[1,224,896]{2,1,0:T(8,128)}, u32[]{:S(2)}) %copy-start.2) | copy-done | bytes 802840
  3.0 0.2 shard_map.93
  3.1 0.0 copy-start.4
  3.1 0.0 copy-start.5
  3.2 3.0 %collective-permute-start.8 = (bf16[1,224,896]{2,1,0:T(8,128)(2,1)S(1)}, bf16[1,224,896]{2,1,0:T(8,128)(2,1)S(1)}, u32[]{:S(2)}, u32[]{:S(2)}) collective-permute-start(bf16[1,224,896]{2,1,0:T(8,128)(2,1)S(1)} %bitcast.20), channel_id=1, source_target_pairs={{0,16},{8,24},{16,0},{24,8},{1,17},{9,25},{17,1},{25,9},{2,18},{10... | collective-permute-start | bytes 1204232 | tf_op jit(solution)/shard_map/ppermute | solution.py:228
  6.2 0.0 copy-done
  6.2 1.6 %collective-permute-start.1 = (bf16[112,896]{1,0:T(8,128)(2,1)S(1)}, bf16[112,896]{1,0:T(8,128)(2,1)S(1)}, u32[]{:S(2)}, u32[]{:S(2)}) collective-permute-start(bf16[112,896]{1,0:T(8,128)(2,1)S(1)} %bitcast_convert_fusion.refs_0_), channel_id=1, source_target_pairs={{2,0},{4,2},{6,4},{7,6},{5,7},{3,5},{1,3},{0,1},{10,8},{12,10},{14... | collective-permute-start | bytes 602120 | tf_op jit(solution)/shard_map/ppermute | solution.py:221
  7.8 0.5 collective-permute-start
  8.3 7.2 %collective-permute-done.8.refs_9_ = bf16[1,224,896]{2,1,0:T(8,128)(2,1)S(1)} collective-permute-done((bf16[1,224,896]{2,1,0:T(8,128)(2,1)S(1)}, bf16[1,224,896]{2,1,0:T(8,128)(2,1)S(1)}, u32[]{:S(2)}, u32[]{:S(2)}) %collective-permute-start.8) | collective-permute-done | bytes 401440 | tf_op jit(solution)/shard_map/ppermute | solution.py:228
  15.5 0.1 pad_maximum_fusion
  15.6 0.1 collective-permute-start.9
  15.6 0.0 collective-permute-done.1.refs_2_
  15.7 0.0 collective-permute-done.refs_1_
  15.7 1.9 %collective-permute-start.2 = (bf16[112,896]{1,0:T(8,128)(2,1)S(1)}, bf16[112,896]{1,0:T(8,128)(2,1)S(1)}, u32[]{:S(2)}, u32[]{:S(2)}) collective-permute-start(bf16[112,896]{1,0:T(8,128)(2,1)S(1)} %collective-permute-done.refs_1_), channel_id=1, source_target_pairs={{0,2},{2,4},{4,6},{6,7},{7,5},{5,3},{3,1},{1,0},{8,10},{10,12},{12... | collective-permute-start | bytes 602120 | tf_op jit(solution)/shard_map/ppermute | solution.py:220
  17.5 0.2 collective-permute-start.3
  17.7 5.3 %collective-permute-done.2.refs_3_ = bf16[112,896]{1,0:T(8,128)(2,1)S(1)} collective-permute-done((bf16[112,896]{1,0:T(8,128)(2,1)S(1)}, bf16[112,896]{1,0:T(8,128)(2,1)S(1)}, u32[]{:S(2)}, u32[]{:S(2)}) %collective-permute-start.2) | collective-permute-done | bytes 200736 | tf_op jit(solution)/shard_map/ppermute | solution.py:220
  23.1 1.5 %collective-permute-done.3.refs_4_ = bf16[112,896]{1,0:T(8,128)(2,1)S(1)} collective-permute-done((bf16[112,896]{1,0:T(8,128)(2,1)S(1)}, bf16[112,896]{1,0:T(8,128)(2,1)S(1)}, u32[]{:S(2)}, u32[]{:S(2)}) %collective-permute-start.3) | collective-permute-done | bytes 200736 | tf_op jit(solution)/shard_map/ppermute | solution.py:221
  24.6 1.6 %collective-permute-start.4 = (bf16[112,896]{1,0:T(8,128)(2,1)S(1)}, bf16[112,896]{1,0:T(8,128)(2,1)S(1)}, u32[]{:S(2)}, u32[]{:S(2)}) collective-permute-start(bf16[112,896]{1,0:T(8,128)(2,1)S(1)} %collective-permute-done.2.refs_3_), channel_id=1, source_target_pairs={{0,2},{2,4},{4,6},{6,7},{7,5},{5,3},{3,1},{1,0},{8,10},{10,12},{12... | collective-permute-start | bytes 602120 | tf_op jit(solution)/shard_map/ppermute | solution.py:220
  26.2 0.4 collective-permute-start.5
  26.6 4.2 %collective-permute-done.4.refs_5_ = bf16[112,896]{1,0:T(8,128)(2,1)S(1)} collective-permute-done((bf16[112,896]{1,0:T(8,128)(2,1)S(1)}, bf16[112,896]{1,0:T(8,128)(2,1)S(1)}, u32[]{:S(2)}, u32[]{:S(2)}) %collective-permute-start.4) | collective-permute-done | bytes 200736 | tf_op jit(solution)/shard_map/ppermute | solution.py:220
  30.8 1.3 %collective-permute-done.5.refs_6_ = bf16[112,896]{1,0:T(8,128)(2,1)S(1)} collective-permute-done((bf16[112,896]{1,0:T(8,128)(2,1)S(1)}, bf16[112,896]{1,0:T(8,128)(2,1)S(1)}, u32[]{:S(2)}, u32[]{:S(2)}) %collective-permute-start.5) | collective-permute-done | bytes 200736 | tf_op jit(solution)/shard_map/ppermute | solution.py:221
  32.1 0.5 collective-permute-start.7
  32.6 1.6 %collective-permute-start.6 = (bf16[56,896]{1,0:T(8,128)(2,1)S(1)}, bf16[56,896]{1,0:T(8,128)(2,1)S(1)}, u32[]{:S(2)}, u32[]{:S(2)}) collective-permute-start(bf16[56,896]{1,0:T(8,128)(2,1)S(1)} %slice.6), channel_id=1, source_target_pairs={{0,2},{2,4},{4,6},{6,7},{7,5},{5,3},{3,1},{1,0},{8,10},{10,12},{12... | collective-permute-start | bytes 301064 | tf_op jit(solution)/shard_map/ppermute | solution.py:220
  34.2 2.6 %collective-permute-done.7 = bf16[56,896]{1,0:T(8,128)(2,1)S(1)} collective-permute-done((bf16[56,896]{1,0:T(8,128)(2,1)S(1)}, bf16[56,896]{1,0:T(8,128)(2,1)S(1)}, u32[]{:S(2)}, u32[]{:S(2)}) %collective-permute-start.7) | collective-permute-done | bytes 100384 | tf_op jit(solution)/shard_map/ppermute | solution.py:221
  36.8 0.4 collective-permute-done.6
  37.3 0.0 collective-permute-done.9.refs_10_
  37.3 4.4 %shard_map.94 = (bf16[2,224,896]{2,1,0:T(8,128)(2,1)S(1)}, bf16[2,224,896]{2,1,0:T(8,128)(2,1)S(1)}, bf16[512,896]{1,0:T(8,128)(2,1)S(1)}, f32[512,896]{1,0:T(8,128)S(1)}, bf16[896,896]{1,0:T(8,128)(2,1)S(1)}) custom-call(bf16[112,896]{1,0:T(8,128)(2,1)S(1)} %bitcast_convert_fusion.refs_0_, bf16[112,896]{1,0:T(8,128)(2,1)S(1)} %collective-permute-done.refs_1_, ...), custom_call_target="tpu_custom_call" | custom-call | flops 2466250752 | bytes 5046272 | tf_op jit(solution)/shard_map/pallas_call | solution.py:24
  41.7 0.1 collective-permute-start.19
  41.8 2.3 %collective-permute-done.19.refs_1_ = bf16[2,224,896]{2,1,0:T(8,128)(2,1)S(1)} collective-permute-done((bf16[2,224,896]{2,1,0:T(8,128)(2,1)S(1)}, bf16[2,224,896]{2,1,0:T(8,128)(2,1)S(1)}, u32[]{:S(2)}, u32[]{:S(2)}) %collective-permute-start.19) | collective-permute-done | bytes 802848 | tf_op jit(solution)/shard_map/ppermute | solution.py:271
  44.1 0.2 shard_map.100
  44.3 1.6 %collective-permute-start.20 = (bf16[1,224,896]{2,1,0:T(8,128)(2,1)S(1)}, bf16[1,224,896]{2,1,0:T(8,128)(2,1)S(1)}, u32[]{:S(2)}, u32[]{:S(2)}) collective-permute-start(bf16[1,224,896]{2,1,0:T(8,128)(2,1)S(1)} %get-tuple-element.72), channel_id=1, source_target_pairs={{0,16},{8,24},{16,0},{24,8},{1,17},{9,25},{17,1},{25,9},{2,18},{10... | collective-permute-start | bytes 1204232 | tf_op jit(solution)/shard_map/ppermute | solution.py:314
  45.8 2.4 %shard_map.95 = (bf16[56,896]{1,0:T(8,128)(2,1)S(1)}, bf16[56,896]{1,0:T(8,128)(2,1)S(1)}, bf16[112,896]{1,0:T(8,128)(2,1)S(1)}, bf16[112,896]{1,0:T(8,128)(2,1)...) custom-call(bf16[512,896]{1,0:T(8,128)(2,1)S(1)} %bitcast.25, ...), custom_call_target="tpu_custom_call" | custom-call | flops 1644167168 | bytes 5275648 | tf_op jit(solution)/shard_map/pallas_call | solution.py:24
  48.2 1.6 %collective-permute-start.10 = (bf16[56,896]{1,0:T(8,128)(2,1)S(1)}, bf16[56,896]{1,0:T(8,128)(2,1)S(1)}, u32[]{:S(2)}, u32[]{:S(2)}) collective-permute-start(bf16[56,896]{1,0:T(8,128)(2,1)S(1)} %get-tuple-element.55), channel_id=1, source_target_pairs={{0,2},{2,4},{4,6},{6,7},{7,5},{5,3},{3,1},{1,0},{8,10},{10,12},{12... | collective-permute-start | bytes 301064 | tf_op jit(solution)/shard_map/ppermute | solution.py:318
  49.9 0.4 collective-permute-start.11
  50.3 2.6 %collective-permute-done.10.forward = bf16[56,896]{1,0:T(8,128)(2,1)S(1)} collective-permute-done((bf16[56,896]{1,0:T(8,128)(2,1)S(1)}, bf16[56,896]{1,0:T(8,128)(2,1)S(1)}, u32[]{:S(2)}, u32[]{:S(2)}) %collective-permute-start.10) | collective-permute-done | bytes 100384 | tf_op jit(solution)/shard_map/ppermute | solution.py:318
  52.9 1.6 %collective-permute-done.11.backward = bf16[56,896]{1,0:T(8,128)(2,1)S(1)} collective-permute-done((bf16[56,896]{1,0:T(8,128)(2,1)S(1)}, bf16[56,896]{1,0:T(8,128)(2,1)S(1)}, u32[]{:S(2)}, u32[]{:S(2)}) %collective-permute-start.11) | collective-permute-done | bytes 100384 | tf_op jit(solution)/shard_map/ppermute | solution.py:319
  54.5 0.1 shard_map.96
  54.6 1.6 %collective-permute-start.12 = (bf16[112,896]{1,0:T(8,128)(2,1)S(1)}, bf16[112,896]{1,0:T(8,128)(2,1)S(1)}, u32[]{:S(2)}, u32[]{:S(2)}) collective-permute-start(bf16[112,896]{1,0:T(8,128)(2,1)S(1)} %get-tuple-element.58), channel_id=1, source_target_pairs={{0,2},{2,4},{4,6},{6,7},{7,5},{5,3},{3,1},{1,0},{8,10},{10,12},{12... | collective-permute-start | bytes 602120 | tf_op jit(solution)/shard_map/ppermute | solution.py:322
  56.2 0.4 collective-permute-start.13
  56.7 1.6 %collective-permute-start.18 = (bf16[224,896]{1,0:T(8,128)(2,1)S(1)}, bf16[224,896]{1,0:T(8,128)(2,1)S(1)}, u32[]{:S(2)}, u32[]{:S(2)}) collective-permute-start(bf16[224,896]{1,0:T(8,128)(2,1)S(1)} %get-tuple-element.68), channel_id=1, source_target_pairs={{0,2},{1,3},{2,4},{3,5},{4,6},{5,7},{6,0},{7,1},{8,10},{9,11},{10,... | collective-permute-start | bytes 1204232 | tf_op jit(solution)/shard_map/ppermute | solution.py:235
  58.2 1.5 %collective-permute-start.22 = (bf16[224,896]{1,0:T(8,128)(2,1)S(1)}, bf16[224,896]{1,0:T(8,128)(2,1)S(1)}, u32[]{:S(2)}, u32[]{:S(2)}) collective-permute-start(bf16[224,896]{1,0:T(8,128)(2,1)S(1)} %get-tuple-element.73), channel_id=1, source_target_pairs={{0,2},{1,3},{2,4},{3,5},{4,6},{5,7},{6,0},{7,1},{8,10},{9,11},{10,... | collective-permute-start | bytes 1204232 | tf_op jit(solution)/shard_map/ppermute | solution.py:236
  59.8 1.8 %collective-permute-done.12.forward = bf16[112,896]{1,0:T(8,128)(2,1)S(1)} collective-permute-done((bf16[112,896]{1,0:T(8,128)(2,1)S(1)}, bf16[112,896]{1,0:T(8,128)(2,1)S(1)}, u32[]{:S(2)}, u32[]{:S(2)}) %collective-permute-start.12) | collective-permute-done | bytes 200736 | tf_op jit(solution)/shard_map/ppermute | solution.py:322
  61.6 2.7 %collective-permute-done.13.backward = bf16[112,896]{1,0:T(8,128)(2,1)S(1)} collective-permute-done((bf16[112,896]{1,0:T(8,128)(2,1)S(1)}, bf16[112,896]{1,0:T(8,128)(2,1)S(1)}, u32[]{:S(2)}, u32[]{:S(2)}) %collective-permute-start.13) | collective-permute-done | bytes 200736 | tf_op jit(solution)/shard_map/ppermute | solution.py:323
  64.2 0.1 shard_map.97
  64.3 15.0 %collective-permute-start.14 = (bf16[112,896]{1,0:T(8,128)(2,1)S(1)}, bf16[112,896]{1,0:T(8,128)(2,1)S(1)}, u32[]{:S(2)}, u32[]{:S(2)}) collective-permute-start(bf16[112,896]{1,0:T(8,128)(2,1)S(1)} %get-tuple-element.61), channel_id=1, source_target_pairs={{0,2},{2,4},{4,6},{6,7},{7,5},{5,3},{3,1},{1,0},{8,10},{10,12},{12... | collective-permute-start | bytes 602120 | tf_op jit(solution)/shard_map/ppermute | solution.py:322
  79.4 0.0 collective-permute-start.15
  79.4 0.0 collective-permute-done.20
  79.4 0.1 fusion.3
  79.5 2.1 %collective-permute-start.21 = (bf16[224,896]{1,0:T(8,128)(2,1)S(1)}, bf16[224,896]{1,0:T(8,128)(2,1)S(1)}, u32[]{:S(2)}, u32[]{:S(2)}) collective-permute-start(bf16[224,896]{1,0:T(8,128)(2,1)S(1)} %fusion.3), channel_id=1, source_target_pairs={{0,2},{1,3},{2,4},{3,5},{4,6},{5,7},{6,0},{7,1},{8,10},{9,11},{10,... | collective-permute-start | bytes 1204232 | tf_op jit(solution)/shard_map/ppermute | solution.py:317
  81.6 3.2 %collective-permute-done.14.forward = bf16[112,896]{1,0:T(8,128)(2,1)S(1)} collective-permute-done((bf16[112,896]{1,0:T(8,128)(2,1)S(1)}, bf16[112,896]{1,0:T(8,128)(2,1)S(1)}, u32[]{:S(2)}, u32[]{:S(2)}) %collective-permute-start.14) | collective-permute-done | bytes 200736 | tf_op jit(solution)/shard_map/ppermute | solution.py:322
  84.8 9.0 %collective-permute-done.15.backward = bf16[112,896]{1,0:T(8,128)(2,1)S(1)} collective-permute-done((bf16[112,896]{1,0:T(8,128)(2,1)S(1)}, bf16[112,896]{1,0:T(8,128)(2,1)S(1)}, u32[]{:S(2)}, u32[]{:S(2)}) %collective-permute-start.15) | collective-permute-done | bytes 200736 | tf_op jit(solution)/shard_map/ppermute | solution.py:323
  93.7 0.1 shard_map.98
  93.8 0.1 collective-permute-start.16
  93.9 2.0 %collective-permute-start.17 = (bf16[112,896]{1,0:T(8,128)(2,1)S(1)}, bf16[112,896]{1,0:T(8,128)(2,1)S(1)}, u32[]{:S(2)}, u32[]{:S(2)}) collective-permute-start(bf16[112,896]{1,0:T(8,128)(2,1)S(1)} %get-tuple-element.65), channel_id=1, source_target_pairs={{2,0},{4,2},{6,4},{7,6},{5,7},{3,5},{1,3},{0,1},{10,8},{12,10},{14... | collective-permute-start | bytes 602120 | tf_op jit(solution)/shard_map/ppermute | solution.py:323
  95.9 3.7 %collective-permute-done.16.refs_1_ = bf16[112,896]{1,0:T(8,128)(2,1)S(1)} collective-permute-done((bf16[112,896]{1,0:T(8,128)(2,1)S(1)}, bf16[112,896]{1,0:T(8,128)(2,1)S(1)}, u32[]{:S(2)}, u32[]{:S(2)}) %collective-permute-start.16) | collective-permute-done | bytes 200736 | tf_op jit(solution)/shard_map/ppermute | solution.py:322
  99.6 0.1 collective-permute-done.17.refs_2_
  99.7 1.0 shard_map.99
  100.7 0.0 collective-permute-done.18
  100.7 0.0 collective-permute-done.22
  100.7 0.0 collective-permute-done.21
  100.7 1.3 %fusion.2 = (f32[1,224,896]{2,1,0:T(8,128)}, f32[1,224,896]{2,1,0:T(8,128)}) fusion(bf16[224,896]{1,0:T(8,128)(2,1)S(1)} %collective-permute-done.21, bf16[224,896]{1,0:T(8,128)(2,1)S(1)} %collective-permute-done.22, bf16[224,896]{1,0:T(8,128)(2,1)S(1)} %collective-permute-done.18), kind=kLoop, calls=%fused_computation.4 | loop fusion | flops 1404928 | bytes 2809856 | tf_op jit(solution)/shard_map/broadcast_in_dim | solution.py:345
  (9 shorter events, 0.1 us)
Async XLA Ops:
  0.6 5.6 %copy-start = (f32[1,112,896]{2,1,0:T(8,128)S(1)}, f32[1,112,896]{2,1,0:T(8,128)}, u32[]{:S(2)}) copy-start(f32[1,112,896]{2,1,0:T(8,128)} %param.8) | copy-start | bytes 1204228
  0.6 1.2 %copy-start.1 = (f32[1,224,896]{2,1,0:T(8,128)S(1)}, f32[1,224,896]{2,1,0:T(8,128)}, u32[]{:S(2)}) copy-start(f32[1,224,896]{2,1,0:T(8,128)} %param.10) | copy-start | bytes 2408452
  1.8 1.1 %copy-start.2 = (f32[1,224,896]{2,1,0:T(8,128)S(1)}, f32[1,224,896]{2,1,0:T(8,128)}, u32[]{:S(2)}) copy-start(f32[1,224,896]{2,1,0:T(8,128)} %param.11) | copy-start | bytes 2408452
  3.1 34.1 %copy-start.4 = (bf16[1,1,512,896]{3,2,1,0:T(8,128)(2,1)S(1)}, bf16[1,1,512,896]{3,2,1,0:T(8,128)(2,1)}, u32[]{:S(2)}) copy-start(bf16[1,1,512,896]{3,2,1,0:T(8,128)(2,1)} %param.7) | copy-start | bytes 2752516
  3.1 34.1 %copy-start.5 = (bf16[1,1,512,896]{3,2,1,0:T(8,128)(2,1)S(1)}, bf16[1,1,512,896]{3,2,1,0:T(8,128)(2,1)}, u32[]{:S(2)}) copy-start(bf16[1,1,512,896]{3,2,1,0:T(8,128)(2,1)} %param.6) | copy-start | bytes 2752516
  3.2 12.3 %collective-permute-start.8 = (bf16[1,224,896]{2,1,0:T(8,128)(2,1)S(1)}, bf16[1,224,896]{2,1,0:T(8,128)(2,1)S(1)}, u32[]{:S(2)}, u32[]{:S(2)}) collective-permute-start(bf16[1,224,896]{2,1,0:T(8,128)(2,1)S(1)} %bitcast.20), channel_id=1, source_target_pairs={{0,16},{8,24},{16,0},{24,8},{1,17},{9,25},{17,1},{25,9},{2,18},{10... | collective-permute-start | bytes 1204232 | tf_op jit(solution)/shard_map/ppermute | solution.py:228
  6.2 9.4 %collective-permute-start.1 = (bf16[112,896]{1,0:T(8,128)(2,1)S(1)}, bf16[112,896]{1,0:T(8,128)(2,1)S(1)}, u32[]{:S(2)}, u32[]{:S(2)}) collective-permute-start(bf16[112,896]{1,0:T(8,128)(2,1)S(1)} %bitcast_convert_fusion.refs_0_), channel_id=1, source_target_pairs={{2,0},{4,2},{6,4},{7,6},{5,7},{3,5},{1,3},{0,1},{10,8},{12,10},{14... | collective-permute-start | bytes 602120 | tf_op jit(solution)/shard_map/ppermute | solution.py:221
  7.8 7.9 %collective-permute-start = (bf16[112,896]{1,0:T(8,128)(2,1)S(1)}, bf16[112,896]{1,0:T(8,128)(2,1)S(1)}, u32[]{:S(2)}, u32[]{:S(2)}) collective-permute-start(bf16[112,896]{1,0:T(8,128)(2,1)S(1)} %bitcast_convert_fusion.refs_0_), channel_id=1, source_target_pairs={{0,2},{2,4},{4,6},{6,7},{7,5},{5,3},{3,1},{1,0},{8,10},{10,12},{12... | collective-permute-start | bytes 602120 | tf_op jit(solution)/shard_map/ppermute | solution.py:220
  15.6 21.7 %collective-permute-start.9 = (bf16[2,224,896]{2,1,0:T(8,128)(2,1)S(1)}, bf16[2,224,896]{2,1,0:T(8,128)(2,1)S(1)}, u32[]{:S(2)}, u32[]{:S(2)}) collective-permute-start(bf16[2,224,896]{2,1,0:T(8,128)(2,1)S(1)} %pad_maximum_fusion), channel_id=1, source_target_pairs={{0,8},{8,0},{16,24},{24,16},{1,9},{9,1},{17,25},{25,17},{2,10},{10... | collective-permute-start | bytes 2408456 | tf_op jit(solution)/shard_map/ppermute | solution.py:228
  15.7 7.4 %collective-permute-start.2 = (bf16[112,896]{1,0:T(8,128)(2,1)S(1)}, bf16[112,896]{1,0:T(8,128)(2,1)S(1)}, u32[]{:S(2)}, u32[]{:S(2)}) collective-permute-start(bf16[112,896]{1,0:T(8,128)(2,1)S(1)} %collective-permute-done.refs_1_), channel_id=1, source_target_pairs={{0,2},{2,4},{4,6},{6,7},{7,5},{5,3},{3,1},{1,0},{8,10},{10,12},{12... | collective-permute-start | bytes 602120 | tf_op jit(solution)/shard_map/ppermute | solution.py:220
  17.5 7.0 %collective-permute-start.3 = (bf16[112,896]{1,0:T(8,128)(2,1)S(1)}, bf16[112,896]{1,0:T(8,128)(2,1)S(1)}, u32[]{:S(2)}, u32[]{:S(2)}) collective-permute-start(bf16[112,896]{1,0:T(8,128)(2,1)S(1)} %collective-permute-done.1.refs_2_), channel_id=1, source_target_pairs={{2,0},{4,2},{6,4},{7,6},{5,7},{3,5},{1,3},{0,1},{10,8},{12,10},{14... | collective-permute-start | bytes 602120 | tf_op jit(solution)/shard_map/ppermute | solution.py:221
  24.6 6.2 %collective-permute-start.4 = (bf16[112,896]{1,0:T(8,128)(2,1)S(1)}, bf16[112,896]{1,0:T(8,128)(2,1)S(1)}, u32[]{:S(2)}, u32[]{:S(2)}) collective-permute-start(bf16[112,896]{1,0:T(8,128)(2,1)S(1)} %collective-permute-done.2.refs_3_), channel_id=1, source_target_pairs={{0,2},{2,4},{4,6},{6,7},{7,5},{5,3},{3,1},{1,0},{8,10},{10,12},{12... | collective-permute-start | bytes 602120 | tf_op jit(solution)/shard_map/ppermute | solution.py:220
  26.2 5.9 %collective-permute-start.5 = (bf16[112,896]{1,0:T(8,128)(2,1)S(1)}, bf16[112,896]{1,0:T(8,128)(2,1)S(1)}, u32[]{:S(2)}, u32[]{:S(2)}) collective-permute-start(bf16[112,896]{1,0:T(8,128)(2,1)S(1)} %collective-permute-done.3.refs_4_), channel_id=1, source_target_pairs={{2,0},{4,2},{6,4},{7,6},{5,7},{3,5},{1,3},{0,1},{10,8},{12,10},{14... | collective-permute-start | bytes 602120 | tf_op jit(solution)/shard_map/ppermute | solution.py:221
  32.1 4.7 %collective-permute-start.7 = (bf16[56,896]{1,0:T(8,128)(2,1)S(1)}, bf16[56,896]{1,0:T(8,128)(2,1)S(1)}, u32[]{:S(2)}, u32[]{:S(2)}) collective-permute-start(bf16[56,896]{1,0:T(8,128)(2,1)S(1)} %slice.7), channel_id=1, source_target_pairs={{2,0},{4,2},{6,4},{7,6},{5,7},{3,5},{1,3},{0,1},{10,8},{12,10},{14... | collective-permute-start | bytes 301064 | tf_op jit(solution)/shard_map/ppermute | solution.py:221
  32.6 4.6 %collective-permute-start.6 = (bf16[56,896]{1,0:T(8,128)(2,1)S(1)}, bf16[56,896]{1,0:T(8,128)(2,1)S(1)}, u32[]{:S(2)}, u32[]{:S(2)}) collective-permute-start(bf16[56,896]{1,0:T(8,128)(2,1)S(1)} %slice.6), channel_id=1, source_target_pairs={{0,2},{2,4},{4,6},{6,7},{7,5},{5,3},{3,1},{1,0},{8,10},{10,12},{12... | collective-permute-start | bytes 301064 | tf_op jit(solution)/shard_map/ppermute | solution.py:220
  41.7 2.4 %collective-permute-start.19 = (bf16[2,224,896]{2,1,0:T(8,128)(2,1)S(1)}, bf16[2,224,896]{2,1,0:T(8,128)(2,1)S(1)}, u32[]{:S(2)}, u32[]{:S(2)}) collective-permute-start(bf16[2,224,896]{2,1,0:T(8,128)(2,1)S(1)} %get-tuple-element.70), channel_id=1, source_target_pairs={{0,8},{8,0},{16,24},{24,16},{1,9},{9,1},{17,25},{25,17},{2,10},{10... | collective-permute-start | bytes 2408456 | tf_op jit(solution)/shard_map/ppermute | solution.py:271
  44.3 35.1 %collective-permute-start.20 = (bf16[1,224,896]{2,1,0:T(8,128)(2,1)S(1)}, bf16[1,224,896]{2,1,0:T(8,128)(2,1)S(1)}, u32[]{:S(2)}, u32[]{:S(2)}) collective-permute-start(bf16[1,224,896]{2,1,0:T(8,128)(2,1)S(1)} %get-tuple-element.72), channel_id=1, source_target_pairs={{0,16},{8,24},{16,0},{24,8},{1,17},{9,25},{17,1},{25,9},{2,18},{10... | collective-permute-start | bytes 1204232 | tf_op jit(solution)/shard_map/ppermute | solution.py:314
  48.2 4.7 %collective-permute-start.10 = (bf16[56,896]{1,0:T(8,128)(2,1)S(1)}, bf16[56,896]{1,0:T(8,128)(2,1)S(1)}, u32[]{:S(2)}, u32[]{:S(2)}) collective-permute-start(bf16[56,896]{1,0:T(8,128)(2,1)S(1)} %get-tuple-element.55), channel_id=1, source_target_pairs={{0,2},{2,4},{4,6},{6,7},{7,5},{5,3},{3,1},{1,0},{8,10},{10,12},{12... | collective-permute-start | bytes 301064 | tf_op jit(solution)/shard_map/ppermute | solution.py:318
  49.9 4.6 %collective-permute-start.11 = (bf16[56,896]{1,0:T(8,128)(2,1)S(1)}, bf16[56,896]{1,0:T(8,128)(2,1)S(1)}, u32[]{:S(2)}, u32[]{:S(2)}) collective-permute-start(bf16[56,896]{1,0:T(8,128)(2,1)S(1)} %get-tuple-element.57), channel_id=1, source_target_pairs={{2,0},{4,2},{6,4},{7,6},{5,7},{3,5},{1,3},{0,1},{10,8},{12,10},{14... | collective-permute-start | bytes 301064 | tf_op jit(solution)/shard_map/ppermute | solution.py:319
  54.5 45.2 %copy-start.3 = (f32[1,112,896]{2,1,0:T(8,128)S(1)}, f32[1,112,896]{2,1,0:T(8,128)}, u32[]{:S(2)}) copy-start(f32[1,112,896]{2,1,0:T(8,128)} %param.9) | copy-start | bytes 1204228
  54.6 7.0 %collective-permute-start.12 = (bf16[112,896]{1,0:T(8,128)(2,1)S(1)}, bf16[112,896]{1,0:T(8,128)(2,1)S(1)}, u32[]{:S(2)}, u32[]{:S(2)}) collective-permute-start(bf16[112,896]{1,0:T(8,128)(2,1)S(1)} %get-tuple-element.58), channel_id=1, source_target_pairs={{0,2},{2,4},{4,6},{6,7},{7,5},{5,3},{3,1},{1,0},{8,10},{10,12},{12... | collective-permute-start | bytes 602120 | tf_op jit(solution)/shard_map/ppermute | solution.py:322
  56.2 8.0 %collective-permute-start.13 = (bf16[112,896]{1,0:T(8,128)(2,1)S(1)}, bf16[112,896]{1,0:T(8,128)(2,1)S(1)}, u32[]{:S(2)}, u32[]{:S(2)}) collective-permute-start(bf16[112,896]{1,0:T(8,128)(2,1)S(1)} %get-tuple-element.60), channel_id=1, source_target_pairs={{2,0},{4,2},{6,4},{7,6},{5,7},{3,5},{1,3},{0,1},{10,8},{12,10},{14... | collective-permute-start | bytes 602120 | tf_op jit(solution)/shard_map/ppermute | solution.py:323
  56.7 44.0 %collective-permute-start.18 = (bf16[224,896]{1,0:T(8,128)(2,1)S(1)}, bf16[224,896]{1,0:T(8,128)(2,1)S(1)}, u32[]{:S(2)}, u32[]{:S(2)}) collective-permute-start(bf16[224,896]{1,0:T(8,128)(2,1)S(1)} %get-tuple-element.68), channel_id=1, source_target_pairs={{0,2},{1,3},{2,4},{3,5},{4,6},{5,7},{6,0},{7,1},{8,10},{9,11},{10,... | collective-permute-start | bytes 1204232 | tf_op jit(solution)/shard_map/ppermute | solution.py:235
  58.2 42.4 %collective-permute-start.22 = (bf16[224,896]{1,0:T(8,128)(2,1)S(1)}, bf16[224,896]{1,0:T(8,128)(2,1)S(1)}, u32[]{:S(2)}, u32[]{:S(2)}) collective-permute-start(bf16[224,896]{1,0:T(8,128)(2,1)S(1)} %get-tuple-element.73), channel_id=1, source_target_pairs={{0,2},{1,3},{2,4},{3,5},{4,6},{5,7},{6,0},{7,1},{8,10},{9,11},{10,... | collective-permute-start | bytes 1204232 | tf_op jit(solution)/shard_map/ppermute | solution.py:236
  64.3 20.4 %collective-permute-start.14 = (bf16[112,896]{1,0:T(8,128)(2,1)S(1)}, bf16[112,896]{1,0:T(8,128)(2,1)S(1)}, u32[]{:S(2)}, u32[]{:S(2)}) collective-permute-start(bf16[112,896]{1,0:T(8,128)(2,1)S(1)} %get-tuple-element.61), channel_id=1, source_target_pairs={{0,2},{2,4},{4,6},{6,7},{7,5},{5,3},{3,1},{1,0},{8,10},{10,12},{12... | collective-permute-start | bytes 602120 | tf_op jit(solution)/shard_map/ppermute | solution.py:322
  79.4 14.3 %collective-permute-start.15 = (bf16[112,896]{1,0:T(8,128)(2,1)S(1)}, bf16[112,896]{1,0:T(8,128)(2,1)S(1)}, u32[]{:S(2)}, u32[]{:S(2)}) collective-permute-start(bf16[112,896]{1,0:T(8,128)(2,1)S(1)} %get-tuple-element.63), channel_id=1, source_target_pairs={{2,0},{4,2},{6,4},{7,6},{5,7},{3,5},{1,3},{0,1},{10,8},{12,10},{14... | collective-permute-start | bytes 602120 | tf_op jit(solution)/shard_map/ppermute | solution.py:323
  79.5 21.2 %collective-permute-start.21 = (bf16[224,896]{1,0:T(8,128)(2,1)S(1)}, bf16[224,896]{1,0:T(8,128)(2,1)S(1)}, u32[]{:S(2)}, u32[]{:S(2)}) collective-permute-start(bf16[224,896]{1,0:T(8,128)(2,1)S(1)} %fusion.3), channel_id=1, source_target_pairs={{0,2},{1,3},{2,4},{3,5},{4,6},{5,7},{6,0},{7,1},{8,10},{9,11},{10,... | collective-permute-start | bytes 1204232 | tf_op jit(solution)/shard_map/ppermute | solution.py:317
  93.8 5.8 %collective-permute-start.16 = (bf16[112,896]{1,0:T(8,128)(2,1)S(1)}, bf16[112,896]{1,0:T(8,128)(2,1)S(1)}, u32[]{:S(2)}, u32[]{:S(2)}) collective-permute-start(bf16[112,896]{1,0:T(8,128)(2,1)S(1)} %get-tuple-element.64), channel_id=1, source_target_pairs={{0,2},{2,4},{4,6},{6,7},{7,5},{5,3},{3,1},{1,0},{8,10},{10,12},{12... | collective-permute-start | bytes 602120 | tf_op jit(solution)/shard_map/ppermute | solution.py:322
  93.9 5.8 %collective-permute-start.17 = (bf16[112,896]{1,0:T(8,128)(2,1)S(1)}, bf16[112,896]{1,0:T(8,128)(2,1)S(1)}, u32[]{:S(2)}, u32[]{:S(2)}) collective-permute-start(bf16[112,896]{1,0:T(8,128)(2,1)S(1)} %get-tuple-element.65), channel_id=1, source_target_pairs={{2,0},{4,2},{6,4},{7,6},{5,7},{3,5},{1,3},{0,1},{10,8},{12,10},{14... | collective-permute-start | bytes 602120 | tf_op jit(solution)/shard_map/ppermute | solution.py:323

commit v4 on v3

--- a/solution.py
+++ b/solution.py
@@ -12,6 +12,7 @@
 outer_rate = 0.7
 BF16 = jnp.bfloat16
 F32 = jnp.float32
+AHEAD = 5
 WHOLE = pl.BlockSpec(memory_space=pltpu.VMEM)
 
 
@@ -45,10 +46,15 @@
     return jnp.where(place < length // 2, 2 * place, 2 * (length - 1 - place) + 1)
 
 
-def ring_pairs(length):
-    order = list(range(0, length, 2)) + list(range(length - 1, 0, -2))
-    up = [(order[i], order[(i + 1) % length]) for i in range(length)]
-    return up, [(b, a) for a, b in up]
+def two_way(n_row, columns):
+    order = list(range(0, columns, 2)) + list(range(columns - 1, 0, -2))
+    pairs = []
+    for row in range(n_row):
+        for i in range(columns):
+            ends = (order[i], order[(i + 1) % columns])
+            source, target = ends if row % 2 == 0 else ends[::-1]
+            pairs.append((row * columns + source, row * columns + target))
+    return pairs
 
 
 def swap_pairs(length, bit):
@@ -66,15 +72,15 @@
 
 def rows_from(pieces, rows, length):
     full = jnp.zeros((rows * length,) + pieces[0][0].shape[1:], pieces[0][0].dtype)
-    for block, member, first in pieces:
-        full = lax.dynamic_update_slice(full, block, (member * rows + first, 0))
+    for block, member in pieces:
+        full = lax.dynamic_update_slice(full, block, (member * rows, 0))
     return full
 
 
-def prepare_kernel(params, moment, params_out, early_params, early_moment):
-    params_out[...] = params[...].astype(BF16)
-    early_params[...] = (params[...] - outer_rate * outer_momentum**2 * moment[...]).astype(BF16)
-    early_moment[...] = moment[...].astype(BF16)
+def prepare_kernel(params, moment, early):
+    ahead = early.shape[1]
+    early[0] = (params[:ahead] - outer_rate * outer_momentum**2 * moment[:ahead]).astype(BF16)
+    early[1] = moment[:ahead].astype(BF16)
 
 
 def forward_kernel(first_plan, second_plan, columns, n_row, *refs):
@@ -85,13 +91,14 @@
     first_full, active, grad = refs[n1 + n2 + 7 :]
     tokens, width = inputs.shape
     col, row = lax.axis_index("col"), lax.axis_index("row")
-    place = place_of(col, columns)
+    place, way = place_of(col, columns), 1 - 2 * (row % 2)
     for ref, back in zip(first_refs, first_plan):
         if back is None:
             first_full[...] = ref[...]
         else:
             rows = ref.shape[0]
-            first_full[pl.ds(pl.multiple_of(member_at(place + back, columns) * rows, rows), rows), :] = ref[...]
+            start = member_at(place + way * back, columns) * rows
+            first_full[pl.ds(pl.multiple_of(start, rows), rows), :] = ref[...]
     for ref, flips in zip(second_refs, second_plan):
         if flips is None:
             second_ref[...] = ref[...]
@@ -132,48 +139,48 @@
     if len(outs) == 1:
         outs[0][...] = value.astype(BF16)
         return
-    grad[...] = value
-    place = place_of(lax.axis_index("col"), columns)
+    grad[...] = value.astype(BF16)
+    place, way = place_of(lax.axis_index("col"), columns), 1 - 2 * (lax.axis_index("row") % 2)
     rows = grad.shape[0] // columns
-    half = rows // 2
-
-    def block(away, first, count):
-        start = member_at(place + away, columns) * rows + first
-        return grad[pl.ds(pl.multiple_of(start, 8), count), :].astype(BF16)
-
-    outs[0][...] = block(columns // 2, 0, half)
-    outs[1][...] = block(columns // 2, half, half)
-    outs[2][...] = block(0, 0, rows)
-    for k in range(1, columns // 2):
-        outs[2 * k + 1][...] = block(k, 0, rows)
-        outs[2 * k + 2][...] = block(-k, 0, rows)
-
-
-def add_kernel(ahead, forward, behind, backward, ahead_out, behind_out):
-    rows, got = ahead.shape[0], forward.shape[0]
-    if rows == got:
-        ahead_out[...] = (ahead[...].astype(F32) + forward[...].astype(F32)).astype(BF16)
-        behind_out[...] = (behind[...].astype(F32) + backward[...].astype(F32)).astype(BF16)
-        return
-    term = ahead[...].astype(F32)
-    top = term[:got] + forward[...].astype(F32)
-    ahead_out[...] = jnp.concatenate([top, term[got:]]).astype(BF16)
-    term = behind[...].astype(F32)
-    low = term[rows - got :] + backward[...].astype(F32)
-    behind_out[...] = jnp.concatenate([term[: rows - got], low]).astype(BF16)
-
-
-def add_both(ahead, forward, behind, backward):
-    rows, got = ahead.shape[0], forward.shape[0]
-    if tiled(rows):
-        outs = [shape_of(ahead.shape)] * 2
-        return call(add_kernel, outs, [], ahead, forward, behind, backward)
-    zero = jnp.zeros((rows - got,) + forward.shape[1:], BF16)
-    forward, backward = jnp.concatenate([forward, zero]), jnp.concatenate([zero, backward])
-    return (
-        (ahead.astype(F32) + forward.astype(F32)).astype(BF16),
-        (behind.astype(F32) + backward.astype(F32)).astype(BF16),
-    )
+
+    def block(away):
+        start = member_at(place + way * away, columns) * rows
+        return grad[pl.ds(pl.multiple_of(start, rows), rows), :]
+
+    *own, other = outs
+    for k, ref in enumerate(own):
+        ref[...] = block(columns // 2 - k)
+    for k in range(other.shape[0]):
+        other[k] = block(-(columns // 2 - 1 - k))
+
+
+def add_kernel(term, came, out):
+    out[...] = (term[...].reshape(out.shape).astype(F32) + came[...].astype(F32)).astype(BF16)
+
+
+def added(term, came):
+    if tiled(came.shape[0]):
+        return call(add_kernel, [shape_of(came.shape)], [], term, came)[0]
+    return (term.reshape(came.shape).astype(F32) + came.astype(F32)).astype(BF16)
+
+
+def second_kernel(n_row, ahead, kept, came, params, moment, late):
+    grad = (kept[0].astype(F32) + came[0].astype(F32)) / n_row
+    rows = grad.shape[0]
+    late[:ahead] = grad[:ahead].astype(BF16)
+    moment_new = outer_momentum * moment[ahead:] + grad[ahead:]
+    params_new = params[ahead:] - outer_rate * (grad[ahead:] + outer_momentum * moment_new)
+    late[ahead:rows] = params_new.astype(BF16)
+    late[rows:] = moment_new.astype(BF16)
+
+
+def arrive_kernel(early, late, params_out, moment_out):
+    ahead, rows = early.shape[1], params_out.shape[0]
+    grad = late[:ahead].astype(F32)
+    params_out[:ahead] = early[0].astype(F32) - outer_rate * (1 + outer_momentum) * grad
+    moment_out[:ahead] = outer_momentum * early[1].astype(F32) + grad
+    params_out[ahead:] = late[ahead:rows].astype(F32)
+    moment_out[ahead:] = late[rows:].astype(F32)
 
 
 def first_kernel(columns, own, forward, backward, params, moment, params_out, moment_out):
@@ -199,29 +206,30 @@
     columns, n_row = lax.axis_size("col"), lax.axis_size("row")
     offset = columns // 4
     rows1, rows2 = first_params.shape[1], second_params.shape[1]
-    up, down = ring_pairs(columns)
+    ring = two_way(n_row, columns)
     ahead_by = [(i, (i + offset) % columns) for i in range(columns)]
     last = columns // 2
-    half = rows1 // 2
     place = place_of(lax.axis_index("col"), columns)
     row = lax.axis_index("row")
-
+    way = 1 - 2 * (row % 2)
+    partner = swap_pairs(n_row, 1)
+
+    ahead = AHEAD * rows2 // 8 // 16 * 16
     own1 = first_params[0].astype(BF16)
-    shard = shape_of((rows2, width))
-    held, early_params, early_moment = call(
-        prepare_kernel, [shard] * 3, [], second_params[0], second_moment[0]
-    )
+    held = second_params[0].astype(BF16)
+    early = call(
+        prepare_kernel, [shape_of((2, ahead, width))], [], second_params[0], second_moment[0]
+    )[0]
     held = held[None]
-    first_pieces = [(own1, 0, 0)]
-    forward = backward = own1
+    first_pieces = [(own1, 0)]
+    ours, theirs = own1, lax.ppermute(own1, "row", partner)
     for step in range(1, last + 1):
-        if step == last:
-            forward, backward = forward[:half], backward[half:]
-        forward = lax.ppermute(forward, "col", up)
-        backward = lax.ppermute(backward, "col", down)
-        forward, backward = lax.optimization_barrier((forward, backward))
+        later = ours
+        ours = lax.ppermute(ours, ("row", "col"), ring)
+        first_pieces.append((ours, -step))
         if step < last:
-            first_pieces += [(forward, -step, 0), (backward, step, 0)]
+            theirs = lax.ppermute(theirs, ("row", "col"), ring)
+            first_pieces.append((lax.ppermute(theirs, "row", partner), step))
     second_pieces, flips = [(held, [0])], [0]
     bit = n_row // 2
     while bit >= 1:
@@ -231,23 +239,20 @@
         flips = flips + others
         bit = bit // 2
         if bit >= 1:
+            other, _ = lax.optimization_barrier((other, later))
             held = jnp.concatenate([held, other])
-    early_params = lax.ppermute(early_params, "col", ahead_by)
-    early_moment = lax.ppermute(early_moment, "col", ahead_by)
+    early, _ = lax.optimization_barrier((early, ours))
+    early = lax.ppermute(early, "col", ahead_by)
     if tiled(rows1):
-        antipode = jnp.concatenate([forward, backward])
-        first_pieces.append((antipode, last, 0))
-        first_plan = [p[1] for p in first_pieces]
-        first_blocks = [p[0] for p in first_pieces]
+        first_blocks, first_plan = [p[0] for p in first_pieces], [p[1] for p in first_pieces]
     else:
-        first_pieces += [(forward, last, 0), (backward, last, half)]
-        placed = [(b, member_at(place + back, columns), at) for b, back, at in first_pieces]
+        placed = [(b, member_at(place + way * back, columns)) for b, back in first_pieces]
         first_blocks, first_plan = [rows_from(placed, rows1, columns)], [None]
     if tiled(rows2):
         second_plan = [p[1] for p in second_pieces]
         second_blocks = [p[0] for p in second_pieces]
     else:
-        placed = [(b[k], row ^ f, 0) for b, fs in second_pieces for k, f in enumerate(fs)]
+        placed = [(b[k], row ^ f) for b, fs in second_pieces for k, f in enumerate(fs)]
         second_blocks, second_plan = [rows_from(placed, rows2, n_row)], [None]
 
     def fwd(*refs):
@@ -273,12 +278,13 @@
     def bwd(*refs):
         backward_kernel(columns, *refs)
 
-    block, piece = shape_of((rows1, width)), shape_of((half, width))
-    outs = [piece, piece] + [block] * (columns - 1) if tiled(rows1) else [shape_of((width, width))]
+    block = shape_of((rows1, width))
+    outs = [block] * (last + 1) + [shape_of((last - 1, rows1, width))]
+    outs = outs if tiled(rows1) else [shape_of((width, width))]
     blocks = call(
         bwd,
         outs,
-        [pltpu.VMEM((width, width), F32)],
+        [pltpu.VMEM((width, width), BF16)],
         inputs,
         second_full,
         error,
@@ -286,14 +292,15 @@
         flops=4 * tokens * width * width,
     )
     if not tiled(rows1):
-        def cut(away, first=0, count=rows1):
-            start = member_at(place + away, columns) * rows1 + first
-            return lax.dynamic_slice_in_dim(blocks_full, start, count, 0)
-
         blocks_full = blocks[0]
-        blocks = [cut(last, 0, half), cut(last, half, half), cut(0)]
-        for k in range(1, last):
-            blocks += [cut(k), cut(-k)]
+
+        def cut(away):
+            start = member_at(place + way * away, columns) * rows1
+            return lax.dynamic_slice_in_dim(blocks_full, start, rows1, 0)
+
+        blocks = [cut(last - k) for k in range(last + 1)]
+        blocks.append(jnp.stack([cut(-(last - 1 - k)) for k in range(last - 1)]))
+    *own_terms, other_terms = blocks
 
     bit = 2
     while bit < n_row:
@@ -313,14 +320,26 @@
             kept = lax.dynamic_index_in_dim(total, mine, 1, keepdims=False)
         came = lax.ppermute(away, "row", swap_pairs(n_row, bit))
         bit = bit * 2
-    grad2 = ((kept[0].astype(F32) + came[0].astype(F32)) / n_row).astype(BF16)
-    grad2 = lax.ppermute(grad2, "col", ahead_by)
-    forward = lax.ppermute(blocks[0], "col", up)
-    backward = lax.ppermute(blocks[1], "col", down)
-    for left in range(last - 1, 0, -1):
-        forward, backward = add_both(blocks[2 * left + 1], forward, blocks[2 * left + 2], backward)
-        forward = lax.ppermute(forward, "col", up)
-        backward = lax.ppermute(backward, "col", down)
+    late = call(
+        lambda *refs: second_kernel(n_row, ahead, *refs),
+        [shape_of((2 * rows2 - ahead, width))],
+        [],
+        kept,
+        came,
+        second_params[0],
+        second_moment[0],
+    )[0]
+    late = lax.ppermute(late, "col", ahead_by)
+    ours = lax.ppermute(own_terms[0], ("row", "col"), ring)
+    other_terms = lax.ppermute(other_terms, "row", partner)
+    theirs = lax.ppermute(other_terms[0], ("row", "col"), ring)
+    for step in range(2, last + 1):
+        ours = added(own_terms[step - 1], ours)
+        ours = lax.ppermute(ours, ("row", "col"), ring)
+        if step < last:
+            theirs = added(other_terms[step - 1], theirs)
+            theirs = lax.ppermute(theirs, ("row", "col"), ring)
+    theirs = lax.ppermute(theirs, "row", partner)
 
     if tiled(rows1):
         out = shape_of((rows1, width), F32)
@@ -328,21 +347,19 @@
             lambda *refs: first_kernel(columns, *refs),
             [out, out],
             [],
-            blocks[2],
-            forward,
-            backward,
+            own_terms[last],
+            ours,
+            theirs,
             first_params[0],
             first_moment[0],
         )
     else:
-        total = blocks[2].astype(F32) + forward.astype(F32) + backward.astype(F32)
+        total = own_terms[last].astype(F32) + ours.astype(F32) + theirs.astype(F32)
         grad = total / columns
         moment_new = outer_momentum * first_moment[0] + grad
         first_new = (first_params[0] - outer_rate * (grad + outer_momentum * moment_new), moment_new)
-    grad2 = grad2.astype(F32)
-    second_moment_new = outer_momentum * early_moment.astype(F32) + grad2
-    second_params_new = early_params.astype(F32) - outer_rate * (1 + outer_momentum) * grad2
-    return (first_new[0][None], first_new[1][None], second_params_new[None], second_moment_new[None])
+    second_new = call(arrive_kernel, [shape_of((rows2, width), F32)] * 2, [], early, late)
+    return (first_new[0][None], first_new[1][None], second_new[0][None], second_new[1][None])
 
 
 def solution(mesh):

time: 102 us -> 93 us (0.912)
  starting transfers between devices: 39.4 us -> 34.2 us
  waiting for transfers between devices: 49.4 us -> 45.6 us
  local copies, waits for them, and re-layouts: 2.36 us -> 0.08 us
  Pallas kernels: 8.43 us -> 9.77 us
    ppermute x2, waiting for transfers between devices: 7.18 us -> 0.01 us  [per_device(): other = lax.ppermute(held, 'row', swap_pairs(n_row, bit))]
    ppermute x19 -> x22, starting transfers between devices: 34.7 us -> 30.9 us  [the longest x7 15.1 us: per_device(): ours = lax.ppermute(ours, ('row', 'col'), ring)]
    ppermute x19 -> x22, waiting for transfers between devices: 39.9 us -> 43.7 us  [the longest x7 34 us: per_device(): ours = lax.ppermute(ours, ('row', 'col'), ring)]
    unnamed x12, local copies, waits for them, and re-layouts: 2.34 us -> 0.03 us
    ppermute x1, waiting for transfers between devices: 2.3 us -> 0.01 us  [per_device(): came = lax.ppermute(away, 'row', swap_pairs(n_row, 1))]
    ppermute x1, waiting for transfers between devices: 0.01 us -> 1.93 us  [per_device(): came = lax.ppermute(away, 'row', swap_pairs(n_row, bit))]
    ppermute x2, starting transfers between devices: 3.1 us -> 1.63 us  [per_device(): other = lax.ppermute(held, 'row', swap_pairs(n_row, bit))]
    pallas_call x8 -> x12, Pallas kernels: 8.43 us -> 9.77 us  [call(): pl.pallas_call(kernel, out_shape=tuple(outs), in_specs=[WHOLE] * len(oper...]
  transfers between devices with their start and end apart: 23 -> 26, of which waited for: 16 -> 12; matrix products, arithmetic and copies ran while one was open for 0% -> 1% of each run, Pallas kernels for 4% -> 4%
where the time goes in v4:
time: 93 us; the launch traced here: 92.8 us
  waiting for transfers between devices  45.6 us (49%)
  starting transfers between devices  34.2 us (37%)
  Pallas kernels  9.77 us (11%)
  other arithmetic  2.42 us (3%)
    ppermute x7, waiting for transfers between devices, per_device(): ours = lax.ppermute(ours, ('row', 'col'), ring)  34 us
    ppermute x7, starting transfers between devices, per_device(): ours = lax.ppermute(ours, ('row', 'col'), ring)  15.1 us
    pallas_call x12, Pallas kernels, call(): pl.pallas_call(kernel, out_shape=tuple(outs), in_specs=[WHOLE] * len(oper...  9.77 us
    ppermute x5, starting transfers between devices, per_device(): theirs = lax.ppermute(theirs, ('row', 'col'), ring)  8.82 us
    ppermute x5, waiting for transfers between devices, per_device(): theirs = lax.ppermute(theirs, ('row', 'col'), ring)  7.68 us
    ppermute x1, starting transfers between devices, per_device(): ours = lax.ppermute(own_terms[0], ('row', 'col'), ring)  2.08 us
    ppermute x1, waiting for transfers between devices, per_device(): came = lax.ppermute(away, 'row', swap_pairs(n_row, bit))  1.93 us
  transfers between devices with their start and end apart: 26, of which 12 were waited for; matrix products, arithmetic and copies ran while one was open for 1% of the time, Pallas kernels for 4%

profile of v4, /device:TPU:0, one launch (start us, length us, event | category | flops | bytes accessed | tf_op | source)
XLA Modules:
  0.0 92.8 jit_solution(16374151862973940006)
XLA Ops:
  0.7 1.2 %bitcast_convert_fusion.refs_0_ = bf16[112,896]{1,0:T(8,128)(2,1)S(1)} fusion(f32[1,112,896]{2,1,0:T(8,128)} %param.8), kind=kLoop, calls=%fused_computation.4 | loop fusion | flops 100352 | bytes 602112 | tf_op jit(solution)/shard_map/convert_element_type | solution.py:218
  1.8 3.1 %collective-permute-start = (bf16[112,896]{1,0:T(8,128)(2,1)S(1)}, bf16[112,896]{1,0:T(8,128)(2,1)S(1)}, u32[]{:S(2)}, u32[]{:S(2)}) collective-permute-start(bf16[112,896]{1,0:T(8,128)(2,1)S(1)} %bitcast_convert_fusion.refs_0_), channel_id=1, source_target_pairs={{0,2},{2,4},{4,6},{6,7},{7,5},{5,3},{3,1},{1,0},{10,8},{12,10},{14... | collective-permute-start | bytes 602120 | tf_op jit(solution)/shard_map/ppermute | solution.py:228
  4.9 1.2 %convert_element_type.8.refs_8_ = bf16[1,224,896]{2,1,0:T(8,128)(2,1)S(1)} convert(f32[1,224,896]{2,1,0:T(8,128)} %param.10) | non-fusion elementwise | flops 200704 | bytes 1204224 | tf_op jit(solution)/shard_map/convert_element_type | solution.py:219
  6.1 1.6 %collective-permute-start.11 = (bf16[1,224,896]{2,1,0:T(8,128)(2,1)S(1)}, bf16[1,224,896]{2,1,0:T(8,128)(2,1)S(1)}, u32[]{:S(2)}, u32[]{:S(2)}) collective-permute-start(bf16[1,224,896]{2,1,0:T(8,128)(2,1)S(1)} %convert_element_type.8.refs_8_), channel_id=1, source_target_pairs={{0,16},{8,24},{16,0},{24,8},{1,17},{9,25},{17,1},{25,9},{2,18},{10... | collective-permute-start | bytes 1204232 | tf_op jit(solution)/shard_map/ppermute | solution.py:236
  7.7 0.9 collective-permute-done.refs_1_
  8.6 2.1 %collective-permute-start.4 = (bf16[112,896]{1,0:T(8,128)(2,1)S(1)}, bf16[112,896]{1,0:T(8,128)(2,1)S(1)}, u32[]{:S(2)}, u32[]{:S(2)}) collective-permute-start(bf16[112,896]{1,0:T(8,128)(2,1)S(1)} %collective-permute-done.refs_1_), channel_id=1, source_target_pairs={{0,2},{2,4},{4,6},{6,7},{7,5},{5,3},{3,1},{1,0},{10,8},{12,10},{14... | collective-permute-start | bytes 602120 | tf_op jit(solution)/shard_map/ppermute | solution.py:228
  10.6 0.0 collective-permute-start.1
  10.6 3.6 %collective-permute-done.4.refs_3_ = bf16[112,896]{1,0:T(8,128)(2,1)S(1)} collective-permute-done((bf16[112,896]{1,0:T(8,128)(2,1)S(1)}, bf16[112,896]{1,0:T(8,128)(2,1)S(1)}, u32[]{:S(2)}, u32[]{:S(2)}) %collective-permute-start.4) | collective-permute-done | bytes 200736 | tf_op jit(solution)/shard_map/ppermute | solution.py:228
  14.3 2.1 %collective-permute-start.7 = (bf16[112,896]{1,0:T(8,128)(2,1)S(1)}, bf16[112,896]{1,0:T(8,128)(2,1)S(1)}, u32[]{:S(2)}, u32[]{:S(2)}) collective-permute-start(bf16[112,896]{1,0:T(8,128)(2,1)S(1)} %collective-permute-done.4.refs_3_), channel_id=1, source_target_pairs={{0,2},{2,4},{4,6},{6,7},{7,5},{5,3},{3,1},{1,0},{10,8},{12,10},{14... | collective-permute-start | bytes 602120 | tf_op jit(solution)/shard_map/ppermute | solution.py:228
  16.3 0.0 collective-permute-done.1
  16.3 1.6 %collective-permute-start.2 = (bf16[112,896]{1,0:T(8,128)(2,1)S(1)}, bf16[112,896]{1,0:T(8,128)(2,1)S(1)}, u32[]{:S(2)}, u32[]{:S(2)}) collective-permute-start(bf16[112,896]{1,0:T(8,128)(2,1)S(1)} %collective-permute-done.1), channel_id=1, source_target_pairs={{0,2},{2,4},{4,6},{6,7},{7,5},{5,3},{3,1},{1,0},{10,8},{12,10},{14... | collective-permute-start | bytes 602120 | tf_op jit(solution)/shard_map/ppermute | solution.py:231
  17.9 0.0 collective-permute-done.11.refs_9_
  17.9 2.1 %collective-permute-done.7.refs_5_ = bf16[112,896]{1,0:T(8,128)(2,1)S(1)} collective-permute-done((bf16[112,896]{1,0:T(8,128)(2,1)S(1)}, bf16[112,896]{1,0:T(8,128)(2,1)S(1)}, u32[]{:S(2)}, u32[]{:S(2)}) %collective-permute-start.7) | collective-permute-done | bytes 200736 | tf_op jit(solution)/shard_map/ppermute | solution.py:228
  20.0 0.1 pad_maximum_fusion
  20.1 0.1 collective-permute-start.12
  20.1 2.0 %collective-permute-done.2 = bf16[112,896]{1,0:T(8,128)(2,1)S(1)} collective-permute-done((bf16[112,896]{1,0:T(8,128)(2,1)S(1)}, bf16[112,896]{1,0:T(8,128)(2,1)S(1)}, u32[]{:S(2)}, u32[]{:S(2)}) %collective-permute-start.2) | collective-permute-done | bytes 200736 | tf_op jit(solution)/shard_map/ppermute | solution.py:231
  22.1 2.1 %collective-permute-start.5 = (bf16[112,896]{1,0:T(8,128)(2,1)S(1)}, bf16[112,896]{1,0:T(8,128)(2,1)S(1)}, u32[]{:S(2)}, u32[]{:S(2)}) collective-permute-start(bf16[112,896]{1,0:T(8,128)(2,1)S(1)} %collective-permute-done.2), channel_id=1, source_target_pairs={{0,2},{2,4},{4,6},{6,7},{7,5},{5,3},{3,1},{1,0},{10,8},{12,10},{14... | collective-permute-start | bytes 602120 | tf_op jit(solution)/shard_map/ppermute | solution.py:231
  24.2 3.6 %collective-permute-done.5 = bf16[112,896]{1,0:T(8,128)(2,1)S(1)} collective-permute-done((bf16[112,896]{1,0:T(8,128)(2,1)S(1)}, bf16[112,896]{1,0:T(8,128)(2,1)S(1)}, u32[]{:S(2)}, u32[]{:S(2)}) %collective-permute-start.5) | collective-permute-done | bytes 200736 | tf_op jit(solution)/shard_map/ppermute | solution.py:231
  27.8 2.1 %collective-permute-start.8 = (bf16[112,896]{1,0:T(8,128)(2,1)S(1)}, bf16[112,896]{1,0:T(8,128)(2,1)S(1)}, u32[]{:S(2)}, u32[]{:S(2)}) collective-permute-start(bf16[112,896]{1,0:T(8,128)(2,1)S(1)} %collective-permute-done.5), channel_id=1, source_target_pairs={{0,2},{2,4},{4,6},{6,7},{7,5},{5,3},{3,1},{1,0},{10,8},{12,10},{14... | collective-permute-start | bytes 602120 | tf_op jit(solution)/shard_map/ppermute | solution.py:231
  29.9 0.0 collective-permute-start.3
  29.9 1.6 %collective-permute-start.10 = (bf16[112,896]{1,0:T(8,128)(2,1)S(1)}, bf16[112,896]{1,0:T(8,128)(2,1)S(1)}, u32[]{:S(2)}, u32[]{:S(2)}) collective-permute-start(bf16[112,896]{1,0:T(8,128)(2,1)S(1)} %collective-permute-done.7.refs_5_), channel_id=1, source_target_pairs={{0,2},{2,4},{4,6},{6,7},{7,5},{5,3},{3,1},{1,0},{10,8},{12,10},{14... | collective-permute-start | bytes 602120 | tf_op jit(solution)/shard_map/ppermute | solution.py:228
  31.5 0.0 collective-permute-start.6
  31.5 2.1 %collective-permute-done.8 = bf16[112,896]{1,0:T(8,128)(2,1)S(1)} collective-permute-done((bf16[112,896]{1,0:T(8,128)(2,1)S(1)}, bf16[112,896]{1,0:T(8,128)(2,1)S(1)}, u32[]{:S(2)}, u32[]{:S(2)}) %collective-permute-start.8) | collective-permute-done | bytes 200736 | tf_op jit(solution)/shard_map/ppermute | solution.py:231
  33.6 0.0 collective-permute-start.9
  33.6 0.0 collective-permute-done.3.refs_2_
  33.6 2.1 %collective-permute-done.10.refs_7_ = bf16[112,896]{1,0:T(8,128)(2,1)S(1)} collective-permute-done((bf16[112,896]{1,0:T(8,128)(2,1)S(1)}, bf16[112,896]{1,0:T(8,128)(2,1)S(1)}, u32[]{:S(2)}, u32[]{:S(2)}) %collective-permute-start.10) | collective-permute-done | bytes 200736 | tf_op jit(solution)/shard_map/ppermute | solution.py:228
  35.7 0.0 collective-permute-done.6.refs_4_
  35.7 0.0 collective-permute-done.9.refs_6_
  35.7 4.4 %shard_map.93 = (bf16[2,224,896]{2,1,0:T(8,128)(2,1)S(1)}, bf16[2,224,896]{2,1,0:T(8,128)(2,1)S(1)}, bf16[512,896]{1,0:T(8,128)(2,1)S(1)}, f32[512,896]{1,0:T(8,128)S(1)}, bf16[896,896]{1,0:T(8,128)(2,1)S(1)}) custom-call(bf16[112,896]{1,0:T(8,128)(2,1)S(1)} %bitcast_convert_fusion.refs_0_, bf16[112,896]{1,0:T(8,128)(2,1)S(1)} %collective-permute-done.refs_1_, ...), custom_call_target="tpu_custom_call" | custom-call | flops 2466250752 | bytes 5046272 | tf_op jit(solution)/shard_map/pallas_call | solution.py:25
  40.2 0.1 collective-permute-start.23
  40.3 2.3 %shard_map.94 = (bf16[112,896]{1,0:T(8,128)(2,1)S(1)}, bf16[112,896]{1,0:T(8,128)(2,1)S(1)}, bf16[112,896]{1,0:T(8,128)(2,1)S(1)}, bf16[112,896]{1,0:T(8,128)(2,...) custom-call(bf16[512,896]{1,0:T(8,128)(2,1)S(1)} %bitcast.25, ...), custom_call_target="tpu_custom_call" | custom-call | flops 1644167168 | bytes 5275648 | tf_op jit(solution)/shard_map/pallas_call | solution.py:25
  42.6 0.6 collective-permute-start.17
  43.2 2.1 %collective-permute-start.13 = (bf16[112,896]{1,0:T(8,128)(2,1)S(1)}, bf16[112,896]{1,0:T(8,128)(2,1)S(1)}, u32[]{:S(2)}, u32[]{:S(2)}) collective-permute-start(bf16[112,896]{1,0:T(8,128)(2,1)S(1)} %get-tuple-element.31), channel_id=1, source_target_pairs={{0,2},{2,4},{4,6},{6,7},{7,5},{5,3},{3,1},{1,0},{10,8},{12,10},{14... | collective-permute-start | bytes 602120 | tf_op jit(solution)/shard_map/ppermute | solution.py:333
  45.3 0.0 collective-permute-done.23.refs_1_
  45.3 0.2 shard_map.102
  45.5 1.5 %collective-permute-start.24 = (bf16[1,224,896]{2,1,0:T(8,128)(2,1)S(1)}, bf16[1,224,896]{2,1,0:T(8,128)(2,1)S(1)}, u32[]{:S(2)}, u32[]{:S(2)}) collective-permute-start(bf16[1,224,896]{2,1,0:T(8,128)(2,1)S(1)} %get-tuple-element.39), channel_id=1, source_target_pairs={{0,16},{8,24},{16,0},{24,8},{1,17},{9,25},{17,1},{25,9},{2,18},{10... | collective-permute-start | bytes 1204232 | tf_op jit(solution)/shard_map/ppermute | solution.py:321
  47.0 0.0 collective-permute-done.17
  47.1 1.6 %collective-permute-start.18 = (bf16[112,896]{1,0:T(8,128)(2,1)S(1)}, bf16[112,896]{1,0:T(8,128)(2,1)S(1)}, u32[]{:S(2)}, u32[]{:S(2)}) collective-permute-start(bf16[112,896]{1,0:T(8,128)(2,1)S(1)} %get-tuple-element.42), channel_id=1, source_target_pairs={{0,2},{2,4},{4,6},{6,7},{7,5},{5,3},{3,1},{1,0},{10,8},{12,10},{14... | collective-permute-start | bytes 602120 | tf_op jit(solution)/shard_map/ppermute | solution.py:335
  48.7 0.2 collective-permute-done.13.came
  48.9 0.1 shard_map.95
  49.0 2.1 %collective-permute-start.14 = (bf16[112,896]{1,0:T(8,128)(2,1)S(1)}, bf16[112,896]{1,0:T(8,128)(2,1)S(1)}, u32[]{:S(2)}, u32[]{:S(2)}) collective-permute-start(bf16[112,896]{1,0:T(8,128)(2,1)S(1)} %shard_map.95), channel_id=1, source_target_pairs={{0,2},{2,4},{4,6},{6,7},{7,5},{5,3},{3,1},{1,0},{10,8},{12,10},{14... | collective-permute-start | bytes 602120 | tf_op jit(solution)/shard_map/ppermute | solution.py:338
  51.1 1.8 %collective-permute-done.18.came = bf16[112,896]{1,0:T(8,128)(2,1)S(1)} collective-permute-done((bf16[112,896]{1,0:T(8,128)(2,1)S(1)}, bf16[112,896]{1,0:T(8,128)(2,1)S(1)}, u32[]{:S(2)}, u32[]{:S(2)}) %collective-permute-start.18) | collective-permute-done | bytes 200736 | tf_op jit(solution)/shard_map/ppermute | solution.py:335
  52.8 0.1 shard_map.98
  52.9 1.6 %collective-permute-start.19 = (bf16[112,896]{1,0:T(8,128)(2,1)S(1)}, bf16[112,896]{1,0:T(8,128)(2,1)S(1)}, u32[]{:S(2)}, u32[]{:S(2)}) collective-permute-start(bf16[112,896]{1,0:T(8,128)(2,1)S(1)} %shard_map.98), channel_id=1, source_target_pairs={{0,2},{2,4},{4,6},{6,7},{7,5},{5,3},{3,1},{1,0},{10,8},{12,10},{14... | collective-permute-start | bytes 602120 | tf_op jit(solution)/shard_map/ppermute | solution.py:341
  54.5 1.9 %collective-permute-done.24.refs_1_ = bf16[1,224,896]{2,1,0:T(8,128)(2,1)S(1)} collective-permute-done((bf16[1,224,896]{2,1,0:T(8,128)(2,1)S(1)}, bf16[1,224,896]{2,1,0:T(8,128)(2,1)S(1)}, u32[]{:S(2)}, u32[]{:S(2)}) %collective-permute-start.24) | collective-permute-done | bytes 401440 | tf_op jit(solution)/shard_map/ppermute | solution.py:321
  56.5 0.2 shard_map.103
  56.6 0.0 copy-start.2
  56.6 0.0 copy-start.3
  56.7 0.5 collective-permute-start.25
  57.1 0.1 shard_map.101
  57.2 1.7 %collective-permute-start.22 = (bf16[2,128,896]{2,1,0:T(8,128)(2,1)S(1)}, bf16[2,128,896]{2,1,0:T(8,128)(2,1)S(1)}, u32[]{:S(2)}, u32[]{:S(2)}) collective-permute-start(bf16[2,128,896]{2,1,0:T(8,128)(2,1)S(1)} %shard_map.101), channel_id=1, source_target_pairs={{0,2},{1,3},{2,4},{3,5},{4,6},{5,7},{6,0},{7,1},{8,10},{9,11},{10,... | collective-permute-start | bytes 1376264 | tf_op jit(solution)/shard_map/ppermute | solution.py:245
  58.9 0.0 collective-permute-done.14.came
  59.0 1.6 %collective-permute-start.15 = (bf16[112,896]{1,0:T(8,128)(2,1)S(1)}, bf16[112,896]{1,0:T(8,128)(2,1)S(1)}, u32[]{:S(2)}, u32[]{:S(2)}) collective-permute-start(bf16[112,896]{1,0:T(8,128)(2,1)S(1)} %shard_map.96), channel_id=1, source_target_pairs={{0,2},{2,4},{4,6},{6,7},{7,5},{5,3},{3,1},{1,0},{10,8},{12,10},{14... | collective-permute-start | bytes 602120 | tf_op jit(solution)/shard_map/ppermute | solution.py:338
  60.6 0.0 collective-permute-done.19.came
  60.6 0.1 shard_map.99
  60.7 1.5 %collective-permute-start.20 = (bf16[112,896]{1,0:T(8,128)(2,1)S(1)}, bf16[112,896]{1,0:T(8,128)(2,1)S(1)}, u32[]{:S(2)}, u32[]{:S(2)}) collective-permute-start(bf16[112,896]{1,0:T(8,128)(2,1)S(1)} %shard_map.99), channel_id=1, source_target_pairs={{0,2},{2,4},{4,6},{6,7},{7,5},{5,3},{3,1},{1,0},{10,8},{12,10},{14... | collective-permute-start | bytes 602120 | tf_op jit(solution)/shard_map/ppermute | solution.py:341
  62.1 19.9 %collective-permute-done.15.came = bf16[112,896]{1,0:T(8,128)(2,1)S(1)} collective-permute-done((bf16[112,896]{1,0:T(8,128)(2,1)S(1)}, bf16[112,896]{1,0:T(8,128)(2,1)S(1)}, u32[]{:S(2)}, u32[]{:S(2)}) %collective-permute-start.15) | collective-permute-done | bytes 200736 | tf_op jit(solution)/shard_map/ppermute | solution.py:338
  82.0 0.1 shard_map.97
  82.1 2.5 %collective-permute-start.16 = (bf16[112,896]{1,0:T(8,128)(2,1)S(1)}, bf16[112,896]{1,0:T(8,128)(2,1)S(1)}, u32[]{:S(2)}, u32[]{:S(2)}) collective-permute-start(bf16[112,896]{1,0:T(8,128)(2,1)S(1)} %shard_map.97), channel_id=1, source_target_pairs={{0,2},{2,4},{4,6},{6,7},{7,5},{5,3},{3,1},{1,0},{10,8},{12,10},{14... | collective-permute-start | bytes 602120 | tf_op jit(solution)/shard_map/ppermute | solution.py:338
  84.6 0.0 collective-permute-done.20
  84.6 0.5 collective-permute-start.21
  85.1 5.4 %collective-permute-done.16.refs_1_ = bf16[112,896]{1,0:T(8,128)(2,1)S(1)} collective-permute-done((bf16[112,896]{1,0:T(8,128)(2,1)S(1)}, bf16[112,896]{1,0:T(8,128)(2,1)S(1)}, u32[]{:S(2)}, u32[]{:S(2)}) %collective-permute-start.16) | collective-permute-done | bytes 200736 | tf_op jit(solution)/shard_map/ppermute | solution.py:338
  90.5 1.0 %shard_map.100 = (f32[112,896]{1,0:T(8,128)}, f32[112,896]{1,0:T(8,128)}) custom-call(bf16[112,896]{1,0:T(8,128)(2,1)S(1)} %get-tuple-element.27.refs_0_, bf16[112,896]{1,0:T(8,128)(2,1)S(1)} %collective-permute-done.16.refs_1_, bf16[112,896]{1,0:T(8,128)(2,1)S(1)} %collective-permute-done.21.refs_2_, f32[112,896]{1,0:T(8,128)S(1)} %bitcast.21, ...), custom_call_target="tpu_custom_call" | custom-call | bytes 1404928 | tf_op jit(solution)/shard_map/pallas_call | solution.py:25
  91.5 1.3 %shard_map.104 = (f32[224,896]{1,0:T(8,128)}, f32[224,896]{1,0:T(8,128)}) custom-call(bf16[2,128,896]{2,1,0:T(8,128)(2,1)S(1)} %collective-permute-done.22.early, bf16[320,896]{1,0:T(8,128)(2,1)S(1)} %collective-permute-done.25.late), custom_call_target="tpu_custom_call" | custom-call | bytes 1032192 | tf_op jit(solution)/shard_map/pallas_call | solution.py:25
  (16 shorter events, 0.1 us)
Async XLA Ops:
  0.6 35.1 %copy-start.5 = (bf16[1,1,512,896]{3,2,1,0:T(8,128)(2,1)S(1)}, bf16[1,1,512,896]{3,2,1,0:T(8,128)(2,1)}, u32[]{:S(2)}) copy-start(bf16[1,1,512,896]{3,2,1,0:T(8,128)(2,1)} %param.6) | copy-start | bytes 2752516
  0.6 35.1 %copy-start.4 = (bf16[1,1,512,896]{3,2,1,0:T(8,128)(2,1)S(1)}, bf16[1,1,512,896]{3,2,1,0:T(8,128)(2,1)}, u32[]{:S(2)}) copy-start(bf16[1,1,512,896]{3,2,1,0:T(8,128)(2,1)} %param.7) | copy-start | bytes 2752516
  1.8 6.7 %collective-permute-start = (bf16[112,896]{1,0:T(8,128)(2,1)S(1)}, bf16[112,896]{1,0:T(8,128)(2,1)S(1)}, u32[]{:S(2)}, u32[]{:S(2)}) collective-permute-start(bf16[112,896]{1,0:T(8,128)(2,1)S(1)} %bitcast_convert_fusion.refs_0_), channel_id=1, source_target_pairs={{0,2},{2,4},{4,6},{6,7},{7,5},{5,3},{3,1},{1,0},{10,8},{12,10},{14... | collective-permute-start | bytes 602120 | tf_op jit(solution)/shard_map/ppermute | solution.py:228
  6.1 11.8 %collective-permute-start.11 = (bf16[1,224,896]{2,1,0:T(8,128)(2,1)S(1)}, bf16[1,224,896]{2,1,0:T(8,128)(2,1)S(1)}, u32[]{:S(2)}, u32[]{:S(2)}) collective-permute-start(bf16[1,224,896]{2,1,0:T(8,128)(2,1)S(1)} %convert_element_type.8.refs_8_), channel_id=1, source_target_pairs={{0,16},{8,24},{16,0},{24,8},{1,17},{9,25},{17,1},{25,9},{2,18},{10... | collective-permute-start | bytes 1204232 | tf_op jit(solution)/shard_map/ppermute | solution.py:236
  8.6 5.7 %collective-permute-start.4 = (bf16[112,896]{1,0:T(8,128)(2,1)S(1)}, bf16[112,896]{1,0:T(8,128)(2,1)S(1)}, u32[]{:S(2)}, u32[]{:S(2)}) collective-permute-start(bf16[112,896]{1,0:T(8,128)(2,1)S(1)} %collective-permute-done.refs_1_), channel_id=1, source_target_pairs={{0,2},{2,4},{4,6},{6,7},{7,5},{5,3},{3,1},{1,0},{10,8},{12,10},{14... | collective-permute-start | bytes 602120 | tf_op jit(solution)/shard_map/ppermute | solution.py:228
  10.6 5.7 %collective-permute-start.1 = (bf16[112,896]{1,0:T(8,128)(2,1)S(1)}, bf16[112,896]{1,0:T(8,128)(2,1)S(1)}, u32[]{:S(2)}, u32[]{:S(2)}) collective-permute-start(bf16[112,896]{1,0:T(8,128)(2,1)S(1)} %bitcast_convert_fusion.refs_0_), channel_id=1, source_target_pairs={{0,8},{8,0},{16,24},{24,16},{1,9},{9,1},{17,25},{25,17},{2,10},{10... | collective-permute-start | bytes 602120 | tf_op jit(solution)/shard_map/ppermute | solution.py:225
  14.3 5.7 %collective-permute-start.7 = (bf16[112,896]{1,0:T(8,128)(2,1)S(1)}, bf16[112,896]{1,0:T(8,128)(2,1)S(1)}, u32[]{:S(2)}, u32[]{:S(2)}) collective-permute-start(bf16[112,896]{1,0:T(8,128)(2,1)S(1)} %collective-permute-done.4.refs_3_), channel_id=1, source_target_pairs={{0,2},{2,4},{4,6},{6,7},{7,5},{5,3},{3,1},{1,0},{10,8},{12,10},{14... | collective-permute-start | bytes 602120 | tf_op jit(solution)/shard_map/ppermute | solution.py:228
  16.3 5.8 %collective-permute-start.2 = (bf16[112,896]{1,0:T(8,128)(2,1)S(1)}, bf16[112,896]{1,0:T(8,128)(2,1)S(1)}, u32[]{:S(2)}, u32[]{:S(2)}) collective-permute-start(bf16[112,896]{1,0:T(8,128)(2,1)S(1)} %collective-permute-done.1), channel_id=1, source_target_pairs={{0,2},{2,4},{4,6},{6,7},{7,5},{5,3},{3,1},{1,0},{10,8},{12,10},{14... | collective-permute-start | bytes 602120 | tf_op jit(solution)/shard_map/ppermute | solution.py:231
  20.1 15.7 %collective-permute-start.12 = (bf16[2,224,896]{2,1,0:T(8,128)(2,1)S(1)}, bf16[2,224,896]{2,1,0:T(8,128)(2,1)S(1)}, u32[]{:S(2)}, u32[]{:S(2)}) collective-permute-start(bf16[2,224,896]{2,1,0:T(8,128)(2,1)S(1)} %pad_maximum_fusion), channel_id=1, source_target_pairs={{0,8},{8,0},{16,24},{24,16},{1,9},{9,1},{17,25},{25,17},{2,10},{10... | collective-permute-start | bytes 2408456 | tf_op jit(solution)/shard_map/ppermute | solution.py:236
  22.1 5.7 %collective-permute-start.5 = (bf16[112,896]{1,0:T(8,128)(2,1)S(1)}, bf16[112,896]{1,0:T(8,128)(2,1)S(1)}, u32[]{:S(2)}, u32[]{:S(2)}) collective-permute-start(bf16[112,896]{1,0:T(8,128)(2,1)S(1)} %collective-permute-done.2), channel_id=1, source_target_pairs={{0,2},{2,4},{4,6},{6,7},{7,5},{5,3},{3,1},{1,0},{10,8},{12,10},{14... | collective-permute-start | bytes 602120 | tf_op jit(solution)/shard_map/ppermute | solution.py:231
  27.8 5.7 %collective-permute-start.8 = (bf16[112,896]{1,0:T(8,128)(2,1)S(1)}, bf16[112,896]{1,0:T(8,128)(2,1)S(1)}, u32[]{:S(2)}, u32[]{:S(2)}) collective-permute-start(bf16[112,896]{1,0:T(8,128)(2,1)S(1)} %collective-permute-done.5), channel_id=1, source_target_pairs={{0,2},{2,4},{4,6},{6,7},{7,5},{5,3},{3,1},{1,0},{10,8},{12,10},{14... | collective-permute-start | bytes 602120 | tf_op jit(solution)/shard_map/ppermute | solution.py:231
  29.9 3.6 %collective-permute-start.3 = (bf16[112,896]{1,0:T(8,128)(2,1)S(1)}, bf16[112,896]{1,0:T(8,128)(2,1)S(1)}, u32[]{:S(2)}, u32[]{:S(2)}) collective-permute-start(bf16[112,896]{1,0:T(8,128)(2,1)S(1)} %collective-permute-done.2), channel_id=1, source_target_pairs={{0,8},{8,0},{16,24},{24,16},{1,9},{9,1},{17,25},{25,17},{2,10},{10... | collective-permute-start | bytes 602120 | tf_op jit(solution)/shard_map/ppermute | solution.py:232
  29.9 5.8 %collective-permute-start.10 = (bf16[112,896]{1,0:T(8,128)(2,1)S(1)}, bf16[112,896]{1,0:T(8,128)(2,1)S(1)}, u32[]{:S(2)}, u32[]{:S(2)}) collective-permute-start(bf16[112,896]{1,0:T(8,128)(2,1)S(1)} %collective-permute-done.7.refs_5_), channel_id=1, source_target_pairs={{0,2},{2,4},{4,6},{6,7},{7,5},{5,3},{3,1},{1,0},{10,8},{12,10},{14... | collective-permute-start | bytes 602120 | tf_op jit(solution)/shard_map/ppermute | solution.py:228
  31.5 4.2 %collective-permute-start.6 = (bf16[112,896]{1,0:T(8,128)(2,1)S(1)}, bf16[112,896]{1,0:T(8,128)(2,1)S(1)}, u32[]{:S(2)}, u32[]{:S(2)}) collective-permute-start(bf16[112,896]{1,0:T(8,128)(2,1)S(1)} %collective-permute-done.5), channel_id=1, source_target_pairs={{0,8},{8,0},{16,24},{24,16},{1,9},{9,1},{17,25},{25,17},{2,10},{10... | collective-permute-start | bytes 602120 | tf_op jit(solution)/shard_map/ppermute | solution.py:232
  33.6 2.2 %collective-permute-start.9 = (bf16[112,896]{1,0:T(8,128)(2,1)S(1)}, bf16[112,896]{1,0:T(8,128)(2,1)S(1)}, u32[]{:S(2)}, u32[]{:S(2)}) collective-permute-start(bf16[112,896]{1,0:T(8,128)(2,1)S(1)} %collective-permute-done.8), channel_id=1, source_target_pairs={{0,8},{8,0},{16,24},{24,16},{1,9},{9,1},{17,25},{25,17},{2,10},{10... | collective-permute-start | bytes 602120 | tf_op jit(solution)/shard_map/ppermute | solution.py:232
  40.2 5.1 %collective-permute-start.23 = (bf16[2,224,896]{2,1,0:T(8,128)(2,1)S(1)}, bf16[2,224,896]{2,1,0:T(8,128)(2,1)S(1)}, u32[]{:S(2)}, u32[]{:S(2)}) collective-permute-start(bf16[2,224,896]{2,1,0:T(8,128)(2,1)S(1)} %get-tuple-element.37), channel_id=1, source_target_pairs={{0,8},{8,0},{16,24},{24,16},{1,9},{9,1},{17,25},{25,17},{2,10},{10... | collective-permute-start | bytes 2408456 | tf_op jit(solution)/shard_map/ppermute | solution.py:276
  42.6 4.4 %collective-permute-start.17 = (bf16[3,112,896]{2,1,0:T(8,128)(2,1)S(1)}, bf16[3,112,896]{2,1,0:T(8,128)(2,1)S(1)}, u32[]{:S(2)}, u32[]{:S(2)}) collective-permute-start(bf16[3,112,896]{2,1,0:T(8,128)(2,1)S(1)} %get-tuple-element.32), channel_id=1, source_target_pairs={{0,8},{8,0},{16,24},{24,16},{1,9},{9,1},{17,25},{25,17},{2,10},{10... | collective-permute-start | bytes 1806344 | tf_op jit(solution)/shard_map/ppermute | solution.py:334
  43.2 5.7 %collective-permute-start.13 = (bf16[112,896]{1,0:T(8,128)(2,1)S(1)}, bf16[112,896]{1,0:T(8,128)(2,1)S(1)}, u32[]{:S(2)}, u32[]{:S(2)}) collective-permute-start(bf16[112,896]{1,0:T(8,128)(2,1)S(1)} %get-tuple-element.31), channel_id=1, source_target_pairs={{0,2},{2,4},{4,6},{6,7},{7,5},{5,3},{3,1},{1,0},{10,8},{12,10},{14... | collective-permute-start | bytes 602120 | tf_op jit(solution)/shard_map/ppermute | solution.py:333
  45.3 11.2 %copy-start = (f32[1,224,896]{2,1,0:T(8,128)S(1)}, f32[1,224,896]{2,1,0:T(8,128)}, u32[]{:S(2)}) copy-start(f32[1,224,896]{2,1,0:T(8,128)} %param.10) | copy-start | bytes 2408452
  45.3 11.2 %copy-start.1 = (f32[1,224,896]{2,1,0:T(8,128)S(1)}, f32[1,224,896]{2,1,0:T(8,128)}, u32[]{:S(2)}) copy-start(f32[1,224,896]{2,1,0:T(8,128)} %param.11) | copy-start | bytes 2408452
  45.5 11.0 %collective-permute-start.24 = (bf16[1,224,896]{2,1,0:T(8,128)(2,1)S(1)}, bf16[1,224,896]{2,1,0:T(8,128)(2,1)S(1)}, u32[]{:S(2)}, u32[]{:S(2)}) collective-permute-start(bf16[1,224,896]{2,1,0:T(8,128)(2,1)S(1)} %get-tuple-element.39), channel_id=1, source_target_pairs={{0,16},{8,24},{16,0},{24,8},{1,17},{9,25},{17,1},{25,9},{2,18},{10... | collective-permute-start | bytes 1204232 | tf_op jit(solution)/shard_map/ppermute | solution.py:321
  47.1 5.8 %collective-permute-start.18 = (bf16[112,896]{1,0:T(8,128)(2,1)S(1)}, bf16[112,896]{1,0:T(8,128)(2,1)S(1)}, u32[]{:S(2)}, u32[]{:S(2)}) collective-permute-start(bf16[112,896]{1,0:T(8,128)(2,1)S(1)} %get-tuple-element.42), channel_id=1, source_target_pairs={{0,2},{2,4},{4,6},{6,7},{7,5},{5,3},{3,1},{1,0},{10,8},{12,10},{14... | collective-permute-start | bytes 602120 | tf_op jit(solution)/shard_map/ppermute | solution.py:335
  49.0 10.0 %collective-permute-start.14 = (bf16[112,896]{1,0:T(8,128)(2,1)S(1)}, bf16[112,896]{1,0:T(8,128)(2,1)S(1)}, u32[]{:S(2)}, u32[]{:S(2)}) collective-permute-start(bf16[112,896]{1,0:T(8,128)(2,1)S(1)} %shard_map.95), channel_id=1, source_target_pairs={{0,2},{2,4},{4,6},{6,7},{7,5},{5,3},{3,1},{1,0},{10,8},{12,10},{14... | collective-permute-start | bytes 602120 | tf_op jit(solution)/shard_map/ppermute | solution.py:338
  52.9 7.7 %collective-permute-start.19 = (bf16[112,896]{1,0:T(8,128)(2,1)S(1)}, bf16[112,896]{1,0:T(8,128)(2,1)S(1)}, u32[]{:S(2)}, u32[]{:S(2)}) collective-permute-start(bf16[112,896]{1,0:T(8,128)(2,1)S(1)} %shard_map.98), channel_id=1, source_target_pairs={{0,2},{2,4},{4,6},{6,7},{7,5},{5,3},{3,1},{1,0},{10,8},{12,10},{14... | collective-permute-start | bytes 602120 | tf_op jit(solution)/shard_map/ppermute | solution.py:341
  56.6 33.9 %copy-start.2 = (f32[1,112,896]{2,1,0:T(8,128)S(1)}, f32[1,112,896]{2,1,0:T(8,128)}, u32[]{:S(2)}) copy-start(f32[1,112,896]{2,1,0:T(8,128)} %param.8) | copy-start | bytes 1204228
  56.6 33.9 %copy-start.3 = (f32[1,112,896]{2,1,0:T(8,128)S(1)}, f32[1,112,896]{2,1,0:T(8,128)}, u32[]{:S(2)}) copy-start(f32[1,112,896]{2,1,0:T(8,128)} %param.9) | copy-start | bytes 1204228
  56.7 34.9 %collective-permute-start.25 = (bf16[320,896]{1,0:T(8,128)(2,1)S(1)}, bf16[320,896]{1,0:T(8,128)(2,1)S(1)}, u32[]{:S(2)}, u32[]{:S(2)}) collective-permute-start(bf16[320,896]{1,0:T(8,128)(2,1)S(1)} %shard_map.103), channel_id=1, source_target_pairs={{0,2},{1,3},{2,4},{3,5},{4,6},{5,7},{6,0},{7,1},{8,10},{9,11},{10,... | collective-permute-start | bytes 1720328 | tf_op jit(solution)/shard_map/ppermute | solution.py:332
  57.2 34.3 %collective-permute-start.22 = (bf16[2,128,896]{2,1,0:T(8,128)(2,1)S(1)}, bf16[2,128,896]{2,1,0:T(8,128)(2,1)S(1)}, u32[]{:S(2)}, u32[]{:S(2)}) collective-permute-start(bf16[2,128,896]{2,1,0:T(8,128)(2,1)S(1)} %shard_map.101), channel_id=1, source_target_pairs={{0,2},{1,3},{2,4},{3,5},{4,6},{5,7},{6,0},{7,1},{8,10},{9,11},{10,... | collective-permute-start | bytes 1376264 | tf_op jit(solution)/shard_map/ppermute | solution.py:245
  59.0 23.0 %collective-permute-start.15 = (bf16[112,896]{1,0:T(8,128)(2,1)S(1)}, bf16[112,896]{1,0:T(8,128)(2,1)S(1)}, u32[]{:S(2)}, u32[]{:S(2)}) collective-permute-start(bf16[112,896]{1,0:T(8,128)(2,1)S(1)} %shard_map.96), channel_id=1, source_target_pairs={{0,2},{2,4},{4,6},{6,7},{7,5},{5,3},{3,1},{1,0},{10,8},{12,10},{14... | collective-permute-start | bytes 602120 | tf_op jit(solution)/shard_map/ppermute | solution.py:338
  60.7 23.9 %collective-permute-start.20 = (bf16[112,896]{1,0:T(8,128)(2,1)S(1)}, bf16[112,896]{1,0:T(8,128)(2,1)S(1)}, u32[]{:S(2)}, u32[]{:S(2)}) collective-permute-start(bf16[112,896]{1,0:T(8,128)(2,1)S(1)} %shard_map.99), channel_id=1, source_target_pairs={{0,2},{2,4},{4,6},{6,7},{7,5},{5,3},{3,1},{1,0},{10,8},{12,10},{14... | collective-permute-start | bytes 602120 | tf_op jit(solution)/shard_map/ppermute | solution.py:341
  82.1 8.4 %collective-permute-start.16 = (bf16[112,896]{1,0:T(8,128)(2,1)S(1)}, bf16[112,896]{1,0:T(8,128)(2,1)S(1)}, u32[]{:S(2)}, u32[]{:S(2)}) collective-permute-start(bf16[112,896]{1,0:T(8,128)(2,1)S(1)} %shard_map.97), channel_id=1, source_target_pairs={{0,2},{2,4},{4,6},{6,7},{7,5},{5,3},{3,1},{1,0},{10,8},{12,10},{14... | collective-permute-start | bytes 602120 | tf_op jit(solution)/shard_map/ppermute | solution.py:338
  84.6 5.9 %collective-permute-start.21 = (bf16[112,896]{1,0:T(8,128)(2,1)S(1)}, bf16[112,896]{1,0:T(8,128)(2,1)S(1)}, u32[]{:S(2)}, u32[]{:S(2)}) collective-permute-start(bf16[112,896]{1,0:T(8,128)(2,1)S(1)} %collective-permute-done.20), channel_id=1, source_target_pairs={{0,8},{8,0},{16,24},{24,16},{1,9},{9,1},{17,25},{25,17},{2,10},{10... | collective-permute-start | bytes 602120 | tf_op jit(solution)/shard_map/ppermute | solution.py:342

commit v5 on v4

--- a/solution.py
+++ b/solution.py
@@ -12,7 +12,7 @@
 outer_rate = 0.7
 BF16 = jnp.bfloat16
 F32 = jnp.float32
-AHEAD = 5
+AHEAD = 9
 WHOLE = pl.BlockSpec(memory_space=pltpu.VMEM)
 
 
@@ -174,18 +174,15 @@
     late[rows:] = moment_new.astype(BF16)
 
 
-def arrive_kernel(early, late, params_out, moment_out):
-    ahead, rows = early.shape[1], params_out.shape[0]
+def closing_kernel(columns, own, ours, theirs, params, moment, early, late, *outs):
+    params_out, moment_out, second_params, second_moment = outs
+    ahead, rows = early.shape[1], second_params.shape[0]
     grad = late[:ahead].astype(F32)
-    params_out[:ahead] = early[0].astype(F32) - outer_rate * (1 + outer_momentum) * grad
-    moment_out[:ahead] = outer_momentum * early[1].astype(F32) + grad
-    params_out[ahead:] = late[ahead:rows].astype(F32)
-    moment_out[ahead:] = late[rows:].astype(F32)
-
-
-def first_kernel(columns, own, forward, backward, params, moment, params_out, moment_out):
-    total = own[...].astype(F32) + forward[...].astype(F32) + backward[...].astype(F32)
-    grad = total / columns
+    second_params[:ahead] = early[0].astype(F32) - outer_rate * (1 + outer_momentum) * grad
+    second_moment[:ahead] = outer_momentum * early[1].astype(F32) + grad
+    second_params[ahead:] = late[ahead:rows].astype(F32)
+    second_moment[ahead:] = late[rows:].astype(F32)
+    grad = (own[...].astype(F32) + ours[...].astype(F32) + theirs[...].astype(F32)) / columns
     moment_new = outer_momentum * moment[...] + grad
     moment_out[...] = moment_new
     params_out[...] = params[...] - outer_rate * (grad + outer_momentum * moment_new)
@@ -214,7 +211,7 @@
     way = 1 - 2 * (row % 2)
     partner = swap_pairs(n_row, 1)
 
-    ahead = AHEAD * rows2 // 8 // 16 * 16
+    ahead = AHEAD * rows2 // 14 // 16 * 16
     own1 = first_params[0].astype(BF16)
     held = second_params[0].astype(BF16)
     early = call(
@@ -341,25 +338,19 @@
             theirs = lax.ppermute(theirs, ("row", "col"), ring)
     theirs = lax.ppermute(theirs, "row", partner)
 
-    if tiled(rows1):
-        out = shape_of((rows1, width), F32)
-        first_new = call(
-            lambda *refs: first_kernel(columns, *refs),
-            [out, out],
-            [],
-            own_terms[last],
-            ours,
-            theirs,
-            first_params[0],
-            first_moment[0],
-        )
-    else:
-        total = own_terms[last].astype(F32) + ours.astype(F32) + theirs.astype(F32)
-        grad = total / columns
-        moment_new = outer_momentum * first_moment[0] + grad
-        first_new = (first_params[0] - outer_rate * (grad + outer_momentum * moment_new), moment_new)
-    second_new = call(arrive_kernel, [shape_of((rows2, width), F32)] * 2, [], early, late)
-    return (first_new[0][None], first_new[1][None], second_new[0][None], second_new[1][None])
+    news = call(
+        lambda *refs: closing_kernel(columns, *refs),
+        [shape_of((rows1, width), F32)] * 2 + [shape_of((rows2, width), F32)] * 2,
+        [],
+        own_terms[last],
+        ours,
+        theirs,
+        first_params[0],
+        first_moment[0],
+        early,
+        late,
+    )
+    return tuple(new[None] for new in news)
 
 
 def solution(mesh):

time: 93 us -> 92.9 us (level)
    pallas_call x12 -> x11, Pallas kernels: 9.77 us -> 9.06 us  [call(): pl.pallas_call(kernel, out_shape=tuple(outs), in_specs=[WHOLE] * len(oper...]
  transfers between devices with their start and end apart: 26 -> 26, of which waited for: 12 -> 12; matrix products, arithmetic and copies ran while one was open for 1% -> 1% of each run, Pallas kernels for 4% -> 3%
where the time goes in v5:
time: 92.9 us; the launch traced here: 92.7 us
  waiting for transfers between devices  46.2 us (50%)
  starting transfers between devices  34.2 us (37%)
  Pallas kernels  9.06 us (10%)
  other arithmetic  2.42 us (3%)
    ppermute x7, waiting for transfers between devices, per_device(): ours = lax.ppermute(ours, ('row', 'col'), ring)  34.6 us
    ppermute x7, starting transfers between devices, per_device(): ours = lax.ppermute(ours, ('row', 'col'), ring)  15.1 us
    pallas_call x11, Pallas kernels, call(): pl.pallas_call(kernel, out_shape=tuple(outs), in_specs=[WHOLE] * len(oper...  9.06 us
    ppermute x5, starting transfers between devices, per_device(): theirs = lax.ppermute(theirs, ('row', 'col'), ring)  8.8 us
    ppermute x5, waiting for transfers between devices, per_device(): theirs = lax.ppermute(theirs, ('row', 'col'), ring)  7.68 us
    ppermute x1, starting transfers between devices, per_device(): ours = lax.ppermute(own_terms[0], ('row', 'col'), ring)  2.08 us
    ppermute x1, waiting for transfers between devices, per_device(): came = lax.ppermute(away, 'row', swap_pairs(n_row, bit))  1.93 us
  transfers between devices with their start and end apart: 26, of which 12 were waited for; matrix products, arithmetic and copies ran while one was open for 1% of the time, Pallas kernels for 3%

profile of v5, /device:TPU:0, one launch (start us, length us, event | category | flops | bytes accessed | tf_op | source)
XLA Modules:
  0.0 92.7 jit_solution(13742605402449779490)
XLA Ops:
  0.7 1.2 %bitcast_convert_fusion.refs_0_ = bf16[112,896]{1,0:T(8,128)(2,1)S(1)} fusion(f32[1,112,896]{2,1,0:T(8,128)} %param.8), kind=kLoop, calls=%fused_computation.4 | loop fusion | flops 100352 | bytes 602112 | tf_op jit(solution)/shard_map/convert_element_type | solution.py:215
  1.8 3.1 %collective-permute-start = (bf16[112,896]{1,0:T(8,128)(2,1)S(1)}, bf16[112,896]{1,0:T(8,128)(2,1)S(1)}, u32[]{:S(2)}, u32[]{:S(2)}) collective-permute-start(bf16[112,896]{1,0:T(8,128)(2,1)S(1)} %bitcast_convert_fusion.refs_0_), channel_id=1, source_target_pairs={{0,2},{2,4},{4,6},{6,7},{7,5},{5,3},{3,1},{1,0},{10,8},{12,10},{14... | collective-permute-start | bytes 602120 | tf_op jit(solution)/shard_map/ppermute | solution.py:225
  4.9 1.2 %convert_element_type.8.refs_8_ = bf16[1,224,896]{2,1,0:T(8,128)(2,1)S(1)} convert(f32[1,224,896]{2,1,0:T(8,128)} %param.10) | non-fusion elementwise | flops 200704 | bytes 1204224 | tf_op jit(solution)/shard_map/convert_element_type | solution.py:216
  6.1 1.6 %collective-permute-start.11 = (bf16[1,224,896]{2,1,0:T(8,128)(2,1)S(1)}, bf16[1,224,896]{2,1,0:T(8,128)(2,1)S(1)}, u32[]{:S(2)}, u32[]{:S(2)}) collective-permute-start(bf16[1,224,896]{2,1,0:T(8,128)(2,1)S(1)} %convert_element_type.8.refs_8_), channel_id=1, source_target_pairs={{0,16},{8,24},{16,0},{24,8},{1,17},{9,25},{17,1},{25,9},{2,18},{10... | collective-permute-start | bytes 1204232 | tf_op jit(solution)/shard_map/ppermute | solution.py:233
  7.7 0.9 collective-permute-done.refs_1_
  8.6 2.1 %collective-permute-start.4 = (bf16[112,896]{1,0:T(8,128)(2,1)S(1)}, bf16[112,896]{1,0:T(8,128)(2,1)S(1)}, u32[]{:S(2)}, u32[]{:S(2)}) collective-permute-start(bf16[112,896]{1,0:T(8,128)(2,1)S(1)} %collective-permute-done.refs_1_), channel_id=1, source_target_pairs={{0,2},{2,4},{4,6},{6,7},{7,5},{5,3},{3,1},{1,0},{10,8},{12,10},{14... | collective-permute-start | bytes 602120 | tf_op jit(solution)/shard_map/ppermute | solution.py:225
  10.6 0.0 collective-permute-start.1
  10.6 3.6 %collective-permute-done.4.refs_3_ = bf16[112,896]{1,0:T(8,128)(2,1)S(1)} collective-permute-done((bf16[112,896]{1,0:T(8,128)(2,1)S(1)}, bf16[112,896]{1,0:T(8,128)(2,1)S(1)}, u32[]{:S(2)}, u32[]{:S(2)}) %collective-permute-start.4) | collective-permute-done | bytes 200736 | tf_op jit(solution)/shard_map/ppermute | solution.py:225
  14.3 2.1 %collective-permute-start.7 = (bf16[112,896]{1,0:T(8,128)(2,1)S(1)}, bf16[112,896]{1,0:T(8,128)(2,1)S(1)}, u32[]{:S(2)}, u32[]{:S(2)}) collective-permute-start(bf16[112,896]{1,0:T(8,128)(2,1)S(1)} %collective-permute-done.4.refs_3_), channel_id=1, source_target_pairs={{0,2},{2,4},{4,6},{6,7},{7,5},{5,3},{3,1},{1,0},{10,8},{12,10},{14... | collective-permute-start | bytes 602120 | tf_op jit(solution)/shard_map/ppermute | solution.py:225
  16.3 0.0 collective-permute-done.1
  16.3 1.6 %collective-permute-start.2 = (bf16[112,896]{1,0:T(8,128)(2,1)S(1)}, bf16[112,896]{1,0:T(8,128)(2,1)S(1)}, u32[]{:S(2)}, u32[]{:S(2)}) collective-permute-start(bf16[112,896]{1,0:T(8,128)(2,1)S(1)} %collective-permute-done.1), channel_id=1, source_target_pairs={{0,2},{2,4},{4,6},{6,7},{7,5},{5,3},{3,1},{1,0},{10,8},{12,10},{14... | collective-permute-start | bytes 602120 | tf_op jit(solution)/shard_map/ppermute | solution.py:228
  17.9 0.0 collective-permute-done.11.refs_9_
  17.9 2.1 %collective-permute-done.7.refs_5_ = bf16[112,896]{1,0:T(8,128)(2,1)S(1)} collective-permute-done((bf16[112,896]{1,0:T(8,128)(2,1)S(1)}, bf16[112,896]{1,0:T(8,128)(2,1)S(1)}, u32[]{:S(2)}, u32[]{:S(2)}) %collective-permute-start.7) | collective-permute-done | bytes 200736 | tf_op jit(solution)/shard_map/ppermute | solution.py:225
  20.0 0.1 pad_maximum_fusion
  20.1 0.1 collective-permute-start.12
  20.1 2.0 %collective-permute-done.2 = bf16[112,896]{1,0:T(8,128)(2,1)S(1)} collective-permute-done((bf16[112,896]{1,0:T(8,128)(2,1)S(1)}, bf16[112,896]{1,0:T(8,128)(2,1)S(1)}, u32[]{:S(2)}, u32[]{:S(2)}) %collective-permute-start.2) | collective-permute-done | bytes 200736 | tf_op jit(solution)/shard_map/ppermute | solution.py:228
  22.1 2.1 %collective-permute-start.5 = (bf16[112,896]{1,0:T(8,128)(2,1)S(1)}, bf16[112,896]{1,0:T(8,128)(2,1)S(1)}, u32[]{:S(2)}, u32[]{:S(2)}) collective-permute-start(bf16[112,896]{1,0:T(8,128)(2,1)S(1)} %collective-permute-done.2), channel_id=1, source_target_pairs={{0,2},{2,4},{4,6},{6,7},{7,5},{5,3},{3,1},{1,0},{10,8},{12,10},{14... | collective-permute-start | bytes 602120 | tf_op jit(solution)/shard_map/ppermute | solution.py:228
  24.2 3.6 %collective-permute-done.5 = bf16[112,896]{1,0:T(8,128)(2,1)S(1)} collective-permute-done((bf16[112,896]{1,0:T(8,128)(2,1)S(1)}, bf16[112,896]{1,0:T(8,128)(2,1)S(1)}, u32[]{:S(2)}, u32[]{:S(2)}) %collective-permute-start.5) | collective-permute-done | bytes 200736 | tf_op jit(solution)/shard_map/ppermute | solution.py:228
  27.8 2.1 %collective-permute-start.8 = (bf16[112,896]{1,0:T(8,128)(2,1)S(1)}, bf16[112,896]{1,0:T(8,128)(2,1)S(1)}, u32[]{:S(2)}, u32[]{:S(2)}) collective-permute-start(bf16[112,896]{1,0:T(8,128)(2,1)S(1)} %collective-permute-done.5), channel_id=1, source_target_pairs={{0,2},{2,4},{4,6},{6,7},{7,5},{5,3},{3,1},{1,0},{10,8},{12,10},{14... | collective-permute-start | bytes 602120 | tf_op jit(solution)/shard_map/ppermute | solution.py:228
  29.9 0.0 collective-permute-start.3
  29.9 1.6 %collective-permute-start.10 = (bf16[112,896]{1,0:T(8,128)(2,1)S(1)}, bf16[112,896]{1,0:T(8,128)(2,1)S(1)}, u32[]{:S(2)}, u32[]{:S(2)}) collective-permute-start(bf16[112,896]{1,0:T(8,128)(2,1)S(1)} %collective-permute-done.7.refs_5_), channel_id=1, source_target_pairs={{0,2},{2,4},{4,6},{6,7},{7,5},{5,3},{3,1},{1,0},{10,8},{12,10},{14... | collective-permute-start | bytes 602120 | tf_op jit(solution)/shard_map/ppermute | solution.py:225
  31.5 0.0 collective-permute-start.6
  31.5 2.1 %collective-permute-done.8 = bf16[112,896]{1,0:T(8,128)(2,1)S(1)} collective-permute-done((bf16[112,896]{1,0:T(8,128)(2,1)S(1)}, bf16[112,896]{1,0:T(8,128)(2,1)S(1)}, u32[]{:S(2)}, u32[]{:S(2)}) %collective-permute-start.8) | collective-permute-done | bytes 200736 | tf_op jit(solution)/shard_map/ppermute | solution.py:228
  33.6 0.0 collective-permute-start.9
  33.6 0.0 collective-permute-done.3.refs_2_
  33.6 2.1 %collective-permute-done.10.refs_7_ = bf16[112,896]{1,0:T(8,128)(2,1)S(1)} collective-permute-done((bf16[112,896]{1,0:T(8,128)(2,1)S(1)}, bf16[112,896]{1,0:T(8,128)(2,1)S(1)}, u32[]{:S(2)}, u32[]{:S(2)}) %collective-permute-start.10) | collective-permute-done | bytes 200736 | tf_op jit(solution)/shard_map/ppermute | solution.py:225
  35.7 0.0 collective-permute-done.6.refs_4_
  35.7 0.0 collective-permute-done.9.refs_6_
  35.7 0.0 collective-permute-done.12.refs_10_
  35.7 4.4 %shard_map.93 = (bf16[2,224,896]{2,1,0:T(8,128)(2,1)S(1)}, bf16[2,224,896]{2,1,0:T(8,128)(2,1)S(1)}, bf16[512,896]{1,0:T(8,128)(2,1)S(1)}, f32[512,896]{1,0:T(8,128)S(1)}, bf16[896,896]{1,0:T(8,128)(2,1)S(1)}) custom-call(bf16[112,896]{1,0:T(8,128)(2,1)S(1)} %bitcast_convert_fusion.refs_0_, bf16[112,896]{1,0:T(8,128)(2,1)S(1)} %collective-permute-done.refs_1_, ...), custom_call_target="tpu_custom_call" | custom-call | flops 2466250752 | bytes 5046272 | tf_op jit(solution)/shard_map/pallas_call | solution.py:25
  40.2 0.1 collective-permute-start.23
  40.3 2.3 %shard_map.94 = (bf16[112,896]{1,0:T(8,128)(2,1)S(1)}, bf16[112,896]{1,0:T(8,128)(2,1)S(1)}, bf16[112,896]{1,0:T(8,128)(2,1)S(1)}, bf16[112,896]{1,0:T(8,128)(2,...) custom-call(bf16[512,896]{1,0:T(8,128)(2,1)S(1)} %bitcast.25, ...), custom_call_target="tpu_custom_call" | custom-call | flops 1644167168 | bytes 5275648 | tf_op jit(solution)/shard_map/pallas_call | solution.py:25
  42.6 0.6 collective-permute-start.17
  43.2 2.1 %collective-permute-start.13 = (bf16[112,896]{1,0:T(8,128)(2,1)S(1)}, bf16[112,896]{1,0:T(8,128)(2,1)S(1)}, u32[]{:S(2)}, u32[]{:S(2)}) collective-permute-start(bf16[112,896]{1,0:T(8,128)(2,1)S(1)} %get-tuple-element.31), channel_id=1, source_target_pairs={{0,2},{2,4},{4,6},{6,7},{7,5},{5,3},{3,1},{1,0},{10,8},{12,10},{14... | collective-permute-start | bytes 602120 | tf_op jit(solution)/shard_map/ppermute | solution.py:330
  45.3 0.0 collective-permute-done.23.refs_1_
  45.3 0.2 shard_map.101
  45.5 1.5 %collective-permute-start.24 = (bf16[1,224,896]{2,1,0:T(8,128)(2,1)S(1)}, bf16[1,224,896]{2,1,0:T(8,128)(2,1)S(1)}, u32[]{:S(2)}, u32[]{:S(2)}) collective-permute-start(bf16[1,224,896]{2,1,0:T(8,128)(2,1)S(1)} %get-tuple-element.37), channel_id=1, source_target_pairs={{0,16},{8,24},{16,0},{24,8},{1,17},{9,25},{17,1},{25,9},{2,18},{10... | collective-permute-start | bytes 1204232 | tf_op jit(solution)/shard_map/ppermute | solution.py:318
  47.0 0.0 collective-permute-done.17
  47.1 1.6 %collective-permute-start.18 = (bf16[112,896]{1,0:T(8,128)(2,1)S(1)}, bf16[112,896]{1,0:T(8,128)(2,1)S(1)}, u32[]{:S(2)}, u32[]{:S(2)}) collective-permute-start(bf16[112,896]{1,0:T(8,128)(2,1)S(1)} %get-tuple-element.42), channel_id=1, source_target_pairs={{0,2},{2,4},{4,6},{6,7},{7,5},{5,3},{3,1},{1,0},{10,8},{12,10},{14... | collective-permute-start | bytes 602120 | tf_op jit(solution)/shard_map/ppermute | solution.py:332
  48.7 0.2 collective-permute-done.13.came
  48.9 0.1 shard_map.95
  49.0 2.1 %collective-permute-start.14 = (bf16[112,896]{1,0:T(8,128)(2,1)S(1)}, bf16[112,896]{1,0:T(8,128)(2,1)S(1)}, u32[]{:S(2)}, u32[]{:S(2)}) collective-permute-start(bf16[112,896]{1,0:T(8,128)(2,1)S(1)} %shard_map.95), channel_id=1, source_target_pairs={{0,2},{2,4},{4,6},{6,7},{7,5},{5,3},{3,1},{1,0},{10,8},{12,10},{14... | collective-permute-start | bytes 602120 | tf_op jit(solution)/shard_map/ppermute | solution.py:335
  51.1 1.7 %collective-permute-done.18.came = bf16[112,896]{1,0:T(8,128)(2,1)S(1)} collective-permute-done((bf16[112,896]{1,0:T(8,128)(2,1)S(1)}, bf16[112,896]{1,0:T(8,128)(2,1)S(1)}, u32[]{:S(2)}, u32[]{:S(2)}) %collective-permute-start.18) | collective-permute-done | bytes 200736 | tf_op jit(solution)/shard_map/ppermute | solution.py:332
  52.8 0.1 shard_map.98
  52.9 1.6 %collective-permute-start.19 = (bf16[112,896]{1,0:T(8,128)(2,1)S(1)}, bf16[112,896]{1,0:T(8,128)(2,1)S(1)}, u32[]{:S(2)}, u32[]{:S(2)}) collective-permute-start(bf16[112,896]{1,0:T(8,128)(2,1)S(1)} %shard_map.98), channel_id=1, source_target_pairs={{0,2},{2,4},{4,6},{6,7},{7,5},{5,3},{3,1},{1,0},{10,8},{12,10},{14... | collective-permute-start | bytes 602120 | tf_op jit(solution)/shard_map/ppermute | solution.py:338
  54.5 1.9 %collective-permute-done.24.refs_1_ = bf16[1,224,896]{2,1,0:T(8,128)(2,1)S(1)} collective-permute-done((bf16[1,224,896]{2,1,0:T(8,128)(2,1)S(1)}, bf16[1,224,896]{2,1,0:T(8,128)(2,1)S(1)}, u32[]{:S(2)}, u32[]{:S(2)}) %collective-permute-start.24) | collective-permute-done | bytes 401440 | tf_op jit(solution)/shard_map/ppermute | solution.py:318
  56.5 0.2 shard_map.102
  56.6 0.0 copy-start.2
  56.7 0.0 copy-start.3
  56.7 0.5 collective-permute-start.25
  57.1 0.1 shard_map.100
  57.2 1.7 %collective-permute-start.22 = (bf16[2,144,896]{2,1,0:T(8,128)(2,1)S(1)}, bf16[2,144,896]{2,1,0:T(8,128)(2,1)S(1)}, u32[]{:S(2)}, u32[]{:S(2)}) collective-permute-start(bf16[2,144,896]{2,1,0:T(8,128)(2,1)S(1)} %shard_map.100), channel_id=1, source_target_pairs={{0,2},{1,3},{2,4},{3,5},{4,6},{5,7},{6,0},{7,1},{8,10},{9,11},{10,... | collective-permute-start | bytes 1548296 | tf_op jit(solution)/shard_map/ppermute | solution.py:242
  58.9 0.1 shard_map.96
  59.0 1.6 %collective-permute-start.15 = (bf16[112,896]{1,0:T(8,128)(2,1)S(1)}, bf16[112,896]{1,0:T(8,128)(2,1)S(1)}, u32[]{:S(2)}, u32[]{:S(2)}) collective-permute-start(bf16[112,896]{1,0:T(8,128)(2,1)S(1)} %shard_map.96), channel_id=1, source_target_pairs={{0,2},{2,4},{4,6},{6,7},{7,5},{5,3},{3,1},{1,0},{10,8},{12,10},{14... | collective-permute-start | bytes 602120 | tf_op jit(solution)/shard_map/ppermute | solution.py:335
  60.6 0.0 collective-permute-done.19.came
  60.6 0.1 shard_map.99
  60.7 1.4 %collective-permute-start.20 = (bf16[112,896]{1,0:T(8,128)(2,1)S(1)}, bf16[112,896]{1,0:T(8,128)(2,1)S(1)}, u32[]{:S(2)}, u32[]{:S(2)}) collective-permute-start(bf16[112,896]{1,0:T(8,128)(2,1)S(1)} %shard_map.99), channel_id=1, source_target_pairs={{0,2},{2,4},{4,6},{6,7},{7,5},{5,3},{3,1},{1,0},{10,8},{12,10},{14... | collective-permute-start | bytes 602120 | tf_op jit(solution)/shard_map/ppermute | solution.py:338
  62.1 20.5 %collective-permute-done.15.came = bf16[112,896]{1,0:T(8,128)(2,1)S(1)} collective-permute-done((bf16[112,896]{1,0:T(8,128)(2,1)S(1)}, bf16[112,896]{1,0:T(8,128)(2,1)S(1)}, u32[]{:S(2)}, u32[]{:S(2)}) %collective-permute-start.15) | collective-permute-done | bytes 200736 | tf_op jit(solution)/shard_map/ppermute | solution.py:335
  82.6 0.1 shard_map.97
  82.7 2.5 %collective-permute-start.16 = (bf16[112,896]{1,0:T(8,128)(2,1)S(1)}, bf16[112,896]{1,0:T(8,128)(2,1)S(1)}, u32[]{:S(2)}, u32[]{:S(2)}) collective-permute-start(bf16[112,896]{1,0:T(8,128)(2,1)S(1)} %shard_map.97), channel_id=1, source_target_pairs={{0,2},{2,4},{4,6},{6,7},{7,5},{5,3},{3,1},{1,0},{10,8},{12,10},{14... | collective-permute-start | bytes 602120 | tf_op jit(solution)/shard_map/ppermute | solution.py:335
  85.2 0.5 collective-permute-start.21
  85.7 0.0 collective-permute-done.22.refs_5_
  85.7 5.4 %collective-permute-done.16.refs_1_ = bf16[112,896]{1,0:T(8,128)(2,1)S(1)} collective-permute-done((bf16[112,896]{1,0:T(8,128)(2,1)S(1)}, bf16[112,896]{1,0:T(8,128)(2,1)S(1)}, u32[]{:S(2)}, u32[]{:S(2)}) %collective-permute-start.16) | collective-permute-done | bytes 200736 | tf_op jit(solution)/shard_map/ppermute | solution.py:335
  91.2 1.6 %shard_map.103 = (f32[112,896]{1,0:T(8,128)}, f32[112,896]{1,0:T(8,128)}, f32[224,896]{1,0:T(8,128)}, f32[224,896]{1,0:T(8,128)}) custom-call(bf16[112,896]{1,0:T(8,128)(2,1)S(1)} %get-tuple-element.27.refs_0_, bf16[112,896]{1,0:T(8,128)(2,1)S(1)} %collective-permute-done.16.refs_1_, bf16[112,896]{1,0:T(8,128)(2,1)S(1)} %collective-permute-done.21.refs_2_, ...), custom_call_target="tpu_custom_call" | custom-call | bytes 2465792 | tf_op jit(solution)/shard_map/pallas_call | solution.py:25
  (15 shorter events, 0.1 us)
Async XLA Ops:
  0.6 35.1 %copy-start.5 = (bf16[1,1,512,896]{3,2,1,0:T(8,128)(2,1)S(1)}, bf16[1,1,512,896]{3,2,1,0:T(8,128)(2,1)}, u32[]{:S(2)}) copy-start(bf16[1,1,512,896]{3,2,1,0:T(8,128)(2,1)} %param.6) | copy-start | bytes 2752516
  0.6 35.1 %copy-start.4 = (bf16[1,1,512,896]{3,2,1,0:T(8,128)(2,1)S(1)}, bf16[1,1,512,896]{3,2,1,0:T(8,128)(2,1)}, u32[]{:S(2)}) copy-start(bf16[1,1,512,896]{3,2,1,0:T(8,128)(2,1)} %param.7) | copy-start | bytes 2752516
  1.8 6.7 %collective-permute-start = (bf16[112,896]{1,0:T(8,128)(2,1)S(1)}, bf16[112,896]{1,0:T(8,128)(2,1)S(1)}, u32[]{:S(2)}, u32[]{:S(2)}) collective-permute-start(bf16[112,896]{1,0:T(8,128)(2,1)S(1)} %bitcast_convert_fusion.refs_0_), channel_id=1, source_target_pairs={{0,2},{2,4},{4,6},{6,7},{7,5},{5,3},{3,1},{1,0},{10,8},{12,10},{14... | collective-permute-start | bytes 602120 | tf_op jit(solution)/shard_map/ppermute | solution.py:225
  6.1 11.8 %collective-permute-start.11 = (bf16[1,224,896]{2,1,0:T(8,128)(2,1)S(1)}, bf16[1,224,896]{2,1,0:T(8,128)(2,1)S(1)}, u32[]{:S(2)}, u32[]{:S(2)}) collective-permute-start(bf16[1,224,896]{2,1,0:T(8,128)(2,1)S(1)} %convert_element_type.8.refs_8_), channel_id=1, source_target_pairs={{0,16},{8,24},{16,0},{24,8},{1,17},{9,25},{17,1},{25,9},{2,18},{10... | collective-permute-start | bytes 1204232 | tf_op jit(solution)/shard_map/ppermute | solution.py:233
  8.6 5.7 %collective-permute-start.4 = (bf16[112,896]{1,0:T(8,128)(2,1)S(1)}, bf16[112,896]{1,0:T(8,128)(2,1)S(1)}, u32[]{:S(2)}, u32[]{:S(2)}) collective-permute-start(bf16[112,896]{1,0:T(8,128)(2,1)S(1)} %collective-permute-done.refs_1_), channel_id=1, source_target_pairs={{0,2},{2,4},{4,6},{6,7},{7,5},{5,3},{3,1},{1,0},{10,8},{12,10},{14... | collective-permute-start | bytes 602120 | tf_op jit(solution)/shard_map/ppermute | solution.py:225
  10.6 5.7 %collective-permute-start.1 = (bf16[112,896]{1,0:T(8,128)(2,1)S(1)}, bf16[112,896]{1,0:T(8,128)(2,1)S(1)}, u32[]{:S(2)}, u32[]{:S(2)}) collective-permute-start(bf16[112,896]{1,0:T(8,128)(2,1)S(1)} %bitcast_convert_fusion.refs_0_), channel_id=1, source_target_pairs={{0,8},{8,0},{16,24},{24,16},{1,9},{9,1},{17,25},{25,17},{2,10},{10... | collective-permute-start | bytes 602120 | tf_op jit(solution)/shard_map/ppermute | solution.py:222
  14.3 5.7 %collective-permute-start.7 = (bf16[112,896]{1,0:T(8,128)(2,1)S(1)}, bf16[112,896]{1,0:T(8,128)(2,1)S(1)}, u32[]{:S(2)}, u32[]{:S(2)}) collective-permute-start(bf16[112,896]{1,0:T(8,128)(2,1)S(1)} %collective-permute-done.4.refs_3_), channel_id=1, source_target_pairs={{0,2},{2,4},{4,6},{6,7},{7,5},{5,3},{3,1},{1,0},{10,8},{12,10},{14... | collective-permute-start | bytes 602120 | tf_op jit(solution)/shard_map/ppermute | solution.py:225
  16.3 5.8 %collective-permute-start.2 = (bf16[112,896]{1,0:T(8,128)(2,1)S(1)}, bf16[112,896]{1,0:T(8,128)(2,1)S(1)}, u32[]{:S(2)}, u32[]{:S(2)}) collective-permute-start(bf16[112,896]{1,0:T(8,128)(2,1)S(1)} %collective-permute-done.1), channel_id=1, source_target_pairs={{0,2},{2,4},{4,6},{6,7},{7,5},{5,3},{3,1},{1,0},{10,8},{12,10},{14... | collective-permute-start | bytes 602120 | tf_op jit(solution)/shard_map/ppermute | solution.py:228
  20.1 15.7 %collective-permute-start.12 = (bf16[2,224,896]{2,1,0:T(8,128)(2,1)S(1)}, bf16[2,224,896]{2,1,0:T(8,128)(2,1)S(1)}, u32[]{:S(2)}, u32[]{:S(2)}) collective-permute-start(bf16[2,224,896]{2,1,0:T(8,128)(2,1)S(1)} %pad_maximum_fusion), channel_id=1, source_target_pairs={{0,8},{8,0},{16,24},{24,16},{1,9},{9,1},{17,25},{25,17},{2,10},{10... | collective-permute-start | bytes 2408456 | tf_op jit(solution)/shard_map/ppermute | solution.py:233
  22.1 5.7 %collective-permute-start.5 = (bf16[112,896]{1,0:T(8,128)(2,1)S(1)}, bf16[112,896]{1,0:T(8,128)(2,1)S(1)}, u32[]{:S(2)}, u32[]{:S(2)}) collective-permute-start(bf16[112,896]{1,0:T(8,128)(2,1)S(1)} %collective-permute-done.2), channel_id=1, source_target_pairs={{0,2},{2,4},{4,6},{6,7},{7,5},{5,3},{3,1},{1,0},{10,8},{12,10},{14... | collective-permute-start | bytes 602120 | tf_op jit(solution)/shard_map/ppermute | solution.py:228
  27.8 5.7 %collective-permute-start.8 = (bf16[112,896]{1,0:T(8,128)(2,1)S(1)}, bf16[112,896]{1,0:T(8,128)(2,1)S(1)}, u32[]{:S(2)}, u32[]{:S(2)}) collective-permute-start(bf16[112,896]{1,0:T(8,128)(2,1)S(1)} %collective-permute-done.5), channel_id=1, source_target_pairs={{0,2},{2,4},{4,6},{6,7},{7,5},{5,3},{3,1},{1,0},{10,8},{12,10},{14... | collective-permute-start | bytes 602120 | tf_op jit(solution)/shard_map/ppermute | solution.py:228
  29.9 3.6 %collective-permute-start.3 = (bf16[112,896]{1,0:T(8,128)(2,1)S(1)}, bf16[112,896]{1,0:T(8,128)(2,1)S(1)}, u32[]{:S(2)}, u32[]{:S(2)}) collective-permute-start(bf16[112,896]{1,0:T(8,128)(2,1)S(1)} %collective-permute-done.2), channel_id=1, source_target_pairs={{0,8},{8,0},{16,24},{24,16},{1,9},{9,1},{17,25},{25,17},{2,10},{10... | collective-permute-start | bytes 602120 | tf_op jit(solution)/shard_map/ppermute | solution.py:229
  29.9 5.8 %collective-permute-start.10 = (bf16[112,896]{1,0:T(8,128)(2,1)S(1)}, bf16[112,896]{1,0:T(8,128)(2,1)S(1)}, u32[]{:S(2)}, u32[]{:S(2)}) collective-permute-start(bf16[112,896]{1,0:T(8,128)(2,1)S(1)} %collective-permute-done.7.refs_5_), channel_id=1, source_target_pairs={{0,2},{2,4},{4,6},{6,7},{7,5},{5,3},{3,1},{1,0},{10,8},{12,10},{14... | collective-permute-start | bytes 602120 | tf_op jit(solution)/shard_map/ppermute | solution.py:225
  31.5 4.2 %collective-permute-start.6 = (bf16[112,896]{1,0:T(8,128)(2,1)S(1)}, bf16[112,896]{1,0:T(8,128)(2,1)S(1)}, u32[]{:S(2)}, u32[]{:S(2)}) collective-permute-start(bf16[112,896]{1,0:T(8,128)(2,1)S(1)} %collective-permute-done.5), channel_id=1, source_target_pairs={{0,8},{8,0},{16,24},{24,16},{1,9},{9,1},{17,25},{25,17},{2,10},{10... | collective-permute-start | bytes 602120 | tf_op jit(solution)/shard_map/ppermute | solution.py:229
  33.6 2.2 %collective-permute-start.9 = (bf16[112,896]{1,0:T(8,128)(2,1)S(1)}, bf16[112,896]{1,0:T(8,128)(2,1)S(1)}, u32[]{:S(2)}, u32[]{:S(2)}) collective-permute-start(bf16[112,896]{1,0:T(8,128)(2,1)S(1)} %collective-permute-done.8), channel_id=1, source_target_pairs={{0,8},{8,0},{16,24},{24,16},{1,9},{9,1},{17,25},{25,17},{2,10},{10... | collective-permute-start | bytes 602120 | tf_op jit(solution)/shard_map/ppermute | solution.py:229
  40.2 5.1 %collective-permute-start.23 = (bf16[2,224,896]{2,1,0:T(8,128)(2,1)S(1)}, bf16[2,224,896]{2,1,0:T(8,128)(2,1)S(1)}, u32[]{:S(2)}, u32[]{:S(2)}) collective-permute-start(bf16[2,224,896]{2,1,0:T(8,128)(2,1)S(1)} %get-tuple-element.35), channel_id=1, source_target_pairs={{0,8},{8,0},{16,24},{24,16},{1,9},{9,1},{17,25},{25,17},{2,10},{10... | collective-permute-start | bytes 2408456 | tf_op jit(solution)/shard_map/ppermute | solution.py:273
  42.6 4.4 %collective-permute-start.17 = (bf16[3,112,896]{2,1,0:T(8,128)(2,1)S(1)}, bf16[3,112,896]{2,1,0:T(8,128)(2,1)S(1)}, u32[]{:S(2)}, u32[]{:S(2)}) collective-permute-start(bf16[3,112,896]{2,1,0:T(8,128)(2,1)S(1)} %get-tuple-element.32), channel_id=1, source_target_pairs={{0,8},{8,0},{16,24},{24,16},{1,9},{9,1},{17,25},{25,17},{2,10},{10... | collective-permute-start | bytes 1806344 | tf_op jit(solution)/shard_map/ppermute | solution.py:331
  43.2 5.7 %collective-permute-start.13 = (bf16[112,896]{1,0:T(8,128)(2,1)S(1)}, bf16[112,896]{1,0:T(8,128)(2,1)S(1)}, u32[]{:S(2)}, u32[]{:S(2)}) collective-permute-start(bf16[112,896]{1,0:T(8,128)(2,1)S(1)} %get-tuple-element.31), channel_id=1, source_target_pairs={{0,2},{2,4},{4,6},{6,7},{7,5},{5,3},{3,1},{1,0},{10,8},{12,10},{14... | collective-permute-start | bytes 602120 | tf_op jit(solution)/shard_map/ppermute | solution.py:330
  45.3 11.2 %copy-start = (f32[1,224,896]{2,1,0:T(8,128)S(1)}, f32[1,224,896]{2,1,0:T(8,128)}, u32[]{:S(2)}) copy-start(f32[1,224,896]{2,1,0:T(8,128)} %param.10) | copy-start | bytes 2408452
  45.3 11.2 %copy-start.1 = (f32[1,224,896]{2,1,0:T(8,128)S(1)}, f32[1,224,896]{2,1,0:T(8,128)}, u32[]{:S(2)}) copy-start(f32[1,224,896]{2,1,0:T(8,128)} %param.11) | copy-start | bytes 2408452
  45.5 11.0 %collective-permute-start.24 = (bf16[1,224,896]{2,1,0:T(8,128)(2,1)S(1)}, bf16[1,224,896]{2,1,0:T(8,128)(2,1)S(1)}, u32[]{:S(2)}, u32[]{:S(2)}) collective-permute-start(bf16[1,224,896]{2,1,0:T(8,128)(2,1)S(1)} %get-tuple-element.37), channel_id=1, source_target_pairs={{0,16},{8,24},{16,0},{24,8},{1,17},{9,25},{17,1},{25,9},{2,18},{10... | collective-permute-start | bytes 1204232 | tf_op jit(solution)/shard_map/ppermute | solution.py:318
  47.1 5.8 %collective-permute-start.18 = (bf16[112,896]{1,0:T(8,128)(2,1)S(1)}, bf16[112,896]{1,0:T(8,128)(2,1)S(1)}, u32[]{:S(2)}, u32[]{:S(2)}) collective-permute-start(bf16[112,896]{1,0:T(8,128)(2,1)S(1)} %get-tuple-element.42), channel_id=1, source_target_pairs={{0,2},{2,4},{4,6},{6,7},{7,5},{5,3},{3,1},{1,0},{10,8},{12,10},{14... | collective-permute-start | bytes 602120 | tf_op jit(solution)/shard_map/ppermute | solution.py:332
  49.0 10.0 %collective-permute-start.14 = (bf16[112,896]{1,0:T(8,128)(2,1)S(1)}, bf16[112,896]{1,0:T(8,128)(2,1)S(1)}, u32[]{:S(2)}, u32[]{:S(2)}) collective-permute-start(bf16[112,896]{1,0:T(8,128)(2,1)S(1)} %shard_map.95), channel_id=1, source_target_pairs={{0,2},{2,4},{4,6},{6,7},{7,5},{5,3},{3,1},{1,0},{10,8},{12,10},{14... | collective-permute-start | bytes 602120 | tf_op jit(solution)/shard_map/ppermute | solution.py:335
  52.9 7.7 %collective-permute-start.19 = (bf16[112,896]{1,0:T(8,128)(2,1)S(1)}, bf16[112,896]{1,0:T(8,128)(2,1)S(1)}, u32[]{:S(2)}, u32[]{:S(2)}) collective-permute-start(bf16[112,896]{1,0:T(8,128)(2,1)S(1)} %shard_map.98), channel_id=1, source_target_pairs={{0,2},{2,4},{4,6},{6,7},{7,5},{5,3},{3,1},{1,0},{10,8},{12,10},{14... | collective-permute-start | bytes 602120 | tf_op jit(solution)/shard_map/ppermute | solution.py:338
  56.6 34.5 %copy-start.2 = (f32[1,112,896]{2,1,0:T(8,128)S(1)}, f32[1,112,896]{2,1,0:T(8,128)}, u32[]{:S(2)}) copy-start(f32[1,112,896]{2,1,0:T(8,128)} %param.8) | copy-start | bytes 1204228
  56.7 34.5 %copy-start.3 = (f32[1,112,896]{2,1,0:T(8,128)S(1)}, f32[1,112,896]{2,1,0:T(8,128)}, u32[]{:S(2)}) copy-start(f32[1,112,896]{2,1,0:T(8,128)} %param.9) | copy-start | bytes 1204228
  56.7 34.5 %collective-permute-start.25 = (bf16[304,896]{1,0:T(8,128)(2,1)S(1)}, bf16[304,896]{1,0:T(8,128)(2,1)S(1)}, u32[]{:S(2)}, u32[]{:S(2)}) collective-permute-start(bf16[304,896]{1,0:T(8,128)(2,1)S(1)} %shard_map.102), channel_id=1, source_target_pairs={{0,2},{1,3},{2,4},{3,5},{4,6},{5,7},{6,0},{7,1},{8,10},{9,11},{10,... | collective-permute-start | bytes 1634312 | tf_op jit(solution)/shard_map/ppermute | solution.py:329
  57.2 28.5 %collective-permute-start.22 = (bf16[2,144,896]{2,1,0:T(8,128)(2,1)S(1)}, bf16[2,144,896]{2,1,0:T(8,128)(2,1)S(1)}, u32[]{:S(2)}, u32[]{:S(2)}) collective-permute-start(bf16[2,144,896]{2,1,0:T(8,128)(2,1)S(1)} %shard_map.100), channel_id=1, source_target_pairs={{0,2},{1,3},{2,4},{3,5},{4,6},{5,7},{6,0},{7,1},{8,10},{9,11},{10,... | collective-permute-start | bytes 1548296 | tf_op jit(solution)/shard_map/ppermute | solution.py:242
  59.0 23.6 %collective-permute-start.15 = (bf16[112,896]{1,0:T(8,128)(2,1)S(1)}, bf16[112,896]{1,0:T(8,128)(2,1)S(1)}, u32[]{:S(2)}, u32[]{:S(2)}) collective-permute-start(bf16[112,896]{1,0:T(8,128)(2,1)S(1)} %shard_map.96), channel_id=1, source_target_pairs={{0,2},{2,4},{4,6},{6,7},{7,5},{5,3},{3,1},{1,0},{10,8},{12,10},{14... | collective-permute-start | bytes 602120 | tf_op jit(solution)/shard_map/ppermute | solution.py:335
  60.7 24.5 %collective-permute-start.20 = (bf16[112,896]{1,0:T(8,128)(2,1)S(1)}, bf16[112,896]{1,0:T(8,128)(2,1)S(1)}, u32[]{:S(2)}, u32[]{:S(2)}) collective-permute-start(bf16[112,896]{1,0:T(8,128)(2,1)S(1)} %shard_map.99), channel_id=1, source_target_pairs={{0,2},{2,4},{4,6},{6,7},{7,5},{5,3},{3,1},{1,0},{10,8},{12,10},{14... | collective-permute-start | bytes 602120 | tf_op jit(solution)/shard_map/ppermute | solution.py:338
  82.7 8.4 %collective-permute-start.16 = (bf16[112,896]{1,0:T(8,128)(2,1)S(1)}, bf16[112,896]{1,0:T(8,128)(2,1)S(1)}, u32[]{:S(2)}, u32[]{:S(2)}) collective-permute-start(bf16[112,896]{1,0:T(8,128)(2,1)S(1)} %shard_map.97), channel_id=1, source_target_pairs={{0,2},{2,4},{4,6},{6,7},{7,5},{5,3},{3,1},{1,0},{10,8},{12,10},{14... | collective-permute-start | bytes 602120 | tf_op jit(solution)/shard_map/ppermute | solution.py:335
  85.2 5.9 %collective-permute-start.21 = (bf16[112,896]{1,0:T(8,128)(2,1)S(1)}, bf16[112,896]{1,0:T(8,128)(2,1)S(1)}, u32[]{:S(2)}, u32[]{:S(2)}) collective-permute-start(bf16[112,896]{1,0:T(8,128)(2,1)S(1)} %collective-permute-done.20), channel_id=1, source_target_pairs={{0,8},{8,0},{16,24},{24,16},{1,9},{9,1},{17,25},{25,17},{2,10},{10... | collective-permute-start | bytes 602120 | tf_op jit(solution)/shard_map/ppermute | solution.py:339

commit v6 on v5

--- a/solution.py
+++ b/solution.py
@@ -12,7 +12,7 @@
 outer_rate = 0.7
 BF16 = jnp.bfloat16
 F32 = jnp.float32
-AHEAD = 9
+AHEAD = 8
 WHOLE = pl.BlockSpec(memory_space=pltpu.VMEM)
 
 
@@ -106,11 +106,14 @@
             rows = ref.shape[1]
             for k, flip in enumerate(flips):
                 second_ref[pl.ds(pl.multiple_of((row ^ flip) * rows, rows), rows), :] = ref[k]
-    pre = jnp.dot(inputs[...], first_full[...], preferred_element_type=F32)
-    value, slope = gelu_and_slope(pre)
-    active[...] = value.astype(BF16)
-    slope_ref[...] = slope
-    output = jnp.dot(active[...], second_ref[...], preferred_element_type=F32)
+    cut = width // 2 // 128 * 128
+    output = 0.0
+    for some in (slice(0, cut), slice(cut, width)):
+        pre = jnp.dot(inputs[...], first_full[:, some], preferred_element_type=F32)
+        value, slope = gelu_and_slope(pre)
+        active[:, some] = value.astype(BF16)
+        slope_ref[:, some] = slope
+        output += jnp.dot(active[:, some], second_ref[some, :], preferred_element_type=F32)
     error = ((output - wanted[...].astype(F32)) / tokens).astype(BF16)
     error_ref[...] = error
     grad[...] = lax.dot_general(
@@ -174,14 +177,16 @@
     late[rows:] = moment_new.astype(BF16)
 
 
-def closing_kernel(columns, own, ours, theirs, params, moment, early, late, *outs):
-    params_out, moment_out, second_params, second_moment = outs
-    ahead, rows = early.shape[1], second_params.shape[0]
+def arrive_kernel(early, late, params_out, moment_out):
+    ahead, rows = early.shape[1], params_out.shape[0]
     grad = late[:ahead].astype(F32)
-    second_params[:ahead] = early[0].astype(F32) - outer_rate * (1 + outer_momentum) * grad
-    second_moment[:ahead] = outer_momentum * early[1].astype(F32) + grad
-    second_params[ahead:] = late[ahead:rows].astype(F32)
-    second_moment[ahead:] = late[rows:].astype(F32)
+    params_out[:ahead] = early[0].astype(F32) - outer_rate * (1 + outer_momentum) * grad
+    moment_out[:ahead] = outer_momentum * early[1].astype(F32) + grad
+    params_out[ahead:] = late[ahead:rows].astype(F32)
+    moment_out[ahead:] = late[rows:].astype(F32)
+
+
+def closing_kernel(columns, own, ours, theirs, params, moment, params_out, moment_out):
     grad = (own[...].astype(F32) + ours[...].astype(F32) + theirs[...].astype(F32)) / columns
     moment_new = outer_momentum * moment[...] + grad
     moment_out[...] = moment_new
@@ -226,7 +231,8 @@
         first_pieces.append((ours, -step))
         if step < last:
             theirs = lax.ppermute(theirs, ("row", "col"), ring)
-            first_pieces.append((lax.ppermute(theirs, "row", partner), step))
+            across = lax.ppermute(theirs, "row", partner)
+            first_pieces.append((across, step))
     second_pieces, flips = [(held, [0])], [0]
     bit = n_row // 2
     while bit >= 1:
@@ -238,7 +244,7 @@
         if bit >= 1:
             other, _ = lax.optimization_barrier((other, later))
             held = jnp.concatenate([held, other])
-    early, _ = lax.optimization_barrier((early, ours))
+    early, _ = lax.optimization_barrier((early, theirs))
     early = lax.ppermute(early, "col", ahead_by)
     if tiled(rows1):
         first_blocks, first_plan = [p[0] for p in first_pieces], [p[1] for p in first_pieces]
@@ -338,19 +344,18 @@
             theirs = lax.ppermute(theirs, ("row", "col"), ring)
     theirs = lax.ppermute(theirs, "row", partner)
 
-    news = call(
+    second_new = call(arrive_kernel, [shape_of((rows2, width), F32)] * 2, [], early, late)
+    first_new = call(
         lambda *refs: closing_kernel(columns, *refs),
-        [shape_of((rows1, width), F32)] * 2 + [shape_of((rows2, width), F32)] * 2,
+        [shape_of((rows1, width), F32)] * 2,
         [],
         own_terms[last],
         ours,
         theirs,
         first_params[0],
         first_moment[0],
-        early,
-        late,
-    )
-    return tuple(new[None] for new in news)
+    )
+    return tuple(new[None] for new in (*first_new, *second_new))
 
 
 def solution(mesh):

time: 92.9 us -> 93 us (level)
    pallas_call x11 -> x12, Pallas kernels: 9.06 us -> 9.75 us  [call(): pl.pallas_call(kernel, out_shape=tuple(outs), in_specs=[WHOLE] * len(oper...]
  transfers between devices with their start and end apart: 26 -> 26, of which waited for: 12 -> 12; matrix products, arithmetic and copies ran while one was open for 1% -> 1% of each run, Pallas kernels for 3% -> 4%
where the time goes in v6:
time: 93 us; the launch traced here: 92.8 us
  waiting for transfers between devices  45.7 us (49%)
  starting transfers between devices  34.1 us (37%)
  Pallas kernels  9.75 us (10%)
  other arithmetic  2.42 us (3%)
    ppermute x7, waiting for transfers between devices, per_device(): ours = lax.ppermute(ours, ('row', 'col'), ring)  34.1 us
    ppermute x7, starting transfers between devices, per_device(): ours = lax.ppermute(ours, ('row', 'col'), ring)  15.1 us
    pallas_call x12, Pallas kernels, call(): pl.pallas_call(kernel, out_shape=tuple(outs), in_specs=[WHOLE] * len(oper...  9.75 us
    ppermute x5, starting transfers between devices, per_device(): theirs = lax.ppermute(theirs, ('row', 'col'), ring)  8.81 us
    ppermute x5, waiting for transfers between devices, per_device(): theirs = lax.ppermute(theirs, ('row', 'col'), ring)  7.68 us
    ppermute x1, starting transfers between devices, per_device(): ours = lax.ppermute(own_terms[0], ('row', 'col'), ring)  2.07 us
    ppermute x1, waiting for transfers between devices, per_device(): came = lax.ppermute(away, 'row', swap_pairs(n_row, bit))  1.93 us
  transfers between devices with their start and end apart: 26, of which 12 were waited for; matrix products, arithmetic and copies ran while one was open for 1% of the time, Pallas kernels for 4%

profile of v6, /device:TPU:0, one launch (start us, length us, event | category | flops | bytes accessed | tf_op | source)
XLA Modules:
  0.0 92.8 jit_solution(2219313094753277505)
XLA Ops:
  0.7 1.2 %bitcast_convert_fusion.refs_0_ = bf16[112,896]{1,0:T(8,128)(2,1)S(1)} fusion(f32[1,112,896]{2,1,0:T(8,128)} %param.8), kind=kLoop, calls=%fused_computation.4 | loop fusion | flops 100352 | bytes 602112 | tf_op jit(solution)/shard_map/convert_element_type | solution.py:220
  1.8 3.1 %collective-permute-start = (bf16[112,896]{1,0:T(8,128)(2,1)S(1)}, bf16[112,896]{1,0:T(8,128)(2,1)S(1)}, u32[]{:S(2)}, u32[]{:S(2)}) collective-permute-start(bf16[112,896]{1,0:T(8,128)(2,1)S(1)} %bitcast_convert_fusion.refs_0_), channel_id=1, source_target_pairs={{0,2},{2,4},{4,6},{6,7},{7,5},{5,3},{3,1},{1,0},{10,8},{12,10},{14... | collective-permute-start | bytes 602120 | tf_op jit(solution)/shard_map/ppermute | solution.py:230
  4.9 1.2 %convert_element_type.8.refs_8_ = bf16[1,224,896]{2,1,0:T(8,128)(2,1)S(1)} convert(f32[1,224,896]{2,1,0:T(8,128)} %param.10) | non-fusion elementwise | flops 200704 | bytes 1204224 | tf_op jit(solution)/shard_map/convert_element_type | solution.py:221
  6.1 1.6 %collective-permute-start.11 = (bf16[1,224,896]{2,1,0:T(8,128)(2,1)S(1)}, bf16[1,224,896]{2,1,0:T(8,128)(2,1)S(1)}, u32[]{:S(2)}, u32[]{:S(2)}) collective-permute-start(bf16[1,224,896]{2,1,0:T(8,128)(2,1)S(1)} %convert_element_type.8.refs_8_), channel_id=1, source_target_pairs={{0,16},{8,24},{16,0},{24,8},{1,17},{9,25},{17,1},{25,9},{2,18},{10... | collective-permute-start | bytes 1204232 | tf_op jit(solution)/shard_map/ppermute | solution.py:239
  7.7 0.9 collective-permute-done.refs_1_
  8.6 2.1 %collective-permute-start.4 = (bf16[112,896]{1,0:T(8,128)(2,1)S(1)}, bf16[112,896]{1,0:T(8,128)(2,1)S(1)}, u32[]{:S(2)}, u32[]{:S(2)}) collective-permute-start(bf16[112,896]{1,0:T(8,128)(2,1)S(1)} %collective-permute-done.refs_1_), channel_id=1, source_target_pairs={{0,2},{2,4},{4,6},{6,7},{7,5},{5,3},{3,1},{1,0},{10,8},{12,10},{14... | collective-permute-start | bytes 602120 | tf_op jit(solution)/shard_map/ppermute | solution.py:230
  10.6 0.0 collective-permute-start.1
  10.6 3.6 %collective-permute-done.4.refs_3_ = bf16[112,896]{1,0:T(8,128)(2,1)S(1)} collective-permute-done((bf16[112,896]{1,0:T(8,128)(2,1)S(1)}, bf16[112,896]{1,0:T(8,128)(2,1)S(1)}, u32[]{:S(2)}, u32[]{:S(2)}) %collective-permute-start.4) | collective-permute-done | bytes 200736 | tf_op jit(solution)/shard_map/ppermute | solution.py:230
  14.3 2.1 %collective-permute-start.7 = (bf16[112,896]{1,0:T(8,128)(2,1)S(1)}, bf16[112,896]{1,0:T(8,128)(2,1)S(1)}, u32[]{:S(2)}, u32[]{:S(2)}) collective-permute-start(bf16[112,896]{1,0:T(8,128)(2,1)S(1)} %collective-permute-done.4.refs_3_), channel_id=1, source_target_pairs={{0,2},{2,4},{4,6},{6,7},{7,5},{5,3},{3,1},{1,0},{10,8},{12,10},{14... | collective-permute-start | bytes 602120 | tf_op jit(solution)/shard_map/ppermute | solution.py:230
  16.3 0.0 collective-permute-done.1
  16.3 1.6 %collective-permute-start.2 = (bf16[112,896]{1,0:T(8,128)(2,1)S(1)}, bf16[112,896]{1,0:T(8,128)(2,1)S(1)}, u32[]{:S(2)}, u32[]{:S(2)}) collective-permute-start(bf16[112,896]{1,0:T(8,128)(2,1)S(1)} %collective-permute-done.1), channel_id=1, source_target_pairs={{0,2},{2,4},{4,6},{6,7},{7,5},{5,3},{3,1},{1,0},{10,8},{12,10},{14... | collective-permute-start | bytes 602120 | tf_op jit(solution)/shard_map/ppermute | solution.py:233
  17.9 0.0 collective-permute-done.11.refs_9_
  17.9 2.1 %collective-permute-done.7.refs_5_ = bf16[112,896]{1,0:T(8,128)(2,1)S(1)} collective-permute-done((bf16[112,896]{1,0:T(8,128)(2,1)S(1)}, bf16[112,896]{1,0:T(8,128)(2,1)S(1)}, u32[]{:S(2)}, u32[]{:S(2)}) %collective-permute-start.7) | collective-permute-done | bytes 200736 | tf_op jit(solution)/shard_map/ppermute | solution.py:230
  20.0 0.1 pad_maximum_fusion
  20.1 0.1 collective-permute-start.12
  20.1 2.0 %collective-permute-done.2 = bf16[112,896]{1,0:T(8,128)(2,1)S(1)} collective-permute-done((bf16[112,896]{1,0:T(8,128)(2,1)S(1)}, bf16[112,896]{1,0:T(8,128)(2,1)S(1)}, u32[]{:S(2)}, u32[]{:S(2)}) %collective-permute-start.2) | collective-permute-done | bytes 200736 | tf_op jit(solution)/shard_map/ppermute | solution.py:233
  22.1 2.1 %collective-permute-start.5 = (bf16[112,896]{1,0:T(8,128)(2,1)S(1)}, bf16[112,896]{1,0:T(8,128)(2,1)S(1)}, u32[]{:S(2)}, u32[]{:S(2)}) collective-permute-start(bf16[112,896]{1,0:T(8,128)(2,1)S(1)} %collective-permute-done.2), channel_id=1, source_target_pairs={{0,2},{2,4},{4,6},{6,7},{7,5},{5,3},{3,1},{1,0},{10,8},{12,10},{14... | collective-permute-start | bytes 602120 | tf_op jit(solution)/shard_map/ppermute | solution.py:233
  24.2 3.6 %collective-permute-done.5 = bf16[112,896]{1,0:T(8,128)(2,1)S(1)} collective-permute-done((bf16[112,896]{1,0:T(8,128)(2,1)S(1)}, bf16[112,896]{1,0:T(8,128)(2,1)S(1)}, u32[]{:S(2)}, u32[]{:S(2)}) %collective-permute-start.5) | collective-permute-done | bytes 200736 | tf_op jit(solution)/shard_map/ppermute | solution.py:233
  27.8 2.1 %collective-permute-start.8 = (bf16[112,896]{1,0:T(8,128)(2,1)S(1)}, bf16[112,896]{1,0:T(8,128)(2,1)S(1)}, u32[]{:S(2)}, u32[]{:S(2)}) collective-permute-start(bf16[112,896]{1,0:T(8,128)(2,1)S(1)} %collective-permute-done.5), channel_id=1, source_target_pairs={{0,2},{2,4},{4,6},{6,7},{7,5},{5,3},{3,1},{1,0},{10,8},{12,10},{14... | collective-permute-start | bytes 602120 | tf_op jit(solution)/shard_map/ppermute | solution.py:233
  29.9 0.0 collective-permute-start.3
  29.9 1.6 %collective-permute-start.10 = (bf16[112,896]{1,0:T(8,128)(2,1)S(1)}, bf16[112,896]{1,0:T(8,128)(2,1)S(1)}, u32[]{:S(2)}, u32[]{:S(2)}) collective-permute-start(bf16[112,896]{1,0:T(8,128)(2,1)S(1)} %collective-permute-done.7.refs_5_), channel_id=1, source_target_pairs={{0,2},{2,4},{4,6},{6,7},{7,5},{5,3},{3,1},{1,0},{10,8},{12,10},{14... | collective-permute-start | bytes 602120 | tf_op jit(solution)/shard_map/ppermute | solution.py:230
  31.5 0.0 collective-permute-start.6
  31.5 2.1 %collective-permute-done.8 = bf16[112,896]{1,0:T(8,128)(2,1)S(1)} collective-permute-done((bf16[112,896]{1,0:T(8,128)(2,1)S(1)}, bf16[112,896]{1,0:T(8,128)(2,1)S(1)}, u32[]{:S(2)}, u32[]{:S(2)}) %collective-permute-start.8) | collective-permute-done | bytes 200736 | tf_op jit(solution)/shard_map/ppermute | solution.py:233
  33.6 0.0 collective-permute-start.9
  33.6 0.0 collective-permute-done.3.refs_2_
  33.6 2.1 %collective-permute-done.10.refs_7_ = bf16[112,896]{1,0:T(8,128)(2,1)S(1)} collective-permute-done((bf16[112,896]{1,0:T(8,128)(2,1)S(1)}, bf16[112,896]{1,0:T(8,128)(2,1)S(1)}, u32[]{:S(2)}, u32[]{:S(2)}) %collective-permute-start.10) | collective-permute-done | bytes 200736 | tf_op jit(solution)/shard_map/ppermute | solution.py:230
  35.7 0.0 collective-permute-done.6.refs_4_
  35.7 0.0 collective-permute-done.9.refs_6_
  35.7 4.4 %shard_map.93 = (bf16[2,224,896]{2,1,0:T(8,128)(2,1)S(1)}, bf16[2,224,896]{2,1,0:T(8,128)(2,1)S(1)}, bf16[512,896]{1,0:T(8,128)(2,1)S(1)}, f32[512,896]{1,0:T(8,128)S(1)}, bf16[896,896]{1,0:T(8,128)(2,1)S(1)}) custom-call(bf16[112,896]{1,0:T(8,128)(2,1)S(1)} %bitcast_convert_fusion.refs_0_, bf16[112,896]{1,0:T(8,128)(2,1)S(1)} %collective-permute-done.refs_1_, ...), custom_call_target="tpu_custom_call" | custom-call | flops 2466250752 | bytes 5046272 | tf_op jit(solution)/shard_map/pallas_call | solution.py:25
  40.2 0.1 collective-permute-start.23
  40.2 2.3 %shard_map.94 = (bf16[112,896]{1,0:T(8,128)(2,1)S(1)}, bf16[112,896]{1,0:T(8,128)(2,1)S(1)}, bf16[112,896]{1,0:T(8,128)(2,1)S(1)}, bf16[112,896]{1,0:T(8,128)(2,...) custom-call(bf16[512,896]{1,0:T(8,128)(2,1)S(1)} %bitcast.25, ...), custom_call_target="tpu_custom_call" | custom-call | flops 1644167168 | bytes 5275648 | tf_op jit(solution)/shard_map/pallas_call | solution.py:25
  42.6 0.6 collective-permute-start.17
  43.2 2.1 %collective-permute-start.13 = (bf16[112,896]{1,0:T(8,128)(2,1)S(1)}, bf16[112,896]{1,0:T(8,128)(2,1)S(1)}, u32[]{:S(2)}, u32[]{:S(2)}) collective-permute-start(bf16[112,896]{1,0:T(8,128)(2,1)S(1)} %get-tuple-element.31), channel_id=1, source_target_pairs={{0,2},{2,4},{4,6},{6,7},{7,5},{5,3},{3,1},{1,0},{10,8},{12,10},{14... | collective-permute-start | bytes 602120 | tf_op jit(solution)/shard_map/ppermute | solution.py:336
  45.2 0.2 shard_map.102
  45.4 1.6 %collective-permute-start.24 = (bf16[1,224,896]{2,1,0:T(8,128)(2,1)S(1)}, bf16[1,224,896]{2,1,0:T(8,128)(2,1)S(1)}, u32[]{:S(2)}, u32[]{:S(2)}) collective-permute-start(bf16[1,224,896]{2,1,0:T(8,128)(2,1)S(1)} %get-tuple-element.39), channel_id=1, source_target_pairs={{0,16},{8,24},{16,0},{24,8},{1,17},{9,25},{17,1},{25,9},{2,18},{10... | collective-permute-start | bytes 1204232 | tf_op jit(solution)/shard_map/ppermute | solution.py:324
  47.0 0.0 collective-permute-done.17
  47.0 1.6 %collective-permute-start.18 = (bf16[112,896]{1,0:T(8,128)(2,1)S(1)}, bf16[112,896]{1,0:T(8,128)(2,1)S(1)}, u32[]{:S(2)}, u32[]{:S(2)}) collective-permute-start(bf16[112,896]{1,0:T(8,128)(2,1)S(1)} %get-tuple-element.42), channel_id=1, source_target_pairs={{0,2},{2,4},{4,6},{6,7},{7,5},{5,3},{3,1},{1,0},{10,8},{12,10},{14... | collective-permute-start | bytes 602120 | tf_op jit(solution)/shard_map/ppermute | solution.py:338
  48.7 0.2 collective-permute-done.13.came
  48.9 0.1 shard_map.95
  48.9 2.1 %collective-permute-start.14 = (bf16[112,896]{1,0:T(8,128)(2,1)S(1)}, bf16[112,896]{1,0:T(8,128)(2,1)S(1)}, u32[]{:S(2)}, u32[]{:S(2)}) collective-permute-start(bf16[112,896]{1,0:T(8,128)(2,1)S(1)} %shard_map.95), channel_id=1, source_target_pairs={{0,2},{2,4},{4,6},{6,7},{7,5},{5,3},{3,1},{1,0},{10,8},{12,10},{14... | collective-permute-start | bytes 602120 | tf_op jit(solution)/shard_map/ppermute | solution.py:341
  51.0 1.8 %collective-permute-done.18.came = bf16[112,896]{1,0:T(8,128)(2,1)S(1)} collective-permute-done((bf16[112,896]{1,0:T(8,128)(2,1)S(1)}, bf16[112,896]{1,0:T(8,128)(2,1)S(1)}, u32[]{:S(2)}, u32[]{:S(2)}) %collective-permute-start.18) | collective-permute-done | bytes 200736 | tf_op jit(solution)/shard_map/ppermute | solution.py:338
  52.8 0.1 shard_map.98
  52.9 1.6 %collective-permute-start.19 = (bf16[112,896]{1,0:T(8,128)(2,1)S(1)}, bf16[112,896]{1,0:T(8,128)(2,1)S(1)}, u32[]{:S(2)}, u32[]{:S(2)}) collective-permute-start(bf16[112,896]{1,0:T(8,128)(2,1)S(1)} %shard_map.98), channel_id=1, source_target_pairs={{0,2},{2,4},{4,6},{6,7},{7,5},{5,3},{3,1},{1,0},{10,8},{12,10},{14... | collective-permute-start | bytes 602120 | tf_op jit(solution)/shard_map/ppermute | solution.py:344
  54.5 1.9 %collective-permute-done.24.refs_1_ = bf16[1,224,896]{2,1,0:T(8,128)(2,1)S(1)} collective-permute-done((bf16[1,224,896]{2,1,0:T(8,128)(2,1)S(1)}, bf16[1,224,896]{2,1,0:T(8,128)(2,1)S(1)}, u32[]{:S(2)}, u32[]{:S(2)}) %collective-permute-start.24) | collective-permute-done | bytes 401440 | tf_op jit(solution)/shard_map/ppermute | solution.py:324
  56.4 0.2 shard_map.103
  56.6 0.0 copy-start.2
  56.6 0.0 copy-start.3
  56.6 0.4 collective-permute-start.25
  57.1 0.1 shard_map.101
  57.1 1.7 %collective-permute-start.22 = (bf16[2,128,896]{2,1,0:T(8,128)(2,1)S(1)}, bf16[2,128,896]{2,1,0:T(8,128)(2,1)S(1)}, u32[]{:S(2)}, u32[]{:S(2)}) collective-permute-start(bf16[2,128,896]{2,1,0:T(8,128)(2,1)S(1)} %shard_map.101), channel_id=1, source_target_pairs={{0,2},{1,3},{2,4},{3,5},{4,6},{5,7},{6,0},{7,1},{8,10},{9,11},{10,... | collective-permute-start | bytes 1376264 | tf_op jit(solution)/shard_map/ppermute | solution.py:248
  58.9 0.0 collective-permute-done.14.came
  58.9 1.6 %collective-permute-start.15 = (bf16[112,896]{1,0:T(8,128)(2,1)S(1)}, bf16[112,896]{1,0:T(8,128)(2,1)S(1)}, u32[]{:S(2)}, u32[]{:S(2)}) collective-permute-start(bf16[112,896]{1,0:T(8,128)(2,1)S(1)} %shard_map.96), channel_id=1, source_target_pairs={{0,2},{2,4},{4,6},{6,7},{7,5},{5,3},{3,1},{1,0},{10,8},{12,10},{14... | collective-permute-start | bytes 602120 | tf_op jit(solution)/shard_map/ppermute | solution.py:341
  60.6 0.1 shard_map.99
  60.6 1.5 %collective-permute-start.20 = (bf16[112,896]{1,0:T(8,128)(2,1)S(1)}, bf16[112,896]{1,0:T(8,128)(2,1)S(1)}, u32[]{:S(2)}, u32[]{:S(2)}) collective-permute-start(bf16[112,896]{1,0:T(8,128)(2,1)S(1)} %shard_map.99), channel_id=1, source_target_pairs={{0,2},{2,4},{4,6},{6,7},{7,5},{5,3},{3,1},{1,0},{10,8},{12,10},{14... | collective-permute-start | bytes 602120 | tf_op jit(solution)/shard_map/ppermute | solution.py:344
  62.1 19.9 %collective-permute-done.15.came = bf16[112,896]{1,0:T(8,128)(2,1)S(1)} collective-permute-done((bf16[112,896]{1,0:T(8,128)(2,1)S(1)}, bf16[112,896]{1,0:T(8,128)(2,1)S(1)}, u32[]{:S(2)}, u32[]{:S(2)}) %collective-permute-start.15) | collective-permute-done | bytes 200736 | tf_op jit(solution)/shard_map/ppermute | solution.py:341
  82.0 0.1 shard_map.97
  82.1 2.5 %collective-permute-start.16 = (bf16[112,896]{1,0:T(8,128)(2,1)S(1)}, bf16[112,896]{1,0:T(8,128)(2,1)S(1)}, u32[]{:S(2)}, u32[]{:S(2)}) collective-permute-start(bf16[112,896]{1,0:T(8,128)(2,1)S(1)} %shard_map.97), channel_id=1, source_target_pairs={{0,2},{2,4},{4,6},{6,7},{7,5},{5,3},{3,1},{1,0},{10,8},{12,10},{14... | collective-permute-start | bytes 602120 | tf_op jit(solution)/shard_map/ppermute | solution.py:341
  84.6 0.0 collective-permute-done.20
  84.6 0.5 collective-permute-start.21
  85.1 5.4 %collective-permute-done.16.refs_1_ = bf16[112,896]{1,0:T(8,128)(2,1)S(1)} collective-permute-done((bf16[112,896]{1,0:T(8,128)(2,1)S(1)}, bf16[112,896]{1,0:T(8,128)(2,1)S(1)}, u32[]{:S(2)}, u32[]{:S(2)}) %collective-permute-start.16) | collective-permute-done | bytes 200736 | tf_op jit(solution)/shard_map/ppermute | solution.py:341
  90.5 0.0 collective-permute-done.21.refs_2_
  90.5 1.0 %shard_map.100 = (f32[112,896]{1,0:T(8,128)}, f32[112,896]{1,0:T(8,128)}) custom-call(bf16[112,896]{1,0:T(8,128)(2,1)S(1)} %get-tuple-element.27.refs_0_, bf16[112,896]{1,0:T(8,128)(2,1)S(1)} %collective-permute-done.16.refs_1_, bf16[112,896]{1,0:T(8,128)(2,1)S(1)} %collective-permute-done.21.refs_2_, f32[112,896]{1,0:T(8,128)S(1)} %bitcast.21, ...), custom_call_target="tpu_custom_call" | custom-call | bytes 1404928 | tf_op jit(solution)/shard_map/pallas_call | solution.py:25
  91.5 0.0 collective-permute-done.25.late
  91.5 1.3 %shard_map.104 = (f32[224,896]{1,0:T(8,128)}, f32[224,896]{1,0:T(8,128)}) custom-call(bf16[2,128,896]{2,1,0:T(8,128)(2,1)S(1)} %collective-permute-done.22.early, bf16[320,896]{1,0:T(8,128)(2,1)S(1)} %collective-permute-done.25.late), custom_call_target="tpu_custom_call" | custom-call | bytes 1032192 | tf_op jit(solution)/shard_map/pallas_call | solution.py:25
  (16 shorter events, 0.1 us)
Async XLA Ops:
  0.6 35.1 %copy-start.5 = (bf16[1,1,512,896]{3,2,1,0:T(8,128)(2,1)S(1)}, bf16[1,1,512,896]{3,2,1,0:T(8,128)(2,1)}, u32[]{:S(2)}) copy-start(bf16[1,1,512,896]{3,2,1,0:T(8,128)(2,1)} %param.6) | copy-start | bytes 2752516
  0.6 35.1 %copy-start.4 = (bf16[1,1,512,896]{3,2,1,0:T(8,128)(2,1)S(1)}, bf16[1,1,512,896]{3,2,1,0:T(8,128)(2,1)}, u32[]{:S(2)}) copy-start(bf16[1,1,512,896]{3,2,1,0:T(8,128)(2,1)} %param.7) | copy-start | bytes 2752516
  1.8 6.7 %collective-permute-start = (bf16[112,896]{1,0:T(8,128)(2,1)S(1)}, bf16[112,896]{1,0:T(8,128)(2,1)S(1)}, u32[]{:S(2)}, u32[]{:S(2)}) collective-permute-start(bf16[112,896]{1,0:T(8,128)(2,1)S(1)} %bitcast_convert_fusion.refs_0_), channel_id=1, source_target_pairs={{0,2},{2,4},{4,6},{6,7},{7,5},{5,3},{3,1},{1,0},{10,8},{12,10},{14... | collective-permute-start | bytes 602120 | tf_op jit(solution)/shard_map/ppermute | solution.py:230
  6.1 11.8 %collective-permute-start.11 = (bf16[1,224,896]{2,1,0:T(8,128)(2,1)S(1)}, bf16[1,224,896]{2,1,0:T(8,128)(2,1)S(1)}, u32[]{:S(2)}, u32[]{:S(2)}) collective-permute-start(bf16[1,224,896]{2,1,0:T(8,128)(2,1)S(1)} %convert_element_type.8.refs_8_), channel_id=1, source_target_pairs={{0,16},{8,24},{16,0},{24,8},{1,17},{9,25},{17,1},{25,9},{2,18},{10... | collective-permute-start | bytes 1204232 | tf_op jit(solution)/shard_map/ppermute | solution.py:239
  8.6 5.7 %collective-permute-start.4 = (bf16[112,896]{1,0:T(8,128)(2,1)S(1)}, bf16[112,896]{1,0:T(8,128)(2,1)S(1)}, u32[]{:S(2)}, u32[]{:S(2)}) collective-permute-start(bf16[112,896]{1,0:T(8,128)(2,1)S(1)} %collective-permute-done.refs_1_), channel_id=1, source_target_pairs={{0,2},{2,4},{4,6},{6,7},{7,5},{5,3},{3,1},{1,0},{10,8},{12,10},{14... | collective-permute-start | bytes 602120 | tf_op jit(solution)/shard_map/ppermute | solution.py:230
  10.6 5.7 %collective-permute-start.1 = (bf16[112,896]{1,0:T(8,128)(2,1)S(1)}, bf16[112,896]{1,0:T(8,128)(2,1)S(1)}, u32[]{:S(2)}, u32[]{:S(2)}) collective-permute-start(bf16[112,896]{1,0:T(8,128)(2,1)S(1)} %bitcast_convert_fusion.refs_0_), channel_id=1, source_target_pairs={{0,8},{8,0},{16,24},{24,16},{1,9},{9,1},{17,25},{25,17},{2,10},{10... | collective-permute-start | bytes 602120 | tf_op jit(solution)/shard_map/ppermute | solution.py:227
  14.3 5.7 %collective-permute-start.7 = (bf16[112,896]{1,0:T(8,128)(2,1)S(1)}, bf16[112,896]{1,0:T(8,128)(2,1)S(1)}, u32[]{:S(2)}, u32[]{:S(2)}) collective-permute-start(bf16[112,896]{1,0:T(8,128)(2,1)S(1)} %collective-permute-done.4.refs_3_), channel_id=1, source_target_pairs={{0,2},{2,4},{4,6},{6,7},{7,5},{5,3},{3,1},{1,0},{10,8},{12,10},{14... | collective-permute-start | bytes 602120 | tf_op jit(solution)/shard_map/ppermute | solution.py:230
  16.3 5.8 %collective-permute-start.2 = (bf16[112,896]{1,0:T(8,128)(2,1)S(1)}, bf16[112,896]{1,0:T(8,128)(2,1)S(1)}, u32[]{:S(2)}, u32[]{:S(2)}) collective-permute-start(bf16[112,896]{1,0:T(8,128)(2,1)S(1)} %collective-permute-done.1), channel_id=1, source_target_pairs={{0,2},{2,4},{4,6},{6,7},{7,5},{5,3},{3,1},{1,0},{10,8},{12,10},{14... | collective-permute-start | bytes 602120 | tf_op jit(solution)/shard_map/ppermute | solution.py:233
  20.1 15.7 %collective-permute-start.12 = (bf16[2,224,896]{2,1,0:T(8,128)(2,1)S(1)}, bf16[2,224,896]{2,1,0:T(8,128)(2,1)S(1)}, u32[]{:S(2)}, u32[]{:S(2)}) collective-permute-start(bf16[2,224,896]{2,1,0:T(8,128)(2,1)S(1)} %pad_maximum_fusion), channel_id=1, source_target_pairs={{0,8},{8,0},{16,24},{24,16},{1,9},{9,1},{17,25},{25,17},{2,10},{10... | collective-permute-start | bytes 2408456 | tf_op jit(solution)/shard_map/ppermute | solution.py:239
  22.1 5.7 %collective-permute-start.5 = (bf16[112,896]{1,0:T(8,128)(2,1)S(1)}, bf16[112,896]{1,0:T(8,128)(2,1)S(1)}, u32[]{:S(2)}, u32[]{:S(2)}) collective-permute-start(bf16[112,896]{1,0:T(8,128)(2,1)S(1)} %collective-permute-done.2), channel_id=1, source_target_pairs={{0,2},{2,4},{4,6},{6,7},{7,5},{5,3},{3,1},{1,0},{10,8},{12,10},{14... | collective-permute-start | bytes 602120 | tf_op jit(solution)/shard_map/ppermute | solution.py:233
  27.8 5.7 %collective-permute-start.8 = (bf16[112,896]{1,0:T(8,128)(2,1)S(1)}, bf16[112,896]{1,0:T(8,128)(2,1)S(1)}, u32[]{:S(2)}, u32[]{:S(2)}) collective-permute-start(bf16[112,896]{1,0:T(8,128)(2,1)S(1)} %collective-permute-done.5), channel_id=1, source_target_pairs={{0,2},{2,4},{4,6},{6,7},{7,5},{5,3},{3,1},{1,0},{10,8},{12,10},{14... | collective-permute-start | bytes 602120 | tf_op jit(solution)/shard_map/ppermute | solution.py:233
  29.9 3.6 %collective-permute-start.3 = (bf16[112,896]{1,0:T(8,128)(2,1)S(1)}, bf16[112,896]{1,0:T(8,128)(2,1)S(1)}, u32[]{:S(2)}, u32[]{:S(2)}) collective-permute-start(bf16[112,896]{1,0:T(8,128)(2,1)S(1)} %collective-permute-done.2), channel_id=1, source_target_pairs={{0,8},{8,0},{16,24},{24,16},{1,9},{9,1},{17,25},{25,17},{2,10},{10... | collective-permute-start | bytes 602120 | tf_op jit(solution)/shard_map/ppermute | solution.py:234
  29.9 5.8 %collective-permute-start.10 = (bf16[112,896]{1,0:T(8,128)(2,1)S(1)}, bf16[112,896]{1,0:T(8,128)(2,1)S(1)}, u32[]{:S(2)}, u32[]{:S(2)}) collective-permute-start(bf16[112,896]{1,0:T(8,128)(2,1)S(1)} %collective-permute-done.7.refs_5_), channel_id=1, source_target_pairs={{0,2},{2,4},{4,6},{6,7},{7,5},{5,3},{3,1},{1,0},{10,8},{12,10},{14... | collective-permute-start | bytes 602120 | tf_op jit(solution)/shard_map/ppermute | solution.py:230
  31.5 4.2 %collective-permute-start.6 = (bf16[112,896]{1,0:T(8,128)(2,1)S(1)}, bf16[112,896]{1,0:T(8,128)(2,1)S(1)}, u32[]{:S(2)}, u32[]{:S(2)}) collective-permute-start(bf16[112,896]{1,0:T(8,128)(2,1)S(1)} %collective-permute-done.5), channel_id=1, source_target_pairs={{0,8},{8,0},{16,24},{24,16},{1,9},{9,1},{17,25},{25,17},{2,10},{10... | collective-permute-start | bytes 602120 | tf_op jit(solution)/shard_map/ppermute | solution.py:234
  33.6 2.2 %collective-permute-start.9 = (bf16[112,896]{1,0:T(8,128)(2,1)S(1)}, bf16[112,896]{1,0:T(8,128)(2,1)S(1)}, u32[]{:S(2)}, u32[]{:S(2)}) collective-permute-start(bf16[112,896]{1,0:T(8,128)(2,1)S(1)} %collective-permute-done.8), channel_id=1, source_target_pairs={{0,8},{8,0},{16,24},{24,16},{1,9},{9,1},{17,25},{25,17},{2,10},{10... | collective-permute-start | bytes 602120 | tf_op jit(solution)/shard_map/ppermute | solution.py:234
  40.2 5.1 %collective-permute-start.23 = (bf16[2,224,896]{2,1,0:T(8,128)(2,1)S(1)}, bf16[2,224,896]{2,1,0:T(8,128)(2,1)S(1)}, u32[]{:S(2)}, u32[]{:S(2)}) collective-permute-start(bf16[2,224,896]{2,1,0:T(8,128)(2,1)S(1)} %get-tuple-element.37), channel_id=1, source_target_pairs={{0,8},{8,0},{16,24},{24,16},{1,9},{9,1},{17,25},{25,17},{2,10},{10... | collective-permute-start | bytes 2408456 | tf_op jit(solution)/shard_map/ppermute | solution.py:279
  42.6 4.4 %collective-permute-start.17 = (bf16[3,112,896]{2,1,0:T(8,128)(2,1)S(1)}, bf16[3,112,896]{2,1,0:T(8,128)(2,1)S(1)}, u32[]{:S(2)}, u32[]{:S(2)}) collective-permute-start(bf16[3,112,896]{2,1,0:T(8,128)(2,1)S(1)} %get-tuple-element.32), channel_id=1, source_target_pairs={{0,8},{8,0},{16,24},{24,16},{1,9},{9,1},{17,25},{25,17},{2,10},{10... | collective-permute-start | bytes 1806344 | tf_op jit(solution)/shard_map/ppermute | solution.py:337
  43.2 5.7 %collective-permute-start.13 = (bf16[112,896]{1,0:T(8,128)(2,1)S(1)}, bf16[112,896]{1,0:T(8,128)(2,1)S(1)}, u32[]{:S(2)}, u32[]{:S(2)}) collective-permute-start(bf16[112,896]{1,0:T(8,128)(2,1)S(1)} %get-tuple-element.31), channel_id=1, source_target_pairs={{0,2},{2,4},{4,6},{6,7},{7,5},{5,3},{3,1},{1,0},{10,8},{12,10},{14... | collective-permute-start | bytes 602120 | tf_op jit(solution)/shard_map/ppermute | solution.py:336
  45.2 11.2 %copy-start = (f32[1,224,896]{2,1,0:T(8,128)S(1)}, f32[1,224,896]{2,1,0:T(8,128)}, u32[]{:S(2)}) copy-start(f32[1,224,896]{2,1,0:T(8,128)} %param.10) | copy-start | bytes 2408452
  45.2 11.2 %copy-start.1 = (f32[1,224,896]{2,1,0:T(8,128)S(1)}, f32[1,224,896]{2,1,0:T(8,128)}, u32[]{:S(2)}) copy-start(f32[1,224,896]{2,1,0:T(8,128)} %param.11) | copy-start | bytes 2408452
  45.4 11.0 %collective-permute-start.24 = (bf16[1,224,896]{2,1,0:T(8,128)(2,1)S(1)}, bf16[1,224,896]{2,1,0:T(8,128)(2,1)S(1)}, u32[]{:S(2)}, u32[]{:S(2)}) collective-permute-start(bf16[1,224,896]{2,1,0:T(8,128)(2,1)S(1)} %get-tuple-element.39), channel_id=1, source_target_pairs={{0,16},{8,24},{16,0},{24,8},{1,17},{9,25},{17,1},{25,9},{2,18},{10... | collective-permute-start | bytes 1204232 | tf_op jit(solution)/shard_map/ppermute | solution.py:324
  47.0 5.8 %collective-permute-start.18 = (bf16[112,896]{1,0:T(8,128)(2,1)S(1)}, bf16[112,896]{1,0:T(8,128)(2,1)S(1)}, u32[]{:S(2)}, u32[]{:S(2)}) collective-permute-start(bf16[112,896]{1,0:T(8,128)(2,1)S(1)} %get-tuple-element.42), channel_id=1, source_target_pairs={{0,2},{2,4},{4,6},{6,7},{7,5},{5,3},{3,1},{1,0},{10,8},{12,10},{14... | collective-permute-start | bytes 602120 | tf_op jit(solution)/shard_map/ppermute | solution.py:338
  48.9 10.0 %collective-permute-start.14 = (bf16[112,896]{1,0:T(8,128)(2,1)S(1)}, bf16[112,896]{1,0:T(8,128)(2,1)S(1)}, u32[]{:S(2)}, u32[]{:S(2)}) collective-permute-start(bf16[112,896]{1,0:T(8,128)(2,1)S(1)} %shard_map.95), channel_id=1, source_target_pairs={{0,2},{2,4},{4,6},{6,7},{7,5},{5,3},{3,1},{1,0},{10,8},{12,10},{14... | collective-permute-start | bytes 602120 | tf_op jit(solution)/shard_map/ppermute | solution.py:341
  52.9 7.7 %collective-permute-start.19 = (bf16[112,896]{1,0:T(8,128)(2,1)S(1)}, bf16[112,896]{1,0:T(8,128)(2,1)S(1)}, u32[]{:S(2)}, u32[]{:S(2)}) collective-permute-start(bf16[112,896]{1,0:T(8,128)(2,1)S(1)} %shard_map.98), channel_id=1, source_target_pairs={{0,2},{2,4},{4,6},{6,7},{7,5},{5,3},{3,1},{1,0},{10,8},{12,10},{14... | collective-permute-start | bytes 602120 | tf_op jit(solution)/shard_map/ppermute | solution.py:344
  56.6 33.9 %copy-start.2 = (f32[1,112,896]{2,1,0:T(8,128)S(1)}, f32[1,112,896]{2,1,0:T(8,128)}, u32[]{:S(2)}) copy-start(f32[1,112,896]{2,1,0:T(8,128)} %param.8) | copy-start | bytes 1204228
  56.6 33.9 %copy-start.3 = (f32[1,112,896]{2,1,0:T(8,128)S(1)}, f32[1,112,896]{2,1,0:T(8,128)}, u32[]{:S(2)}) copy-start(f32[1,112,896]{2,1,0:T(8,128)} %param.9) | copy-start | bytes 1204228
  56.6 34.9 %collective-permute-start.25 = (bf16[320,896]{1,0:T(8,128)(2,1)S(1)}, bf16[320,896]{1,0:T(8,128)(2,1)S(1)}, u32[]{:S(2)}, u32[]{:S(2)}) collective-permute-start(bf16[320,896]{1,0:T(8,128)(2,1)S(1)} %shard_map.103), channel_id=1, source_target_pairs={{0,2},{1,3},{2,4},{3,5},{4,6},{5,7},{6,0},{7,1},{8,10},{9,11},{10,... | collective-permute-start | bytes 1720328 | tf_op jit(solution)/shard_map/ppermute | solution.py:335
  57.1 34.4 %collective-permute-start.22 = (bf16[2,128,896]{2,1,0:T(8,128)(2,1)S(1)}, bf16[2,128,896]{2,1,0:T(8,128)(2,1)S(1)}, u32[]{:S(2)}, u32[]{:S(2)}) collective-permute-start(bf16[2,128,896]{2,1,0:T(8,128)(2,1)S(1)} %shard_map.101), channel_id=1, source_target_pairs={{0,2},{1,3},{2,4},{3,5},{4,6},{5,7},{6,0},{7,1},{8,10},{9,11},{10,... | collective-permute-start | bytes 1376264 | tf_op jit(solution)/shard_map/ppermute | solution.py:248
  58.9 23.1 %collective-permute-start.15 = (bf16[112,896]{1,0:T(8,128)(2,1)S(1)}, bf16[112,896]{1,0:T(8,128)(2,1)S(1)}, u32[]{:S(2)}, u32[]{:S(2)}) collective-permute-start(bf16[112,896]{1,0:T(8,128)(2,1)S(1)} %shard_map.96), channel_id=1, source_target_pairs={{0,2},{2,4},{4,6},{6,7},{7,5},{5,3},{3,1},{1,0},{10,8},{12,10},{14... | collective-permute-start | bytes 602120 | tf_op jit(solution)/shard_map/ppermute | solution.py:341
  60.6 24.0 %collective-permute-start.20 = (bf16[112,896]{1,0:T(8,128)(2,1)S(1)}, bf16[112,896]{1,0:T(8,128)(2,1)S(1)}, u32[]{:S(2)}, u32[]{:S(2)}) collective-permute-start(bf16[112,896]{1,0:T(8,128)(2,1)S(1)} %shard_map.99), channel_id=1, source_target_pairs={{0,2},{2,4},{4,6},{6,7},{7,5},{5,3},{3,1},{1,0},{10,8},{12,10},{14... | collective-permute-start | bytes 602120 | tf_op jit(solution)/shard_map/ppermute | solution.py:344
  82.1 8.4 %collective-permute-start.16 = (bf16[112,896]{1,0:T(8,128)(2,1)S(1)}, bf16[112,896]{1,0:T(8,128)(2,1)S(1)}, u32[]{:S(2)}, u32[]{:S(2)}) collective-permute-start(bf16[112,896]{1,0:T(8,128)(2,1)S(1)} %shard_map.97), channel_id=1, source_target_pairs={{0,2},{2,4},{4,6},{6,7},{7,5},{5,3},{3,1},{1,0},{10,8},{12,10},{14... | collective-permute-start | bytes 602120 | tf_op jit(solution)/shard_map/ppermute | solution.py:341
  84.6 5.9 %collective-permute-start.21 = (bf16[112,896]{1,0:T(8,128)(2,1)S(1)}, bf16[112,896]{1,0:T(8,128)(2,1)S(1)}, u32[]{:S(2)}, u32[]{:S(2)}) collective-permute-start(bf16[112,896]{1,0:T(8,128)(2,1)S(1)} %collective-permute-done.20), channel_id=1, source_target_pairs={{0,8},{8,0},{16,24},{24,16},{1,9},{9,1},{17,25},{25,17},{2,10},{10... | collective-permute-start | bytes 602120 | tf_op jit(solution)/shard_map/ppermute | solution.py:345

commit v7 on v6

--- a/solution.py
+++ b/solution.py
@@ -64,10 +64,10 @@
 def gelu_and_slope(value):
     scale = math.sqrt(2 / math.pi)
     square = value * value
-    bent = jnp.tanh(scale * (value + 0.044715 * value * square))
-    half = 0.5 * (1 + bent)
-    slope = half + (0.5 * scale) * value * (1 - bent * bent) * (1 + 3 * 0.044715 * square)
-    return value * half, slope
+    half = 0.5 + 0.5 * jnp.tanh(value * (scale + scale * 0.044715 * square))
+    result = value * half
+    slope = half + (result - result * half) * (2 * scale + 6 * scale * 0.044715 * square)
+    return result, slope
 
 
 def rows_from(pieces, rows, length):

time: 93 us -> 92.8 us (level)
  no operation moved by 1% of the time
where the time goes in v7:
time: 92.8 us; the launch traced here: 92.6 us
  waiting for transfers between devices  45.6 us (49%)
  starting transfers between devices  34.2 us (37%)
  Pallas kernels  9.56 us (10%)
  other arithmetic  2.42 us (3%)
    ppermute x7, waiting for transfers between devices, per_device(): ours = lax.ppermute(ours, ('row', 'col'), ring)  34 us
    ppermute x7, starting transfers between devices, per_device(): ours = lax.ppermute(ours, ('row', 'col'), ring)  15.1 us
    pallas_call x12, Pallas kernels, call(): pl.pallas_call(kernel, out_shape=tuple(outs), in_specs=[WHOLE] * len(oper...  9.56 us
    ppermute x5, starting transfers between devices, per_device(): theirs = lax.ppermute(theirs, ('row', 'col'), ring)  8.84 us
    ppermute x5, waiting for transfers between devices, per_device(): theirs = lax.ppermute(theirs, ('row', 'col'), ring)  7.68 us
    ppermute x1, starting transfers between devices, per_device(): ours = lax.ppermute(own_terms[0], ('row', 'col'), ring)  2.08 us
    ppermute x1, waiting for transfers between devices, per_device(): came = lax.ppermute(away, 'row', swap_pairs(n_row, bit))  1.92 us
  transfers between devices with their start and end apart: 26, of which 12 were waited for; matrix products, arithmetic and copies ran while one was open for 1% of the time, Pallas kernels for 4%

profile of v7, /device:TPU:0, one launch (start us, length us, event | category | flops | bytes accessed | tf_op | source)
XLA Modules:
  0.0 92.6 jit_solution(5722622219583169393)
XLA Ops:
  0.7 1.2 %bitcast_convert_fusion.refs_0_ = bf16[112,896]{1,0:T(8,128)(2,1)S(1)} fusion(f32[1,112,896]{2,1,0:T(8,128)} %param.8), kind=kLoop, calls=%fused_computation.4 | loop fusion | flops 100352 | bytes 602112 | tf_op jit(solution)/shard_map/convert_element_type | solution.py:220
  1.8 3.1 %collective-permute-start = (bf16[112,896]{1,0:T(8,128)(2,1)S(1)}, bf16[112,896]{1,0:T(8,128)(2,1)S(1)}, u32[]{:S(2)}, u32[]{:S(2)}) collective-permute-start(bf16[112,896]{1,0:T(8,128)(2,1)S(1)} %bitcast_convert_fusion.refs_0_), channel_id=1, source_target_pairs={{0,2},{2,4},{4,6},{6,7},{7,5},{5,3},{3,1},{1,0},{10,8},{12,10},{14... | collective-permute-start | bytes 602120 | tf_op jit(solution)/shard_map/ppermute | solution.py:230
  4.9 1.2 %convert_element_type.8.refs_8_ = bf16[1,224,896]{2,1,0:T(8,128)(2,1)S(1)} convert(f32[1,224,896]{2,1,0:T(8,128)} %param.10) | non-fusion elementwise | flops 200704 | bytes 1204224 | tf_op jit(solution)/shard_map/convert_element_type | solution.py:221
  6.1 1.6 %collective-permute-start.11 = (bf16[1,224,896]{2,1,0:T(8,128)(2,1)S(1)}, bf16[1,224,896]{2,1,0:T(8,128)(2,1)S(1)}, u32[]{:S(2)}, u32[]{:S(2)}) collective-permute-start(bf16[1,224,896]{2,1,0:T(8,128)(2,1)S(1)} %convert_element_type.8.refs_8_), channel_id=1, source_target_pairs={{0,16},{8,24},{16,0},{24,8},{1,17},{9,25},{17,1},{25,9},{2,18},{10... | collective-permute-start | bytes 1204232 | tf_op jit(solution)/shard_map/ppermute | solution.py:239
  7.7 0.9 collective-permute-done.refs_1_
  8.6 2.1 %collective-permute-start.4 = (bf16[112,896]{1,0:T(8,128)(2,1)S(1)}, bf16[112,896]{1,0:T(8,128)(2,1)S(1)}, u32[]{:S(2)}, u32[]{:S(2)}) collective-permute-start(bf16[112,896]{1,0:T(8,128)(2,1)S(1)} %collective-permute-done.refs_1_), channel_id=1, source_target_pairs={{0,2},{2,4},{4,6},{6,7},{7,5},{5,3},{3,1},{1,0},{10,8},{12,10},{14... | collective-permute-start | bytes 602120 | tf_op jit(solution)/shard_map/ppermute | solution.py:230
  10.6 0.0 collective-permute-start.1
  10.6 3.6 %collective-permute-done.4.refs_3_ = bf16[112,896]{1,0:T(8,128)(2,1)S(1)} collective-permute-done((bf16[112,896]{1,0:T(8,128)(2,1)S(1)}, bf16[112,896]{1,0:T(8,128)(2,1)S(1)}, u32[]{:S(2)}, u32[]{:S(2)}) %collective-permute-start.4) | collective-permute-done | bytes 200736 | tf_op jit(solution)/shard_map/ppermute | solution.py:230
  14.3 2.1 %collective-permute-start.7 = (bf16[112,896]{1,0:T(8,128)(2,1)S(1)}, bf16[112,896]{1,0:T(8,128)(2,1)S(1)}, u32[]{:S(2)}, u32[]{:S(2)}) collective-permute-start(bf16[112,896]{1,0:T(8,128)(2,1)S(1)} %collective-permute-done.4.refs_3_), channel_id=1, source_target_pairs={{0,2},{2,4},{4,6},{6,7},{7,5},{5,3},{3,1},{1,0},{10,8},{12,10},{14... | collective-permute-start | bytes 602120 | tf_op jit(solution)/shard_map/ppermute | solution.py:230
  16.3 0.0 collective-permute-done.1
  16.3 1.6 %collective-permute-start.2 = (bf16[112,896]{1,0:T(8,128)(2,1)S(1)}, bf16[112,896]{1,0:T(8,128)(2,1)S(1)}, u32[]{:S(2)}, u32[]{:S(2)}) collective-permute-start(bf16[112,896]{1,0:T(8,128)(2,1)S(1)} %collective-permute-done.1), channel_id=1, source_target_pairs={{0,2},{2,4},{4,6},{6,7},{7,5},{5,3},{3,1},{1,0},{10,8},{12,10},{14... | collective-permute-start | bytes 602120 | tf_op jit(solution)/shard_map/ppermute | solution.py:233
  17.9 0.0 collective-permute-done.11.refs_9_
  17.9 2.1 %collective-permute-done.7.refs_5_ = bf16[112,896]{1,0:T(8,128)(2,1)S(1)} collective-permute-done((bf16[112,896]{1,0:T(8,128)(2,1)S(1)}, bf16[112,896]{1,0:T(8,128)(2,1)S(1)}, u32[]{:S(2)}, u32[]{:S(2)}) %collective-permute-start.7) | collective-permute-done | bytes 200736 | tf_op jit(solution)/shard_map/ppermute | solution.py:230
  20.0 0.1 pad_maximum_fusion
  20.1 0.1 collective-permute-start.12
  20.1 2.0 %collective-permute-done.2 = bf16[112,896]{1,0:T(8,128)(2,1)S(1)} collective-permute-done((bf16[112,896]{1,0:T(8,128)(2,1)S(1)}, bf16[112,896]{1,0:T(8,128)(2,1)S(1)}, u32[]{:S(2)}, u32[]{:S(2)}) %collective-permute-start.2) | collective-permute-done | bytes 200736 | tf_op jit(solution)/shard_map/ppermute | solution.py:233
  22.1 2.1 %collective-permute-start.5 = (bf16[112,896]{1,0:T(8,128)(2,1)S(1)}, bf16[112,896]{1,0:T(8,128)(2,1)S(1)}, u32[]{:S(2)}, u32[]{:S(2)}) collective-permute-start(bf16[112,896]{1,0:T(8,128)(2,1)S(1)} %collective-permute-done.2), channel_id=1, source_target_pairs={{0,2},{2,4},{4,6},{6,7},{7,5},{5,3},{3,1},{1,0},{10,8},{12,10},{14... | collective-permute-start | bytes 602120 | tf_op jit(solution)/shard_map/ppermute | solution.py:233
  24.2 3.6 %collective-permute-done.5 = bf16[112,896]{1,0:T(8,128)(2,1)S(1)} collective-permute-done((bf16[112,896]{1,0:T(8,128)(2,1)S(1)}, bf16[112,896]{1,0:T(8,128)(2,1)S(1)}, u32[]{:S(2)}, u32[]{:S(2)}) %collective-permute-start.5) | collective-permute-done | bytes 200736 | tf_op jit(solution)/shard_map/ppermute | solution.py:233
  27.8 2.1 %collective-permute-start.8 = (bf16[112,896]{1,0:T(8,128)(2,1)S(1)}, bf16[112,896]{1,0:T(8,128)(2,1)S(1)}, u32[]{:S(2)}, u32[]{:S(2)}) collective-permute-start(bf16[112,896]{1,0:T(8,128)(2,1)S(1)} %collective-permute-done.5), channel_id=1, source_target_pairs={{0,2},{2,4},{4,6},{6,7},{7,5},{5,3},{3,1},{1,0},{10,8},{12,10},{14... | collective-permute-start | bytes 602120 | tf_op jit(solution)/shard_map/ppermute | solution.py:233
  29.9 0.0 collective-permute-start.3
  29.9 1.6 %collective-permute-start.10 = (bf16[112,896]{1,0:T(8,128)(2,1)S(1)}, bf16[112,896]{1,0:T(8,128)(2,1)S(1)}, u32[]{:S(2)}, u32[]{:S(2)}) collective-permute-start(bf16[112,896]{1,0:T(8,128)(2,1)S(1)} %collective-permute-done.7.refs_5_), channel_id=1, source_target_pairs={{0,2},{2,4},{4,6},{6,7},{7,5},{5,3},{3,1},{1,0},{10,8},{12,10},{14... | collective-permute-start | bytes 602120 | tf_op jit(solution)/shard_map/ppermute | solution.py:230
  31.5 0.0 collective-permute-start.6
  31.5 2.1 %collective-permute-done.8 = bf16[112,896]{1,0:T(8,128)(2,1)S(1)} collective-permute-done((bf16[112,896]{1,0:T(8,128)(2,1)S(1)}, bf16[112,896]{1,0:T(8,128)(2,1)S(1)}, u32[]{:S(2)}, u32[]{:S(2)}) %collective-permute-start.8) | collective-permute-done | bytes 200736 | tf_op jit(solution)/shard_map/ppermute | solution.py:233
  33.6 0.0 collective-permute-done.3.refs_2_
  33.6 2.1 %collective-permute-done.10.refs_7_ = bf16[112,896]{1,0:T(8,128)(2,1)S(1)} collective-permute-done((bf16[112,896]{1,0:T(8,128)(2,1)S(1)}, bf16[112,896]{1,0:T(8,128)(2,1)S(1)}, u32[]{:S(2)}, u32[]{:S(2)}) %collective-permute-start.10) | collective-permute-done | bytes 200736 | tf_op jit(solution)/shard_map/ppermute | solution.py:230
  35.7 4.2 %shard_map.93 = (bf16[2,224,896]{2,1,0:T(8,128)(2,1)S(1)}, bf16[2,224,896]{2,1,0:T(8,128)(2,1)S(1)}, bf16[512,896]{1,0:T(8,128)(2,1)S(1)}, f32[512,896]{1,0:T(8,128)S(1)}, bf16[896,896]{1,0:T(8,128)(2,1)S(1)}) custom-call(bf16[112,896]{1,0:T(8,128)(2,1)S(1)} %bitcast_convert_fusion.refs_0_, bf16[112,896]{1,0:T(8,128)(2,1)S(1)} %collective-permute-done.refs_1_, ...), custom_call_target="tpu_custom_call" | custom-call | flops 2466250752 | bytes 5046272 | tf_op jit(solution)/shard_map/pallas_call | solution.py:25
  40.0 0.1 collective-permute-start.23
  40.1 2.3 %shard_map.94 = (bf16[112,896]{1,0:T(8,128)(2,1)S(1)}, bf16[112,896]{1,0:T(8,128)(2,1)S(1)}, bf16[112,896]{1,0:T(8,128)(2,1)S(1)}, bf16[112,896]{1,0:T(8,128)(2,...) custom-call(bf16[512,896]{1,0:T(8,128)(2,1)S(1)} %bitcast.25, ...), custom_call_target="tpu_custom_call" | custom-call | flops 1644167168 | bytes 5275648 | tf_op jit(solution)/shard_map/pallas_call | solution.py:25
  42.4 0.6 collective-permute-start.17
  43.0 2.1 %collective-permute-start.13 = (bf16[112,896]{1,0:T(8,128)(2,1)S(1)}, bf16[112,896]{1,0:T(8,128)(2,1)S(1)}, u32[]{:S(2)}, u32[]{:S(2)}) collective-permute-start(bf16[112,896]{1,0:T(8,128)(2,1)S(1)} %get-tuple-element.31), channel_id=1, source_target_pairs={{0,2},{2,4},{4,6},{6,7},{7,5},{5,3},{3,1},{1,0},{10,8},{12,10},{14... | collective-permute-start | bytes 602120 | tf_op jit(solution)/shard_map/ppermute | solution.py:336
  45.1 0.0 collective-permute-done.23.refs_1_
  45.1 0.2 shard_map.102
  45.3 1.6 %collective-permute-start.24 = (bf16[1,224,896]{2,1,0:T(8,128)(2,1)S(1)}, bf16[1,224,896]{2,1,0:T(8,128)(2,1)S(1)}, u32[]{:S(2)}, u32[]{:S(2)}) collective-permute-start(bf16[1,224,896]{2,1,0:T(8,128)(2,1)S(1)} %get-tuple-element.39), channel_id=1, source_target_pairs={{0,16},{8,24},{16,0},{24,8},{1,17},{9,25},{17,1},{25,9},{2,18},{10... | collective-permute-start | bytes 1204232 | tf_op jit(solution)/shard_map/ppermute | solution.py:324
  46.8 0.0 collective-permute-done.17
  46.9 1.6 %collective-permute-start.18 = (bf16[112,896]{1,0:T(8,128)(2,1)S(1)}, bf16[112,896]{1,0:T(8,128)(2,1)S(1)}, u32[]{:S(2)}, u32[]{:S(2)}) collective-permute-start(bf16[112,896]{1,0:T(8,128)(2,1)S(1)} %get-tuple-element.42), channel_id=1, source_target_pairs={{0,2},{2,4},{4,6},{6,7},{7,5},{5,3},{3,1},{1,0},{10,8},{12,10},{14... | collective-permute-start | bytes 602120 | tf_op jit(solution)/shard_map/ppermute | solution.py:338
  48.5 0.2 collective-permute-done.13.came
  48.7 0.1 shard_map.95
  48.7 2.1 %collective-permute-start.14 = (bf16[112,896]{1,0:T(8,128)(2,1)S(1)}, bf16[112,896]{1,0:T(8,128)(2,1)S(1)}, u32[]{:S(2)}, u32[]{:S(2)}) collective-permute-start(bf16[112,896]{1,0:T(8,128)(2,1)S(1)} %shard_map.95), channel_id=1, source_target_pairs={{0,2},{2,4},{4,6},{6,7},{7,5},{5,3},{3,1},{1,0},{10,8},{12,10},{14... | collective-permute-start | bytes 602120 | tf_op jit(solution)/shard_map/ppermute | solution.py:341
  50.9 1.8 %collective-permute-done.18.came = bf16[112,896]{1,0:T(8,128)(2,1)S(1)} collective-permute-done((bf16[112,896]{1,0:T(8,128)(2,1)S(1)}, bf16[112,896]{1,0:T(8,128)(2,1)S(1)}, u32[]{:S(2)}, u32[]{:S(2)}) %collective-permute-start.18) | collective-permute-done | bytes 200736 | tf_op jit(solution)/shard_map/ppermute | solution.py:338
  52.6 0.1 shard_map.98
  52.7 1.6 %collective-permute-start.19 = (bf16[112,896]{1,0:T(8,128)(2,1)S(1)}, bf16[112,896]{1,0:T(8,128)(2,1)S(1)}, u32[]{:S(2)}, u32[]{:S(2)}) collective-permute-start(bf16[112,896]{1,0:T(8,128)(2,1)S(1)} %shard_map.98), channel_id=1, source_target_pairs={{0,2},{2,4},{4,6},{6,7},{7,5},{5,3},{3,1},{1,0},{10,8},{12,10},{14... | collective-permute-start | bytes 602120 | tf_op jit(solution)/shard_map/ppermute | solution.py:344
  54.3 1.9 %collective-permute-done.24.refs_1_ = bf16[1,224,896]{2,1,0:T(8,128)(2,1)S(1)} collective-permute-done((bf16[1,224,896]{2,1,0:T(8,128)(2,1)S(1)}, bf16[1,224,896]{2,1,0:T(8,128)(2,1)S(1)}, u32[]{:S(2)}, u32[]{:S(2)}) %collective-permute-start.24) | collective-permute-done | bytes 401440 | tf_op jit(solution)/shard_map/ppermute | solution.py:324
  56.3 0.2 shard_map.103
  56.4 0.0 copy-start.2
  56.4 0.0 copy-start.3
  56.5 0.5 collective-permute-start.25
  56.9 0.1 shard_map.101
  57.0 1.7 %collective-permute-start.22 = (bf16[2,128,896]{2,1,0:T(8,128)(2,1)S(1)}, bf16[2,128,896]{2,1,0:T(8,128)(2,1)S(1)}, u32[]{:S(2)}, u32[]{:S(2)}) collective-permute-start(bf16[2,128,896]{2,1,0:T(8,128)(2,1)S(1)} %shard_map.101), channel_id=1, source_target_pairs={{0,2},{1,3},{2,4},{3,5},{4,6},{5,7},{6,0},{7,1},{8,10},{9,11},{10,... | collective-permute-start | bytes 1376264 | tf_op jit(solution)/shard_map/ppermute | solution.py:248
  58.7 0.0 collective-permute-done.14.came
  58.8 1.6 %collective-permute-start.15 = (bf16[112,896]{1,0:T(8,128)(2,1)S(1)}, bf16[112,896]{1,0:T(8,128)(2,1)S(1)}, u32[]{:S(2)}, u32[]{:S(2)}) collective-permute-start(bf16[112,896]{1,0:T(8,128)(2,1)S(1)} %shard_map.96), channel_id=1, source_target_pairs={{0,2},{2,4},{4,6},{6,7},{7,5},{5,3},{3,1},{1,0},{10,8},{12,10},{14... | collective-permute-start | bytes 602120 | tf_op jit(solution)/shard_map/ppermute | solution.py:341
  60.4 0.0 collective-permute-done.19.came
  60.4 0.1 shard_map.99
  60.5 1.5 %collective-permute-start.20 = (bf16[112,896]{1,0:T(8,128)(2,1)S(1)}, bf16[112,896]{1,0:T(8,128)(2,1)S(1)}, u32[]{:S(2)}, u32[]{:S(2)}) collective-permute-start(bf16[112,896]{1,0:T(8,128)(2,1)S(1)} %shard_map.99), channel_id=1, source_target_pairs={{0,2},{2,4},{4,6},{6,7},{7,5},{5,3},{3,1},{1,0},{10,8},{12,10},{14... | collective-permute-start | bytes 602120 | tf_op jit(solution)/shard_map/ppermute | solution.py:344
  61.9 19.9 %collective-permute-done.15.came = bf16[112,896]{1,0:T(8,128)(2,1)S(1)} collective-permute-done((bf16[112,896]{1,0:T(8,128)(2,1)S(1)}, bf16[112,896]{1,0:T(8,128)(2,1)S(1)}, u32[]{:S(2)}, u32[]{:S(2)}) %collective-permute-start.15) | collective-permute-done | bytes 200736 | tf_op jit(solution)/shard_map/ppermute | solution.py:341
  81.8 0.1 shard_map.97
  81.9 2.5 %collective-permute-start.16 = (bf16[112,896]{1,0:T(8,128)(2,1)S(1)}, bf16[112,896]{1,0:T(8,128)(2,1)S(1)}, u32[]{:S(2)}, u32[]{:S(2)}) collective-permute-start(bf16[112,896]{1,0:T(8,128)(2,1)S(1)} %shard_map.97), channel_id=1, source_target_pairs={{0,2},{2,4},{4,6},{6,7},{7,5},{5,3},{3,1},{1,0},{10,8},{12,10},{14... | collective-permute-start | bytes 602120 | tf_op jit(solution)/shard_map/ppermute | solution.py:341
  84.4 0.0 collective-permute-done.20
  84.4 0.5 collective-permute-start.21
  84.9 5.4 %collective-permute-done.16.refs_1_ = bf16[112,896]{1,0:T(8,128)(2,1)S(1)} collective-permute-done((bf16[112,896]{1,0:T(8,128)(2,1)S(1)}, bf16[112,896]{1,0:T(8,128)(2,1)S(1)}, u32[]{:S(2)}, u32[]{:S(2)}) %collective-permute-start.16) | collective-permute-done | bytes 200736 | tf_op jit(solution)/shard_map/ppermute | solution.py:341
  90.3 0.0 collective-permute-done.21.refs_2_
  90.3 1.0 %shard_map.100 = (f32[112,896]{1,0:T(8,128)}, f32[112,896]{1,0:T(8,128)}) custom-call(bf16[112,896]{1,0:T(8,128)(2,1)S(1)} %get-tuple-element.27.refs_0_, bf16[112,896]{1,0:T(8,128)(2,1)S(1)} %collective-permute-done.16.refs_1_, bf16[112,896]{1,0:T(8,128)(2,1)S(1)} %collective-permute-done.21.refs_2_, f32[112,896]{1,0:T(8,128)S(1)} %bitcast.21, ...), custom_call_target="tpu_custom_call" | custom-call | bytes 1404928 | tf_op jit(solution)/shard_map/pallas_call | solution.py:25
  91.3 0.0 collective-permute-done.22.early
  91.3 0.0 collective-permute-done.25.late
  91.3 1.3 %shard_map.104 = (f32[224,896]{1,0:T(8,128)}, f32[224,896]{1,0:T(8,128)}) custom-call(bf16[2,128,896]{2,1,0:T(8,128)(2,1)S(1)} %collective-permute-done.22.early, bf16[320,896]{1,0:T(8,128)(2,1)S(1)} %collective-permute-done.25.late), custom_call_target="tpu_custom_call" | custom-call | bytes 1032192 | tf_op jit(solution)/shard_map/pallas_call | solution.py:25
  (16 shorter events, 0.1 us)
Async XLA Ops:
  0.6 35.1 %copy-start.5 = (bf16[1,1,512,896]{3,2,1,0:T(8,128)(2,1)S(1)}, bf16[1,1,512,896]{3,2,1,0:T(8,128)(2,1)}, u32[]{:S(2)}) copy-start(bf16[1,1,512,896]{3,2,1,0:T(8,128)(2,1)} %param.6) | copy-start | bytes 2752516
  0.6 35.1 %copy-start.4 = (bf16[1,1,512,896]{3,2,1,0:T(8,128)(2,1)S(1)}, bf16[1,1,512,896]{3,2,1,0:T(8,128)(2,1)}, u32[]{:S(2)}) copy-start(bf16[1,1,512,896]{3,2,1,0:T(8,128)(2,1)} %param.7) | copy-start | bytes 2752516
  1.8 6.7 %collective-permute-start = (bf16[112,896]{1,0:T(8,128)(2,1)S(1)}, bf16[112,896]{1,0:T(8,128)(2,1)S(1)}, u32[]{:S(2)}, u32[]{:S(2)}) collective-permute-start(bf16[112,896]{1,0:T(8,128)(2,1)S(1)} %bitcast_convert_fusion.refs_0_), channel_id=1, source_target_pairs={{0,2},{2,4},{4,6},{6,7},{7,5},{5,3},{3,1},{1,0},{10,8},{12,10},{14... | collective-permute-start | bytes 602120 | tf_op jit(solution)/shard_map/ppermute | solution.py:230
  6.1 11.8 %collective-permute-start.11 = (bf16[1,224,896]{2,1,0:T(8,128)(2,1)S(1)}, bf16[1,224,896]{2,1,0:T(8,128)(2,1)S(1)}, u32[]{:S(2)}, u32[]{:S(2)}) collective-permute-start(bf16[1,224,896]{2,1,0:T(8,128)(2,1)S(1)} %convert_element_type.8.refs_8_), channel_id=1, source_target_pairs={{0,16},{8,24},{16,0},{24,8},{1,17},{9,25},{17,1},{25,9},{2,18},{10... | collective-permute-start | bytes 1204232 | tf_op jit(solution)/shard_map/ppermute | solution.py:239
  8.6 5.7 %collective-permute-start.4 = (bf16[112,896]{1,0:T(8,128)(2,1)S(1)}, bf16[112,896]{1,0:T(8,128)(2,1)S(1)}, u32[]{:S(2)}, u32[]{:S(2)}) collective-permute-start(bf16[112,896]{1,0:T(8,128)(2,1)S(1)} %collective-permute-done.refs_1_), channel_id=1, source_target_pairs={{0,2},{2,4},{4,6},{6,7},{7,5},{5,3},{3,1},{1,0},{10,8},{12,10},{14... | collective-permute-start | bytes 602120 | tf_op jit(solution)/shard_map/ppermute | solution.py:230
  10.6 5.7 %collective-permute-start.1 = (bf16[112,896]{1,0:T(8,128)(2,1)S(1)}, bf16[112,896]{1,0:T(8,128)(2,1)S(1)}, u32[]{:S(2)}, u32[]{:S(2)}) collective-permute-start(bf16[112,896]{1,0:T(8,128)(2,1)S(1)} %bitcast_convert_fusion.refs_0_), channel_id=1, source_target_pairs={{0,8},{8,0},{16,24},{24,16},{1,9},{9,1},{17,25},{25,17},{2,10},{10... | collective-permute-start | bytes 602120 | tf_op jit(solution)/shard_map/ppermute | solution.py:227
  14.3 5.7 %collective-permute-start.7 = (bf16[112,896]{1,0:T(8,128)(2,1)S(1)}, bf16[112,896]{1,0:T(8,128)(2,1)S(1)}, u32[]{:S(2)}, u32[]{:S(2)}) collective-permute-start(bf16[112,896]{1,0:T(8,128)(2,1)S(1)} %collective-permute-done.4.refs_3_), channel_id=1, source_target_pairs={{0,2},{2,4},{4,6},{6,7},{7,5},{5,3},{3,1},{1,0},{10,8},{12,10},{14... | collective-permute-start | bytes 602120 | tf_op jit(solution)/shard_map/ppermute | solution.py:230
  16.3 5.8 %collective-permute-start.2 = (bf16[112,896]{1,0:T(8,128)(2,1)S(1)}, bf16[112,896]{1,0:T(8,128)(2,1)S(1)}, u32[]{:S(2)}, u32[]{:S(2)}) collective-permute-start(bf16[112,896]{1,0:T(8,128)(2,1)S(1)} %collective-permute-done.1), channel_id=1, source_target_pairs={{0,2},{2,4},{4,6},{6,7},{7,5},{5,3},{3,1},{1,0},{10,8},{12,10},{14... | collective-permute-start | bytes 602120 | tf_op jit(solution)/shard_map/ppermute | solution.py:233
  20.1 15.7 %collective-permute-start.12 = (bf16[2,224,896]{2,1,0:T(8,128)(2,1)S(1)}, bf16[2,224,896]{2,1,0:T(8,128)(2,1)S(1)}, u32[]{:S(2)}, u32[]{:S(2)}) collective-permute-start(bf16[2,224,896]{2,1,0:T(8,128)(2,1)S(1)} %pad_maximum_fusion), channel_id=1, source_target_pairs={{0,8},{8,0},{16,24},{24,16},{1,9},{9,1},{17,25},{25,17},{2,10},{10... | collective-permute-start | bytes 2408456 | tf_op jit(solution)/shard_map/ppermute | solution.py:239
  22.1 5.7 %collective-permute-start.5 = (bf16[112,896]{1,0:T(8,128)(2,1)S(1)}, bf16[112,896]{1,0:T(8,128)(2,1)S(1)}, u32[]{:S(2)}, u32[]{:S(2)}) collective-permute-start(bf16[112,896]{1,0:T(8,128)(2,1)S(1)} %collective-permute-done.2), channel_id=1, source_target_pairs={{0,2},{2,4},{4,6},{6,7},{7,5},{5,3},{3,1},{1,0},{10,8},{12,10},{14... | collective-permute-start | bytes 602120 | tf_op jit(solution)/shard_map/ppermute | solution.py:233
  27.8 5.7 %collective-permute-start.8 = (bf16[112,896]{1,0:T(8,128)(2,1)S(1)}, bf16[112,896]{1,0:T(8,128)(2,1)S(1)}, u32[]{:S(2)}, u32[]{:S(2)}) collective-permute-start(bf16[112,896]{1,0:T(8,128)(2,1)S(1)} %collective-permute-done.5), channel_id=1, source_target_pairs={{0,2},{2,4},{4,6},{6,7},{7,5},{5,3},{3,1},{1,0},{10,8},{12,10},{14... | collective-permute-start | bytes 602120 | tf_op jit(solution)/shard_map/ppermute | solution.py:233
  29.9 3.6 %collective-permute-start.3 = (bf16[112,896]{1,0:T(8,128)(2,1)S(1)}, bf16[112,896]{1,0:T(8,128)(2,1)S(1)}, u32[]{:S(2)}, u32[]{:S(2)}) collective-permute-start(bf16[112,896]{1,0:T(8,128)(2,1)S(1)} %collective-permute-done.2), channel_id=1, source_target_pairs={{0,8},{8,0},{16,24},{24,16},{1,9},{9,1},{17,25},{25,17},{2,10},{10... | collective-permute-start | bytes 602120 | tf_op jit(solution)/shard_map/ppermute | solution.py:234
  29.9 5.8 %collective-permute-start.10 = (bf16[112,896]{1,0:T(8,128)(2,1)S(1)}, bf16[112,896]{1,0:T(8,128)(2,1)S(1)}, u32[]{:S(2)}, u32[]{:S(2)}) collective-permute-start(bf16[112,896]{1,0:T(8,128)(2,1)S(1)} %collective-permute-done.7.refs_5_), channel_id=1, source_target_pairs={{0,2},{2,4},{4,6},{6,7},{7,5},{5,3},{3,1},{1,0},{10,8},{12,10},{14... | collective-permute-start | bytes 602120 | tf_op jit(solution)/shard_map/ppermute | solution.py:230
  31.5 4.2 %collective-permute-start.6 = (bf16[112,896]{1,0:T(8,128)(2,1)S(1)}, bf16[112,896]{1,0:T(8,128)(2,1)S(1)}, u32[]{:S(2)}, u32[]{:S(2)}) collective-permute-start(bf16[112,896]{1,0:T(8,128)(2,1)S(1)} %collective-permute-done.5), channel_id=1, source_target_pairs={{0,8},{8,0},{16,24},{24,16},{1,9},{9,1},{17,25},{25,17},{2,10},{10... | collective-permute-start | bytes 602120 | tf_op jit(solution)/shard_map/ppermute | solution.py:234
  33.6 2.2 %collective-permute-start.9 = (bf16[112,896]{1,0:T(8,128)(2,1)S(1)}, bf16[112,896]{1,0:T(8,128)(2,1)S(1)}, u32[]{:S(2)}, u32[]{:S(2)}) collective-permute-start(bf16[112,896]{1,0:T(8,128)(2,1)S(1)} %collective-permute-done.8), channel_id=1, source_target_pairs={{0,8},{8,0},{16,24},{24,16},{1,9},{9,1},{17,25},{25,17},{2,10},{10... | collective-permute-start | bytes 602120 | tf_op jit(solution)/shard_map/ppermute | solution.py:234
  40.0 5.1 %collective-permute-start.23 = (bf16[2,224,896]{2,1,0:T(8,128)(2,1)S(1)}, bf16[2,224,896]{2,1,0:T(8,128)(2,1)S(1)}, u32[]{:S(2)}, u32[]{:S(2)}) collective-permute-start(bf16[2,224,896]{2,1,0:T(8,128)(2,1)S(1)} %get-tuple-element.37), channel_id=1, source_target_pairs={{0,8},{8,0},{16,24},{24,16},{1,9},{9,1},{17,25},{25,17},{2,10},{10... | collective-permute-start | bytes 2408456 | tf_op jit(solution)/shard_map/ppermute | solution.py:279
  42.4 4.4 %collective-permute-start.17 = (bf16[3,112,896]{2,1,0:T(8,128)(2,1)S(1)}, bf16[3,112,896]{2,1,0:T(8,128)(2,1)S(1)}, u32[]{:S(2)}, u32[]{:S(2)}) collective-permute-start(bf16[3,112,896]{2,1,0:T(8,128)(2,1)S(1)} %get-tuple-element.32), channel_id=1, source_target_pairs={{0,8},{8,0},{16,24},{24,16},{1,9},{9,1},{17,25},{25,17},{2,10},{10... | collective-permute-start | bytes 1806344 | tf_op jit(solution)/shard_map/ppermute | solution.py:337
  43.0 5.7 %collective-permute-start.13 = (bf16[112,896]{1,0:T(8,128)(2,1)S(1)}, bf16[112,896]{1,0:T(8,128)(2,1)S(1)}, u32[]{:S(2)}, u32[]{:S(2)}) collective-permute-start(bf16[112,896]{1,0:T(8,128)(2,1)S(1)} %get-tuple-element.31), channel_id=1, source_target_pairs={{0,2},{2,4},{4,6},{6,7},{7,5},{5,3},{3,1},{1,0},{10,8},{12,10},{14... | collective-permute-start | bytes 602120 | tf_op jit(solution)/shard_map/ppermute | solution.py:336
  45.1 11.2 %copy-start = (f32[1,224,896]{2,1,0:T(8,128)S(1)}, f32[1,224,896]{2,1,0:T(8,128)}, u32[]{:S(2)}) copy-start(f32[1,224,896]{2,1,0:T(8,128)} %param.10) | copy-start | bytes 2408452
  45.1 11.2 %copy-start.1 = (f32[1,224,896]{2,1,0:T(8,128)S(1)}, f32[1,224,896]{2,1,0:T(8,128)}, u32[]{:S(2)}) copy-start(f32[1,224,896]{2,1,0:T(8,128)} %param.11) | copy-start | bytes 2408452
  45.3 11.0 %collective-permute-start.24 = (bf16[1,224,896]{2,1,0:T(8,128)(2,1)S(1)}, bf16[1,224,896]{2,1,0:T(8,128)(2,1)S(1)}, u32[]{:S(2)}, u32[]{:S(2)}) collective-permute-start(bf16[1,224,896]{2,1,0:T(8,128)(2,1)S(1)} %get-tuple-element.39), channel_id=1, source_target_pairs={{0,16},{8,24},{16,0},{24,8},{1,17},{9,25},{17,1},{25,9},{2,18},{10... | collective-permute-start | bytes 1204232 | tf_op jit(solution)/shard_map/ppermute | solution.py:324
  46.9 5.8 %collective-permute-start.18 = (bf16[112,896]{1,0:T(8,128)(2,1)S(1)}, bf16[112,896]{1,0:T(8,128)(2,1)S(1)}, u32[]{:S(2)}, u32[]{:S(2)}) collective-permute-start(bf16[112,896]{1,0:T(8,128)(2,1)S(1)} %get-tuple-element.42), channel_id=1, source_target_pairs={{0,2},{2,4},{4,6},{6,7},{7,5},{5,3},{3,1},{1,0},{10,8},{12,10},{14... | collective-permute-start | bytes 602120 | tf_op jit(solution)/shard_map/ppermute | solution.py:338
  48.7 10.0 %collective-permute-start.14 = (bf16[112,896]{1,0:T(8,128)(2,1)S(1)}, bf16[112,896]{1,0:T(8,128)(2,1)S(1)}, u32[]{:S(2)}, u32[]{:S(2)}) collective-permute-start(bf16[112,896]{1,0:T(8,128)(2,1)S(1)} %shard_map.95), channel_id=1, source_target_pairs={{0,2},{2,4},{4,6},{6,7},{7,5},{5,3},{3,1},{1,0},{10,8},{12,10},{14... | collective-permute-start | bytes 602120 | tf_op jit(solution)/shard_map/ppermute | solution.py:341
  52.7 7.7 %collective-permute-start.19 = (bf16[112,896]{1,0:T(8,128)(2,1)S(1)}, bf16[112,896]{1,0:T(8,128)(2,1)S(1)}, u32[]{:S(2)}, u32[]{:S(2)}) collective-permute-start(bf16[112,896]{1,0:T(8,128)(2,1)S(1)} %shard_map.98), channel_id=1, source_target_pairs={{0,2},{2,4},{4,6},{6,7},{7,5},{5,3},{3,1},{1,0},{10,8},{12,10},{14... | collective-permute-start | bytes 602120 | tf_op jit(solution)/shard_map/ppermute | solution.py:344
  56.4 33.9 %copy-start.2 = (f32[1,112,896]{2,1,0:T(8,128)S(1)}, f32[1,112,896]{2,1,0:T(8,128)}, u32[]{:S(2)}) copy-start(f32[1,112,896]{2,1,0:T(8,128)} %param.8) | copy-start | bytes 1204228
  56.4 33.9 %copy-start.3 = (f32[1,112,896]{2,1,0:T(8,128)S(1)}, f32[1,112,896]{2,1,0:T(8,128)}, u32[]{:S(2)}) copy-start(f32[1,112,896]{2,1,0:T(8,128)} %param.9) | copy-start | bytes 1204228
  56.5 34.9 %collective-permute-start.25 = (bf16[320,896]{1,0:T(8,128)(2,1)S(1)}, bf16[320,896]{1,0:T(8,128)(2,1)S(1)}, u32[]{:S(2)}, u32[]{:S(2)}) collective-permute-start(bf16[320,896]{1,0:T(8,128)(2,1)S(1)} %shard_map.103), channel_id=1, source_target_pairs={{0,2},{1,3},{2,4},{3,5},{4,6},{5,7},{6,0},{7,1},{8,10},{9,11},{10,... | collective-permute-start | bytes 1720328 | tf_op jit(solution)/shard_map/ppermute | solution.py:335
  57.0 34.4 %collective-permute-start.22 = (bf16[2,128,896]{2,1,0:T(8,128)(2,1)S(1)}, bf16[2,128,896]{2,1,0:T(8,128)(2,1)S(1)}, u32[]{:S(2)}, u32[]{:S(2)}) collective-permute-start(bf16[2,128,896]{2,1,0:T(8,128)(2,1)S(1)} %shard_map.101), channel_id=1, source_target_pairs={{0,2},{1,3},{2,4},{3,5},{4,6},{5,7},{6,0},{7,1},{8,10},{9,11},{10,... | collective-permute-start | bytes 1376264 | tf_op jit(solution)/shard_map/ppermute | solution.py:248
  58.8 23.1 %collective-permute-start.15 = (bf16[112,896]{1,0:T(8,128)(2,1)S(1)}, bf16[112,896]{1,0:T(8,128)(2,1)S(1)}, u32[]{:S(2)}, u32[]{:S(2)}) collective-permute-start(bf16[112,896]{1,0:T(8,128)(2,1)S(1)} %shard_map.96), channel_id=1, source_target_pairs={{0,2},{2,4},{4,6},{6,7},{7,5},{5,3},{3,1},{1,0},{10,8},{12,10},{14... | collective-permute-start | bytes 602120 | tf_op jit(solution)/shard_map/ppermute | solution.py:341
  60.5 24.0 %collective-permute-start.20 = (bf16[112,896]{1,0:T(8,128)(2,1)S(1)}, bf16[112,896]{1,0:T(8,128)(2,1)S(1)}, u32[]{:S(2)}, u32[]{:S(2)}) collective-permute-start(bf16[112,896]{1,0:T(8,128)(2,1)S(1)} %shard_map.99), channel_id=1, source_target_pairs={{0,2},{2,4},{4,6},{6,7},{7,5},{5,3},{3,1},{1,0},{10,8},{12,10},{14... | collective-permute-start | bytes 602120 | tf_op jit(solution)/shard_map/ppermute | solution.py:344
  81.9 8.4 %collective-permute-start.16 = (bf16[112,896]{1,0:T(8,128)(2,1)S(1)}, bf16[112,896]{1,0:T(8,128)(2,1)S(1)}, u32[]{:S(2)}, u32[]{:S(2)}) collective-permute-start(bf16[112,896]{1,0:T(8,128)(2,1)S(1)} %shard_map.97), channel_id=1, source_target_pairs={{0,2},{2,4},{4,6},{6,7},{7,5},{5,3},{3,1},{1,0},{10,8},{12,10},{14... | collective-permute-start | bytes 602120 | tf_op jit(solution)/shard_map/ppermute | solution.py:341
  84.4 5.9 %collective-permute-start.21 = (bf16[112,896]{1,0:T(8,128)(2,1)S(1)}, bf16[112,896]{1,0:T(8,128)(2,1)S(1)}, u32[]{:S(2)}, u32[]{:S(2)}) collective-permute-start(bf16[112,896]{1,0:T(8,128)(2,1)S(1)} %collective-permute-done.20), channel_id=1, source_target_pairs={{0,8},{8,0},{16,24},{24,16},{1,9},{9,1},{17,25},{25,17},{2,10},{10... | collective-permute-start | bytes 602120 | tf_op jit(solution)/shard_map/ppermute | solution.py:345
